TPU v7x, 256 devices: a whole 4x4x8 slice. The times are simulated.
256 devices in a mesh: grp: 4 (over x), tok: 16 (over z, core), mdl: 4 (over y).
Axes of the slice: x: 4, y: 4, z: 8, core: 2. Of those that a mesh axis runs over, the one named last changes fastest.
Arguments:
- hidden_in: bfloat16 [4, 4096, 2048], P('grp', 'tok', 'mdl'), may hold values from -6 to 6
- suffix_len: int32 [4], P('grp'), may hold values from 512 to 4096, as said below
- norm_gain: bfloat16 [2048], replicated, may hold values from 0.099609375 to 1.8984375
- w_query: bfloat16 [2048, 2048], P(('grp', 'tok'), 'mdl'), may hold values from -0.5 to 0.5
- w_key: bfloat16 [2048, 512], P(('grp', 'tok'), 'mdl'), may hold values from -0.5 to 0.5
- w_value: bfloat16 [2048, 512], P(('grp', 'tok'), 'mdl'), may hold values from -0.125 to 0.125
- w_out: bfloat16 [2048, 2048], P(('grp', 'tok'), 'mdl'), may hold values from -0.5 to 0.5
- sink_logits: float32 [32], P('mdl'), may hold values from 8 to 12
- prefix_keys: bfloat16 [4, 4096, 512], P('grp', 'tok', 'mdl'), may hold values from -280 to 280
- prefix_values: bfloat16 [4, 4096, 512], P('grp', 'tok', 'mdl'), may hold values from -6 to 6
Outputs:
- attn_out: bfloat16 [4, 4096, 2048], P('grp', 'tok', 'mdl')
Inputs may be any that keep to these rules, and one draw needn't show every extreme that they name: `suffix_len`: one group in every draw has all 4096 slots live.
All inputs are finite; a program needn't handle non-finite values.
Results may differ from a plain program's by a relative error of at most 0.015.
The roundings to bfloat16 on the way count: a program that leaves them out, or rounds other values in their place, can miss the bound.
Values may be sent and summed in bfloat16 or wider, within the bound.
No kernel may reach another device: no remote copies, remote signals or barrier semaphores. Data moves between devices by JAX's collectives and lax.ppermute only.
A program may use at most 64 MiB of HBM per device.

v0:
```python
import jax
import jax.numpy as jnp
from jax import lax
from jax.sharding import PartitionSpec as P

HD = 64


SCORE_SCALE = 0.015625
EPSILON = 1e-05
LOG_THETA = 16.11809565095832


def rotate(heads_in, positions):
    half_dim = heads_in.shape[-1] // 2
    frequency = jnp.exp(
        -LOG_THETA * 2.0 * jnp.arange(half_dim, dtype=jnp.float32) / heads_in.shape[-1]
    )
    angles = positions[:, None] * frequency[None, :]
    cosine = jnp.concatenate([jnp.cos(angles), jnp.cos(angles)], axis=-1)[:, None, :]
    sine_part = jnp.concatenate([jnp.sin(angles), jnp.sin(angles)], axis=-1)[:, None, :]
    turned = jnp.concatenate([-heads_in[..., half_dim:], heads_in[..., :half_dim]], axis=-1)
    return heads_in * cosine + turned * sine_part


def on_device(
    hidden_in,
    suffix_len,
    norm_gain,
    w_query,
    w_key,
    w_value,
    w_out,
    sink_logits,
    prefix_keys,
    prefix_values,
):
    group_count, tok_rows, _ = hidden_in.shape
    head_count = sink_logits.shape[0]
    kv_width = prefix_keys.shape[2]
    kv_heads = kv_width // HD
    repeat = head_count // kv_heads
    tok_count = lax.axis_size("tok")
    own_index = lax.axis_index("tok")
    seq_span = tok_rows * tok_count
    gathered = lax.all_gather(hidden_in, "mdl", axis=2, tiled=True)
    features = gathered.astype(jnp.float32)
    normed = (
        features
        * lax.rsqrt(jnp.mean(features * features, axis=-1, keepdims=True) + EPSILON)
        * norm_gain.astype(jnp.float32)
    ).astype(jnp.bfloat16)
    normed = normed.reshape(group_count * tok_rows, -1)
    shard_rows = (
        lax.all_gather(w_query, ("grp", "tok"), axis=0, tiled=True),
        lax.all_gather(w_key, ("grp", "tok"), axis=0, tiled=True),
        lax.all_gather(w_value, ("grp", "tok"), axis=0, tiled=True),
    )
    query_sums, key_sums, value_sums = tuple(
        (
            jnp.dot(normed, weight_rows, preferred_element_type=jnp.float32)
            for weight_rows in shard_rows
        )
    )
    local_slots = own_index * tok_rows + jnp.arange(tok_rows, dtype=jnp.int32)
    query_pos = seq_span + local_slots
    positions = query_pos.astype(jnp.float32)
    queries = rotate(query_sums.reshape(group_count, tok_rows, head_count, HD), positions).astype(
        jnp.bfloat16
    )
    query_groups = queries.reshape(group_count, tok_rows, kv_heads, repeat, HD)
    new_keys = rotate(key_sums.reshape(group_count, tok_rows, kv_heads, HD), positions).astype(
        jnp.bfloat16
    )
    new_values = value_sums.astype(jnp.bfloat16).reshape(group_count, tok_rows, kv_width)
    kv_new = jnp.concatenate(
        [new_keys.reshape(group_count, tok_rows, kv_width), new_values], axis=2
    )
    kv_prefix = jnp.concatenate([prefix_keys, prefix_values], axis=2)

    def attend_part(softmax_state, key_block, key_pos):
        row_top, denoms, weighted = softmax_state
        key_count = key_block.shape[1]
        key_rows = key_block[..., :kv_width].reshape(group_count, key_count, kv_heads, HD)
        value_rows = key_block[..., kv_width:].reshape(group_count, key_count, kv_heads, HD)
        scores = (
            jnp.einsum(
                "gbkrh,gskh->gkrbs", query_groups, key_rows, preferred_element_type=jnp.float32
            )
            * SCORE_SCALE
        )
        allowed = (key_pos[None, :] <= query_pos[:, None]) & (
            key_pos[None, :] > query_pos[:, None] - seq_span
        )
        scores = jnp.where(allowed, scores, -jnp.inf)
        new_top = jnp.maximum(row_top, jnp.max(scores, axis=-1))
        expo_terms = jnp.where(allowed, jnp.exp(scores - new_top[..., None]), 0.0)
        rescale = jnp.exp(row_top - new_top)
        denoms = denoms * rescale + jnp.sum(expo_terms, axis=-1)
        weighted = weighted * rescale[..., None] + jnp.einsum(
            "gkrbs,gskh->gkrbh",
            expo_terms.astype(jnp.bfloat16),
            value_rows,
            preferred_element_type=jnp.float32,
        )
        return (new_top, denoms, weighted)

    def attend(softmax_state, key_block, key_pos):
        key_count = key_block.shape[1]
        block_count = key_count // 512
        blocks = jnp.swapaxes(
            key_block.reshape(group_count, block_count, 512, key_block.shape[2]), 0, 1
        )
        block_pos = key_pos.reshape(block_count, 512)

        def scan_step(inner_state, inputs):
            return (attend_part(inner_state, inputs[0], inputs[1]), None)

        final_state, _ = lax.scan(scan_step, softmax_state, (blocks, block_pos))
        return final_state

    sinks = sink_logits.reshape(1, kv_heads, repeat, 1)
    state_shape = (group_count, kv_heads, repeat, tok_rows)
    initial_state = (
        jnp.broadcast_to(sinks, state_shape),
        jnp.ones(state_shape, jnp.float32),
        jnp.zeros(state_shape + (HD,), jnp.float32),
    )
    softmax_state = initial_state
    shard_pair = (
        lax.all_gather(kv_prefix, "tok", axis=1, tiled=True),
        lax.all_gather(kv_new, "tok", axis=1, tiled=True),
    )
    row_count = shard_pair[0].shape[1]
    offsets = jnp.arange(row_count, dtype=jnp.int32)
    softmax_state = attend(softmax_state, shard_pair[0], offsets)
    final_state = attend(softmax_state, shard_pair[1], seq_span + offsets)
    row_top, denoms, weighted = final_state
    mixed = weighted / denoms[..., None]
    mixed = jnp.transpose(mixed, (0, 3, 1, 2, 4)).reshape(group_count, tok_rows, head_count * HD)
    live = local_slots[None, :] < suffix_len[:, None]
    mixed = jnp.where(live[..., None], mixed, 0.0).astype(jnp.bfloat16)
    mixed_rows = mixed.reshape(group_count * tok_rows, head_count * HD)
    partial_out = lax.dot_general(
        mixed_rows,
        lax.all_gather(w_out, ("grp", "tok"), axis=0, tiled=True),
        (((1,), (1,)), ((), ())),
        preferred_element_type=jnp.float32,
    )
    partial_out = partial_out.reshape(group_count, tok_rows, -1)
    summed = lax.psum_scatter(
        partial_out.astype(jnp.bfloat16), "mdl", scatter_dimension=2, tiled=True
    )
    return summed


def solution(mesh):
    placed = (
        P("grp", "tok", "mdl"),
        P("grp"),
        P(),
        P(("grp", "tok"), "mdl"),
        P(("grp", "tok"), "mdl"),
        P(("grp", "tok"), "mdl"),
        P(("grp", "tok"), "mdl"),
        P("mdl"),
        P("grp", "tok", "mdl"),
        P("grp", "tok", "mdl"),
    )
    return jax.shard_map(
        on_device, mesh=mesh, in_specs=placed, out_specs=P("grp", "tok", "mdl"), check_vma=False
    )
```

profile of v0, /device:TPU:32, one launch (start us, length us, event | category | flops | bytes accessed | tf_op | source)
XLA Modules:
  0.0 312.3 jit_solution(16367372434368591461)
XLA Ops:
  8.1 1.5 pad_maximum_fusion
  10.6 52.4 %all_gather.25 = bf16[2048,128]{1,0:T(8,128)(2,1)S(1)} all-gather(bf16[32,128]{1,0:T(8,128)(2,1)} %param.19), channel_id=1, replica_groups=mesh['grp'=4,'tok'=16,'mdl'=4] {'grp','tok'}, dimensions={0}, use_global_device_ids=true | all-gather | bytes 532480 | tf_op jit(solution)/shard_map/all_gather | solution.py:57
  63.1 47.9 %all_gather.24 = bf16[2048,128]{1,0:T(8,128)(2,1)S(1)} all-gather(bf16[32,128]{1,0:T(8,128)(2,1)} %param.18), channel_id=1, replica_groups=mesh['grp'=4,'tok'=16,'mdl'=4] {'grp','tok'}, dimensions={0}, use_global_device_ids=true | all-gather | bytes 532480 | tf_op jit(solution)/shard_map/all_gather | solution.py:56
  111.0 1.6 fusion.43
  112.6 1.8 fusion.55
  117.9 2.6 fusion.57
  120.7 36.7 %all-gather.6.cloned.1.call-done = bf16[1,4096,256]{2,1,0:T(8,128)(2,1)} async-done(((bf16[1,256,256]{2,1,0:T(8,128)(2,1)}), bf16[1,4096,256]{2,1,0:T(8,128)(2,1)}) %all-gather.6.cloned.1.call-update) | async-done | bytes 2097168 | tf_op jit(solution)/shard_map/all_gather | solution.py:131
  157.4 68.9 %while.35 = (s32[]{:T(128)}, f32[1,2,4,256]{3,2,1,0:T(4,128)S(1)}, f32[1,2,4,256]{3,2,1,0:T(4,128)S(1)}, f32[1,2,4,256,64]{3,4,2,1,0:T(8,128)S(1)}, s32[8,512]{1...) while((s32[]{:T(128)}, f32[1,2,4,256]{3,2,1,0:T(4,128)S(1)}, ...), condition=%wide.region_4.5_spmd.clone, body=%wide.region_1.4_spmd.clone.sunk | while | flops 282862080 | bytes 33171616 | solution.py:119
  157.6 1.0 constant_dynamic-slice_fusion.8
  159.6 1.9 copy-done
  161.6 1.0 fusion.100
  162.6 3.4 %fusion.101 = f32[1,2,4,256,64]{3,4,2,1,0:T(8,128)S(1)} fusion(bf16[512,2,64,1]{0,2,3,1:T(8,128)(2,1)S(1)} %bitcast.229, f32[2,512,256,4]{2,1,3,0:T(8,128)} %copy-done, f32[2,4,256]{2,1,0:T(4,128)S(1)} %bitcast.228, pred[256,512]{0,1:T(8,128)(4,1)S(1)} %compare_and_fusion.5, f32[1,2,4,256,64]{3,4,2,1,0:T(8,128)S(1)} %get-tuple-element.487, ...), kind=kOutput, calls=%fused_computation.35.clone.1 | convolution fusion | flops 139853824 | bytes 5521409 | tf_op jit(solution)/shard_map/while/body/eval_jaxpr/gkrbs,gskh->gkrbh/dot_general | solution.py:100
  166.2 1.0 constant_dynamic-slice_fusion.8
  168.2 1.9 copy-done
  170.2 1.0 fusion.100
  171.2 3.4 %fusion.101 = f32[1,2,4,256,64]{3,4,2,1,0:T(8,128)S(1)} fusion(bf16[512,2,64,1]{0,2,3,1:T(8,128)(2,1)S(1)} %bitcast.229, f32[2,512,256,4]{2,1,3,0:T(8,128)} %copy-done, f32[2,4,256]{2,1,0:T(4,128)S(1)} %bitcast.228, pred[256,512]{0,1:T(8,128)(4,1)S(1)} %compare_and_fusion.5, f32[1,2,4,256,64]{3,4,2,1,0:T(8,128)S(1)} %get-tuple-element.487, ...), kind=kOutput, calls=%fused_computation.35.clone.1 | convolution fusion | flops 139853824 | bytes 5521409 | tf_op jit(solution)/shard_map/while/body/eval_jaxpr/gkrbs,gskh->gkrbh/dot_general | solution.py:100
  174.9 1.0 constant_dynamic-slice_fusion.8
  176.0 0.8 fusion.98
  176.9 1.9 copy-done
  178.8 1.0 fusion.100
  179.9 3.4 %fusion.101 = f32[1,2,4,256,64]{3,4,2,1,0:T(8,128)S(1)} fusion(bf16[512,2,64,1]{0,2,3,1:T(8,128)(2,1)S(1)} %bitcast.229, f32[2,512,256,4]{2,1,3,0:T(8,128)} %copy-done, f32[2,4,256]{2,1,0:T(4,128)S(1)} %bitcast.228, pred[256,512]{0,1:T(8,128)(4,1)S(1)} %compare_and_fusion.5, f32[1,2,4,256,64]{3,4,2,1,0:T(8,128)S(1)} %get-tuple-element.487, ...), kind=kOutput, calls=%fused_computation.35.clone.1 | convolution fusion | flops 139853824 | bytes 5521409 | tf_op jit(solution)/shard_map/while/body/eval_jaxpr/gkrbs,gskh->gkrbh/dot_general | solution.py:100
  183.5 1.0 constant_dynamic-slice_fusion.8
  184.7 0.8 fusion.98
  185.5 1.9 copy-done
  187.4 1.0 fusion.100
  188.5 3.4 %fusion.101 = f32[1,2,4,256,64]{3,4,2,1,0:T(8,128)S(1)} fusion(bf16[512,2,64,1]{0,2,3,1:T(8,128)(2,1)S(1)} %bitcast.229, f32[2,512,256,4]{2,1,3,0:T(8,128)} %copy-done, f32[2,4,256]{2,1,0:T(4,128)S(1)} %bitcast.228, pred[256,512]{0,1:T(8,128)(4,1)S(1)} %compare_and_fusion.5, f32[1,2,4,256,64]{3,4,2,1,0:T(8,128)S(1)} %get-tuple-element.487, ...), kind=kOutput, calls=%fused_computation.35.clone.1 | convolution fusion | flops 139853824 | bytes 5521409 | tf_op jit(solution)/shard_map/while/body/eval_jaxpr/gkrbs,gskh->gkrbh/dot_general | solution.py:100
  192.1 1.0 constant_dynamic-slice_fusion.8
  194.1 1.9 copy-done
  196.1 1.0 fusion.100
  197.1 3.4 %fusion.101 = f32[1,2,4,256,64]{3,4,2,1,0:T(8,128)S(1)} fusion(bf16[512,2,64,1]{0,2,3,1:T(8,128)(2,1)S(1)} %bitcast.229, f32[2,512,256,4]{2,1,3,0:T(8,128)} %copy-done, f32[2,4,256]{2,1,0:T(4,128)S(1)} %bitcast.228, pred[256,512]{0,1:T(8,128)(4,1)S(1)} %compare_and_fusion.5, f32[1,2,4,256,64]{3,4,2,1,0:T(8,128)S(1)} %get-tuple-element.487, ...), kind=kOutput, calls=%fused_computation.35.clone.1 | convolution fusion | flops 139853824 | bytes 5521409 | tf_op jit(solution)/shard_map/while/body/eval_jaxpr/gkrbs,gskh->gkrbh/dot_general | solution.py:100
  200.8 1.0 constant_dynamic-slice_fusion.8
  202.8 1.9 copy-done
  204.7 1.0 fusion.100
  205.7 3.4 %fusion.101 = f32[1,2,4,256,64]{3,4,2,1,0:T(8,128)S(1)} fusion(bf16[512,2,64,1]{0,2,3,1:T(8,128)(2,1)S(1)} %bitcast.229, f32[2,512,256,4]{2,1,3,0:T(8,128)} %copy-done, f32[2,4,256]{2,1,0:T(4,128)S(1)} %bitcast.228, pred[256,512]{0,1:T(8,128)(4,1)S(1)} %compare_and_fusion.5, f32[1,2,4,256,64]{3,4,2,1,0:T(8,128)S(1)} %get-tuple-element.487, ...), kind=kOutput, calls=%fused_computation.35.clone.1 | convolution fusion | flops 139853824 | bytes 5521409 | tf_op jit(solution)/shard_map/while/body/eval_jaxpr/gkrbs,gskh->gkrbh/dot_general | solution.py:100
  209.4 1.0 constant_dynamic-slice_fusion.8
  211.4 1.9 copy-done
  213.3 1.0 fusion.100
  214.4 3.4 %fusion.101 = f32[1,2,4,256,64]{3,4,2,1,0:T(8,128)S(1)} fusion(bf16[512,2,64,1]{0,2,3,1:T(8,128)(2,1)S(1)} %bitcast.229, f32[2,512,256,4]{2,1,3,0:T(8,128)} %copy-done, f32[2,4,256]{2,1,0:T(4,128)S(1)} %bitcast.228, pred[256,512]{0,1:T(8,128)(4,1)S(1)} %compare_and_fusion.5, f32[1,2,4,256,64]{3,4,2,1,0:T(8,128)S(1)} %get-tuple-element.487, ...), kind=kOutput, calls=%fused_computation.35.clone.1 | convolution fusion | flops 139853824 | bytes 5521409 | tf_op jit(solution)/shard_map/while/body/eval_jaxpr/gkrbs,gskh->gkrbh/dot_general | solution.py:100
  218.0 1.0 constant_dynamic-slice_fusion.8
  219.1 0.8 fusion.98
  220.0 1.9 copy-done
  221.9 1.0 fusion.100
  223.0 3.4 %fusion.101 = f32[1,2,4,256,64]{3,4,2,1,0:T(8,128)S(1)} fusion(bf16[512,2,64,1]{0,2,3,1:T(8,128)(2,1)S(1)} %bitcast.229, f32[2,512,256,4]{2,1,3,0:T(8,128)} %copy-done, f32[2,4,256]{2,1,0:T(4,128)S(1)} %bitcast.228, pred[256,512]{0,1:T(8,128)(4,1)S(1)} %compare_and_fusion.5, f32[1,2,4,256,64]{3,4,2,1,0:T(8,128)S(1)} %get-tuple-element.487, ...), kind=kOutput, calls=%fused_computation.35.clone.1 | convolution fusion | flops 139853824 | bytes 5521409 | tf_op jit(solution)/shard_map/while/body/eval_jaxpr/gkrbs,gskh->gkrbh/dot_general | solution.py:100
  226.4 1.8 copy.33
  228.2 27.5 %while.34 = (s32[]{:T(128)}, f32[1,2,4,256]{3,2,1,0:T(4,128)S(1)}, f32[1,2,4,256]{3,2,1,0:T(4,128)S(1)}, f32[1,2,4,256,64]{3,4,2,1,0:T(8,128)S(1)}, s32[8,512]{1...) while((s32[]{:T(128)}, f32[1,2,4,256]{3,2,1,0:T(4,128)S(1)}, ...), condition=%wide.region_8.9_spmd.clone, body=%wide.region_5.8_spmd.clone.sunk | while | flops 282728960 | bytes 15870065 | solution.py:119
  229.3 1.0 fusion.92
  230.4 1.3 fusion.93
  232.8 1.0 fusion.92
  233.8 1.3 fusion.93
  236.2 1.0 fusion.92
  237.2 1.3 fusion.93
  239.6 1.0 fusion.92
  240.7 1.3 fusion.93
  243.1 1.0 fusion.92
  244.1 1.3 fusion.93
  246.5 1.0 fusion.92
  247.5 1.3 fusion.93
  249.9 1.0 fusion.92
  251.0 1.3 fusion.93
  253.4 1.0 fusion.92
  254.4 1.3 fusion.93
  255.8 21.4 %all-gather.14.cloned.1.call-done = bf16[2048,512]{1,0:T(8,128)(2,1)} async-done(((bf16[32,512]{1,0:T(8,128)(2,1)}), bf16[2048,512]{1,0:T(8,128)(2,1)}) %all-gather.14.cloned.1.call-update) | async-done | bytes 2097168 | tf_op jit(solution)/shard_map/all_gather | solution.py:146
  277.2 3.3 %fusion.42 = bf16[1,256,2048]{2,1,0:T(8,128)(2,1)} fusion(bf16[256,512]{0,1:T(8,128)(2,1)S(1)} %fusion.50, bf16[2048,512]{1,0:T(8,128)(2,1)} %all-gather.14.cloned.1.call-done), kind=kOutput, calls=%fused_computation.55 | convolution fusion | flops 537395200 | bytes 3407872 | tf_op jit(solution)/shard_map/dot_general | solution.py:144
  280.6 24.9 %reduce-scatter.2.cloned.1.call-done = bf16[1,256,512]{2,1,0:T(8,128)(2,1)} async-done(((bf16[1,256,2048]{2,1,0:T(8,128)(2,1)}), bf16[1,256,512]{2,1,0:T(8,128)(2,1)}) %reduce-scatter.2.cloned.1.call-update) | async-done | bytes 262160 | tf_op jit(solution)/shard_map/reduce_scatter | solution.py:151
  (190 shorter events, 21.2 us)
Async XLA Ops:
  6.5 104.5 %all-gather.8.cloned.1.call-start = ((), (), s32[]{:S(2)}) async-start(), calls=%async_computation.2 | async-start | bytes 1310720 | tf_op jit(solution)/shard_map/all_gather | solution.py:46
  7.3 110.7 %all-gather.10.cloned.1.call-start = ((), (), s32[]{:S(2)}) async-start(), calls=%async_computation.3 | async-start | bytes 2129920 | tf_op jit(solution)/shard_map/all_gather | solution.py:55
  8.0 149.4 %all-gather.6.cloned.1.call-start = ((), (), s32[]{:S(2)}) async-start(), calls=%async_computation.1 | async-start | bytes 2228224 | tf_op jit(solution)/shard_map/all_gather | solution.py:131
  9.6 107.0 %copy-start.2 = (f32[8]{0:T(128)S(1)}, f32[8]{0:T(128)}, u32[]{:S(2)}) copy-start(f32[8]{0:T(128)} %param.21) | copy-start | bytes 100
  9.6 216.8 %all-gather.12.cloned.1.call-start = ((), (), s32[]{:S(2)}) async-start(), calls=%async_computation.4 | async-start | bytes 2228224 | tf_op jit(solution)/shard_map/all_gather | solution.py:132
  111.0 3.5 %copy-start.1 = (bf16[1,256,2048]{2,1,0:T(8,128)(2,1)S(1)}, bf16[1,256,2048]{2,1,0:T(8,128)(2,1)}, u32[]{:S(2)}) copy-start(bf16[1,256,2048]{2,1,0:T(8,128)(2,1)} %all-gather.8.cloned.1.call-done) | copy-start | bytes 3145732
  115.8 161.4 %all-gather.14.cloned.1.call-start = ((), (), s32[]{:S(2)}) async-start(), calls=%async_computation.5 | async-start | bytes 2129920 | tf_op jit(solution)/shard_map/all_gather | solution.py:146
  116.4 189.1 %reduce-scatter.2.cloned.1.call-start = ((), (), s32[]{:S(2)}) async-start(), calls=%async_computation.6 | async-start | bytes 1310720 | tf_op jit(solution)/shard_map/reduce_scatter | solution.py:151
  159.6 2.0 copy-start
  168.2 2.0 copy-start
  176.9 2.0 copy-start
  185.5 2.0 copy-start
  194.1 2.0 copy-start
  202.7 2.0 copy-start
  211.3 2.0 copy-start
  220.0 2.0 copy-start
Sparse Core Ops, SparseCore 0:
  9.2 29.1 all-gather.7
  41.1 76.7 all-gather.9
  119.7 37.5 all-gather.5
  159.0 39.8 all-gather.11
  201.5 75.6 all-gather.13
  280.7 24.7 reduce-scatter.1
where the time goes:
time: 314 us; the launch traced here: 312 us
  blocking collectives  100 us (32%)
  waiting for transfers between devices  85.5 us (27%)
  matrix products  58.7 us (19%)
  local copies, waits for them, and re-layouts  27.1 us (9%)
  other arithmetic  24.6 us (8%)
  between operations  14.3 us (5%)
    all_gather x1, blocking collectives, on_device(): lax.all_gather(w_value, ('grp', 'tok'), axis=0, tiled=True)  52.4 us
    all_gather x1, blocking collectives, on_device(): lax.all_gather(w_key, ('grp', 'tok'), axis=0, tiled=True)  47.9 us
    dot_general x16, matrix products, attend_part(): jnp.einsum('gkrbs,gskh->gkrbh', expo_terms.astype(jnp.bfloat16), value_ro...  37.5 us
    all_gather x1, waiting for transfers between devices, on_device(): lax.all_gather(kv_prefix, 'tok', axis=1, tiled=True)  36.7 us
    reduce_scatter x1, waiting for transfers between devices, on_device(): lax.psum_scatter(partial_out.astype(jnp.bfloat16), 'mdl', scatter_dimensi...  24.9 us
    all_gather x1, waiting for transfers between devices, on_device(): lax.all_gather(w_out, ('grp', 'tok'), axis=0, tiled=True)  21.4 us
    reduce_sum x16, other arithmetic, attend_part(): denoms = denoms * rescale + jnp.sum(expo_terms, axis=-1)  16.2 us
    while x32, local copies, waits for them, and re-layouts  15.5 us
  transfers between devices with their start and end apart: 6, of which 4 were waited for; matrix products, arithmetic and copies ran while one was open for 29% of the time, Pallas kernels for 0%

commit v1 on v0

v1 whole, which is shorter than its diff:
```python
import functools

import jax
import jax.numpy as jnp
from jax import lax
from jax.experimental import pallas as pl
from jax.experimental.pallas import tpu as pltpu
from jax.sharding import Mesh
from jax.sharding import PartitionSpec as P

HD = 64
SCORE_SCALE = 0.015625
EPSILON = 1e-05
LOG_THETA = 16.11809565095832
LOG2E = 1.4426950408889634
BF16 = jnp.bfloat16
F32 = jnp.float32
VMEM_LIMIT = 50 * 1024 * 1024

NT = (((1,), (1,)), ((), ()))


def params(semantics=None):
    return pltpu.CompilerParams(vmem_limit_bytes=VMEM_LIMIT, dimension_semantics=semantics)


def vspec():
    return pl.BlockSpec(memory_space=pltpu.VMEM)


def sspec():
    return pl.BlockSpec(memory_space=pltpu.SMEM)


def half_turn(x):
    width = x.shape[1]
    lane = lax.broadcasted_iota(jnp.int32, x.shape, 1) % HD
    up = pltpu.roll(x, width - HD // 2, 1)
    down = pltpu.roll(x, HD // 2, 1)
    return jnp.where(lane < HD // 2, -up, down)


def kv_kernel(ids, *refs):
    hid = refs[0:8]
    wts = refs[8:12]
    gain, cos, sin, prefix, normed, own_new, send = refs[12:]
    mdl, grp, zed = ids[0], ids[1], ids[2]
    rows, cols = hid[0].shape
    count = 4
    for side in range(2):
        total = jnp.zeros((rows, 1), F32)
        for k in range(count):
            part = hid[side * count + k][...].astype(F32)
            total = total + jnp.sum(part * part, axis=1, keepdims=True)
        scale = lax.rsqrt(total / (cols * count) + EPSILON)
        for k in range(count):
            at = pl.multiple_of(lax.rem(mdl + k, count) * cols, cols)
            part = hid[side * count + k][...].astype(F32)
            part = part * scale * gain[:, pl.ds(at, cols)].astype(F32)
            normed[side * rows : (side + 1) * rows, pl.ds(at, cols)] = part.astype(BF16)
    depth = wts[0].shape[0]
    acc = None
    for k in range(4):
        at = pl.multiple_of(lax.rem(grp + k, 4) * depth, depth)
        part = jnp.dot(normed[:, pl.ds(at, depth)], wts[k][...], preferred_element_type=F32)
        acc = part if acc is None else acc + part
    lane = lax.broadcasted_iota(jnp.int32, acc.shape, 1)
    turned = acc * cos[...] + half_turn(acc) * sin[...]
    own = jnp.where(lane < HD, turned, acc).astype(BF16)
    own_new[...] = own
    for d in range(send.shape[0]):
        send[d] = jnp.where(zed > d, prefix[...].astype(F32), own.astype(F32)).astype(BF16)


def q_kernel(ids, normed, w0, w1, w2, w3, cos, sin, out):
    grp = ids[1]
    depth = w0.shape[0]
    acc = None
    for k, w in enumerate((w0, w1, w2, w3)):
        at = pl.multiple_of(lax.rem(grp + k, 4) * depth, depth)
        part = jnp.dot(normed[:, pl.ds(at, depth)], w[...], preferred_element_type=F32)
        acc = part if acc is None else acc + part
    turned = half_turn(acc)
    lane = lax.broadcasted_iota(jnp.int32, (acc.shape[0], 2 * HD), 1)
    for pair in range(2):
        cut = slice(pair * 2 * HD, (pair + 1) * 2 * HD)
        both = acc[:, cut] * cos[...] + turned[:, cut] * sin[...]
        both = both.astype(BF16).astype(F32) * SCORE_SCALE
        out[2 * pair] = jnp.where(lane < HD, both, 0.0).astype(BF16)
        out[2 * pair + 1] = jnp.where(lane < HD, pltpu.roll(both, HD, 1), 0.0).astype(BF16)


def attn_kernel(ids, sinks, q, own_prefix, own_new, recv, out, vals):
    zed, core, length = ids[2], ids[3], ids[4]
    half, pair = pl.program_id(0), pl.program_id(1)
    slots, block, _ = recv.shape
    rows = q.shape[1]
    lane = lax.broadcasted_iota(jnp.int32, (block, 2 * HD), 1)

    @pl.when((half == 0) & (pair == 0))
    def _():
        for j in range(slots - 1):
            src = lax.rem(zed + 1 + j, slots)
            vals[j] = jnp.where(lane < HD, 1.0, recv[src].astype(F32)).astype(BF16)
        vals[slots - 1] = jnp.where(lane < HD, 1.0, own_prefix[...].astype(F32)).astype(BF16)
        vals[slots] = jnp.where(lane < HD, 1.0, own_new[...].astype(F32)).astype(BF16)

    row = lax.broadcasted_iota(jnp.int32, (rows, block), 0) + half * rows
    col = lax.broadcasted_iota(jnp.int32, (rows, block), 1)
    swing = core * (block // 2)
    row_pos = lax.rem(row + swing, block)
    col_pos = lax.rem(col + swing, block)
    new_side = col_pos <= row_pos
    accs = []
    for i in range(2):
        queries = q[i]
        sink = sinks[core * 4 + pair * 2 + i]
        scores = []
        for j in range(slots - 1):
            src = lax.rem(zed + 1 + j, slots)
            scores.append(lax.dot_general(queries, recv[src], NT, preferred_element_type=F32))
        before = lax.dot_general(queries, own_prefix[...], NT, preferred_element_type=F32)
        after = lax.dot_general(queries, own_new[...], NT, preferred_element_type=F32)
        diagonal = jnp.where(new_side, after, before)
        top = diagonal
        for s in scores:
            top = jnp.maximum(top, s)
        top = jnp.maximum(jnp.max(top, axis=1, keepdims=True), sink)
        shift = top * LOG2E
        acc = jnp.zeros((rows, 2 * HD), F32)
        for j, s in enumerate(scores):
            p = jnp.exp2(s * LOG2E - shift).astype(BF16)
            acc = acc + jnp.dot(p, vals[j], preferred_element_type=F32)
        p = jnp.exp2(diagonal * LOG2E - shift)
        acc = acc + jnp.dot(
            jnp.where(new_side, 0.0, p).astype(BF16), vals[slots - 1], preferred_element_type=F32
        )
        acc = acc + jnp.dot(
            jnp.where(new_side, p, 0.0).astype(BF16), vals[slots], preferred_element_type=F32
        )
        lane2 = lax.broadcasted_iota(jnp.int32, acc.shape, 1)
        extra = jnp.exp2(sink * LOG2E - shift)
        accs.append(jnp.where(lane2 < HD, acc + extra, acc))
    first, second = accs
    lane2 = lax.broadcasted_iota(jnp.int32, first.shape, 1)
    low = lane2 < HD
    numer = jnp.where(low, pltpu.roll(first, HD, 1), second)
    denom = jnp.where(low, first, pltpu.roll(second, HD, 1))
    pos = lax.broadcasted_iota(jnp.int32, first.shape, 0) + half * rows
    pos = lax.rem(pos + swing, block) + zed * block
    out[0] = jnp.where(pos < length, numer / denom, 0.0).astype(BF16)


def out_kernel(ids, keep, got, *refs):
    grp, core = ids[1], ids[3]
    mine, theirs, out = refs[0:4], refs[4:8], refs[8]
    for k in range(4):
        part = lax.dot_general(keep[...], mine[k][...], NT, preferred_element_type=F32)
        part = part + lax.dot_general(got[...], theirs[k][...], NT, preferred_element_type=F32)
        out[lax.rem(grp + k, 4)] = part.astype(BF16)


def around(x, axis, size):
    got = {k: lax.ppermute(x, axis, [((i + k) % size, i) for i in range(size)]) for k in (1, 3, 2)}
    return [x, got[1], got[2], got[3]]


def swap(x):
    return lax.ppermute(x, "core", [(0, 1), (1, 0)])


def by_core(core, x, width):
    return jnp.stack([x[:, :width], x[:, width:]])


def on_device(
    hidden_in,
    suffix_len,
    norm_gain,
    w_query,
    w_key,
    w_value,
    w_out,
    sink_logits,
    prefix_keys,
    prefix_values,
):
    grp, zed, core, mdl = (lax.axis_index(a) for a in ("grp", "z", "core", "mdl"))
    zsize = lax.axis_size("z")
    hidden = hidden_in[0]
    tok_rows, feats = hidden.shape
    chip_rows = 2 * tok_rows
    ids = jnp.stack([mdl, grp, zed, core, suffix_len[0]]).astype(jnp.int32)

    w_kv = jnp.concatenate([by_core(core, w_key, HD), by_core(core, w_value, HD)], axis=2)
    w_rest = jnp.concatenate(
        [by_core(core, w_query, 4 * HD), by_core(core, w_out, 4 * HD)], axis=2
    )

    def spread(w):
        full = jnp.broadcast_to(w[None], (zsize,) + w.shape).reshape((2 * zsize,) + w.shape[1:])
        got = lax.all_to_all(full, ("z", "core"), 0, 0, tiled=True)
        return got.reshape(-1, w.shape[2])

    w_kv = around(spread(w_kv), "grp", 4)
    hid = around(hidden, "mdl", 4)
    hid_other = [swap(h) for h in hid]
    w_rest = spread(w_rest)
    w_q = around(w_rest[:, : 4 * HD], "grp", 4)
    w_o = around(w_rest[:, 4 * HD :], "grp", 4)
    w_o_other = [swap(w) for w in w_o]

    heads = jnp.concatenate(
        [by_core(core, prefix_keys[0], HD), by_core(core, prefix_values[0], HD)], axis=2
    )
    mine = jnp.where(core == 0, heads[0], heads[1])
    others = jnp.where(core == 0, heads[1], heads[0])
    prefix = jnp.concatenate([mine, swap(others)], axis=0)

    row = jnp.arange(chip_rows, dtype=jnp.int32)
    slot = lax.rem(row + core * tok_rows, chip_rows) + zed * chip_rows
    position = (slot + zsize * chip_rows).astype(F32)
    frequency = jnp.exp(-LOG_THETA * 2.0 * jnp.arange(HD // 2, dtype=F32) / HD)
    angles = position[:, None] * frequency[None, :]
    cos = jnp.tile(jnp.cos(angles), (1, 4))
    sin = jnp.tile(jnp.sin(angles), (1, 4))

    normed, own_new, send = pl.pallas_call(
        kv_kernel,
        out_shape=(
            jax.ShapeDtypeStruct((chip_rows, 4 * feats), BF16),
            jax.ShapeDtypeStruct((chip_rows, 2 * HD), BF16),
            jax.ShapeDtypeStruct((zsize, chip_rows, 2 * HD), BF16),
        ),
        in_specs=[sspec()] + [vspec()] * 16,
        out_specs=(vspec(),) * 3,
        compiler_params=params(),
        name="kv_proj",
    )(ids, *hid, *hid_other, *w_kv, norm_gain.reshape(1, -1), cos, sin, prefix)
    recv = lax.all_to_all(send, "z", 0, 0)

    q = pl.pallas_call(
        q_kernel,
        out_shape=jax.ShapeDtypeStruct((4, chip_rows, 2 * HD), BF16),
        in_specs=[sspec()] + [vspec()] * 7,
        out_specs=vspec(),
        compiler_params=params(),
        name="q_proj",
    )(ids, normed, *w_q, cos, sin)

    mixed = pl.pallas_call(
        attn_kernel,
        out_shape=jax.ShapeDtypeStruct((2, tok_rows, 4 * HD), BF16),
        grid=(2, 2),
        in_specs=[
            sspec(),
            sspec(),
            pl.BlockSpec((2, tok_rows, 2 * HD), lambda i, j: (j, i, 0)),
            vspec(),
            vspec(),
            vspec(),
        ],
        out_specs=pl.BlockSpec((1, tok_rows, 2 * HD), lambda i, j: (i, 0, j)),
        scratch_shapes=[pltpu.VMEM((zsize + 1, chip_rows, 2 * HD), BF16)],
        compiler_params=params(("arbitrary", "arbitrary")),
        name="attention",
    )(ids, sink_logits, q, prefix, own_new, recv)

    got = swap(mixed[1])
    partial_out = pl.pallas_call(
        out_kernel,
        out_shape=jax.ShapeDtypeStruct((4, tok_rows, feats), BF16),
        in_specs=[sspec()] + [vspec()] * 10,
        out_specs=vspec(),
        compiler_params=params(),
        name="out_proj",
    )(ids, mixed[0], got, *w_o, *w_o_other)
    parts = lax.all_to_all(partial_out, "mdl", 0, 0)
    return jnp.sum(parts.astype(F32), axis=0).astype(BF16)[None]


def solution(mesh):
    groups, toks, mdls = mesh.devices.shape
    cores = Mesh(
        mesh.devices.reshape(groups, toks // 2, 2, mdls), ("grp", "z", "core", "mdl")
    )
    tok = ("z", "core")
    placed = (
        P("grp", tok, "mdl"),
        P("grp"),
        P(),
        P(("grp",) + tok, "mdl"),
        P(("grp",) + tok, "mdl"),
        P(("grp",) + tok, "mdl"),
        P(("grp",) + tok, "mdl"),
        P("mdl"),
        P("grp", tok, "mdl"),
        P("grp", tok, "mdl"),
    )
    return jax.shard_map(
        on_device,
        mesh=cores,
        in_specs=placed,
        out_specs=P("grp", tok, "mdl"),
        check_vma=False,
    )
```

time: 314 us -> 133 us (0.42)
  blocking collectives: 100 us -> 20 us
  matrix products: 58.7 us -> 0 us
  waiting for transfers between devices: 85.5 us -> 34.1 us
  starting transfers between devices: 0.38 us -> 43.5 us
  Pallas kernels: 0 us -> 25.1 us
  other arithmetic: 24.6 us -> 2.96 us
  local copies, waits for them, and re-layouts: 27.1 us -> 6.33 us
  between operations: 14.3 us -> 0.87 us
    all_gather x2 -> x0, blocking collectives: 100 us -> none  [the longest x1 52.4 us: on_device(): lax.all_gather(w_value, ('grp', 'tok'), axis=0, tiled=True)]
    dot_general x36 -> x0, matrix products: 58.7 us -> none  [the longest x16 37.5 us: attend_part(): jnp.einsum('gkrbs,gskh->gkrbh', expo_terms.astype(jnp.bfloat16), value_ro...]
    all_gather x5 -> x0, waiting for transfers between devices: 58.6 us -> none  [the longest x1 36.7 us: on_device(): lax.all_gather(kv_prefix, 'tok', axis=1, tiled=True)]
    ppermute x0 -> x22, waiting for transfers between devices: none -> 27.5 us  [the longest x12 26.2 us: around(): lax.ppermute(x, axis, [((i + k) % size, i) for i in range(size)])]
    pallas_call x0 -> x4, Pallas kernels: none -> 25.1 us  [the longest x1 17 us: on_device(): pl.pallas_call(attn_kernel, out_shape=jax.ShapeDtypeStruct((2, tok_rows,...]
    reduce_scatter x1 -> x0, waiting for transfers between devices: 24.9 us -> none  [on_device(): lax.psum_scatter(partial_out.astype(jnp.bfloat16), 'mdl', scatter_dimensi...]
    ppermute x0 -> x22, starting transfers between devices: none -> 22.1 us  [the longest x12 20.7 us: around(): lax.ppermute(x, axis, [((i + k) % size, i) for i in range(size)])]
    all_to_all x0 -> x3, starting transfers between devices: none -> 21.4 us  [the longest x2 14.2 us: spread(): got = lax.all_to_all(full, ('z', 'core'), 0, 0, tiled=True)]
  transfers between devices with their start and end apart: 6 -> 25, of which waited for: 4 -> 9; matrix products, arithmetic and copies ran while one was open for 29% -> 3% of each run, Pallas kernels for 0% -> 17%
where the time goes in v1:
time: 133 us
  starting transfers between devices  43.5 us (33%)
  waiting for transfers between devices  34.1 us (26%)
  Pallas kernels  25.1 us (19%)
  blocking collectives  20 us (15%)
  local copies, waits for them, and re-layouts  6.33 us (5%)
  other arithmetic  2.96 us (2%)
    ppermute x12, waiting for transfers between devices, around(): lax.ppermute(x, axis, [((i + k) % size, i) for i in range(size)])  26.2 us
    ppermute x12, starting transfers between devices, around(): lax.ppermute(x, axis, [((i + k) % size, i) for i in range(size)])  20.7 us
    all_to_all x1, blocking collectives, on_device(): parts = lax.all_to_all(partial_out, 'mdl', 0, 0)  20 us
    pallas_call x1, Pallas kernels, on_device(): pl.pallas_call(attn_kernel, out_shape=jax.ShapeDtypeStruct((2, tok_rows,...  17 us
    all_to_all x2, starting transfers between devices, spread(): got = lax.all_to_all(full, ('z', 'core'), 0, 0, tiled=True)  14.2 us
    all_to_all x1, starting transfers between devices, on_device(): recv = lax.all_to_all(send, 'z', 0, 0)  7.25 us
    all_to_all x2, waiting for transfers between devices, spread(): got = lax.all_to_all(full, ('z', 'core'), 0, 0, tiled=True)  6.6 us
    pallas_call x1, Pallas kernels, on_device(): pl.pallas_call(kv_kernel, out_shape=(jax.ShapeDtypeStruct((chip_rows, 4 *...  3.56 us
  transfers between devices with their start and end apart: 25, of which 9 were waited for; matrix products, arithmetic and copies ran while one was open for 3% of the time, Pallas kernels for 17%

profile of v1, /device:TPU:32, one launch (start us, length us, event | category | flops | bytes accessed | tf_op | source)
XLA Modules:
  0.0 132.8 jit_solution(14633094967297515070)
XLA Ops:
  0.0 0.9 slice_bitcast_fusion.11
  0.9 0.1 maximum_maximum_fusion.2
  1.0 0.7 broadcast_in_dim.6
  1.6 8.6 %all-to-all-start = ((bf16[16,32,128]{2,1,0:T(8,128)(2,1)}), bf16[16,32,128]{2,1,0:T(8,128)(2,1)S(1)}, u32[]{:S(2)}, u32[]{:S(2)}) async-start(bf16[16,32,128]{2,1,0:T(8,128)(2,1)} %bitcast.9), calls=%async_computation | async-start | bytes 262144 | tf_op jit(solution)/shard_map/all_to_all | solution.py:202
  10.2 0.8 slice_bitcast_fusion.7
  11.0 6.6 %all-to-all-done = bf16[16,32,128]{2,1,0:T(8,128)(2,1)S(1)} async-done(((bf16[16,32,128]{2,1,0:T(8,128)(2,1)}), bf16[16,32,128]{2,1,0:T(8,128)(2,1)S(1)}, u32[]{:S(2)}, u32[]{:S(2)}) %all-to-all-start) | async-done | bytes 131104 | tf_op jit(solution)/shard_map/all_to_all | solution.py:202
  17.6 0.9 broadcast_in_dim.7
  18.5 5.6 %all-to-all-start.1 = ((bf16[16,32,512]{2,1,0:T(8,128)(2,1)}), bf16[16,32,512]{2,1,0:T(8,128)(2,1)}, u32[]{:S(2)}, u32[]{:S(2)}) async-start(bf16[16,32,512]{2,1,0:T(8,128)(2,1)} %bitcast.25), calls=%async_computation.1 | async-start | bytes 1048576 | tf_op jit(solution)/shard_map/all_to_all | solution.py:202
  24.1 0.1 slice_bitcast_fusion.3
  24.2 0.1 maximum_maximum_fusion
  24.3 0.6 select_bitcast_fusion.1
  24.9 0.1 collective-permute-start.10
  25.1 3.0 %collective-permute-start = (bf16[256,512]{1,0:T(8,128)(2,1)S(1)}, bf16[256,512]{1,0:T(8,128)(2,1)S(1)}, u32[]{:S(2)}, u32[]{:S(2)}) collective-permute-start(bf16[256,512]{1,0:T(8,128)(2,1)S(1)} %bitcast.50), channel_id=1, source_target_pairs={{1,0},{2,1},{3,2},{0,3},{5,4},{6,5},{7,6},{4,7},{9,8},{10,9},{11,1... | collective-permute-start | bytes 786440 | tf_op jit(solution)/shard_map/ppermute | solution.py:164
  28.1 0.6 collective-permute-start.1
  28.8 1.0 collective-permute-start.2
  29.7 0.0 collective-permute-start.3
  29.7 2.8 %collective-permute-start.7 = (bf16[512,128]{1,0:T(8,128)(2,1)S(1)}, bf16[512,128]{1,0:T(8,128)(2,1)S(1)}, u32[]{:S(2)}, u32[]{:S(2)}) collective-permute-start(bf16[512,128]{1,0:T(8,128)(2,1)S(1)} %bitcast.46), channel_id=1, source_target_pairs={{64,0},{128,64},{192,128},{0,192},{65,1},{129,65},{193,129},{1,193... | collective-permute-start | bytes 393224 | tf_op jit(solution)/shard_map/ppermute | solution.py:164
  32.6 7.2 %collective-permute-done.refs_1_ = bf16[256,512]{1,0:T(8,128)(2,1)S(1)} collective-permute-done((bf16[256,512]{1,0:T(8,128)(2,1)S(1)}, bf16[256,512]{1,0:T(8,128)(2,1)S(1)}, u32[]{:S(2)}, u32[]{:S(2)}) %collective-permute-start) | collective-permute-done | bytes 262176 | tf_op jit(solution)/shard_map/ppermute | solution.py:164
  39.8 3.0 %collective-permute-start.8 = (bf16[512,128]{1,0:T(8,128)(2,1)S(1)}, bf16[512,128]{1,0:T(8,128)(2,1)S(1)}, u32[]{:S(2)}, u32[]{:S(2)}) collective-permute-start(bf16[512,128]{1,0:T(8,128)(2,1)S(1)} %bitcast.47), channel_id=1, source_target_pairs={{128,0},{192,64},{0,128},{64,192},{129,1},{193,65},{1,129},{65,193... | collective-permute-start | bytes 393224 | tf_op jit(solution)/shard_map/ppermute | solution.py:164
  42.8 0.0 collective-permute-done.1.refs_2_
  42.8 0.6 collective-permute-start.9
  43.4 0.1 collective-permute-done.2.refs_3_
  43.5 0.0 collective-permute-start.4
  43.5 0.0 collective-permute-done.3.refs_4_
  43.5 0.5 collective-permute-start.5
  44.0 0.0 collective-permute-done.7.refs_9_
  44.0 0.1 collective-permute-start.6
  44.1 0.3 multiply_sine_fusion
  45.1 0.1 copy.11.refs_13_.cos
  45.3 0.1 copy.12.refs_14_.sin
  45.5 0.1 stack.73.ids
  45.5 0.9 pad_maximum_fusion.refs_15_.own_prefix
  46.4 1.0 collective-permute-done.8.refs_10_
  47.4 2.0 %collective-permute-done.9.refs_11_ = bf16[512,128]{1,0:T(8,128)(2,1)S(1)} collective-permute-done((bf16[512,128]{1,0:T(8,128)(2,1)S(1)}, bf16[512,128]{1,0:T(8,128)(2,1)S(1)}, u32[]{:S(2)}, u32[]{:S(2)}) %collective-permute-start.9) | collective-permute-done | bytes 131104 | tf_op jit(solution)/shard_map/ppermute | solution.py:164
  49.4 0.0 collective-permute-done.4.refs_5_
  49.4 3.6 %kv_proj.1 = (bf16[512,2048]{1,0:T(8,128)(2,1)}, bf16[512,128]{1,0:T(8,128)(2,1)S(1)}, bf16[8,512,128]{2,1,0:T(8,128)(2,1)}) custom-call(s32[5]{0:T(128)S(1)} %stack.73.ids, bf16[256,512]{1,0:T(8,128)(2,1)S(1)} %bitcast.54, bf16[256,512]{1,0:T(8,128)(2,1)S(1)} %collective-permute-done.refs_1_, bf16[256,512]{1,0:T(8,128)(2,1)S(1)} %collective-permute-done.1.refs_2_, ...), custom_call_target="tpu_custom_call" | custom-call | tf_op jit(solution)/shard_map/kv_proj/pallas_call | solution.py:228
  53.0 0.7 copy-done.1
  53.6 0.0 all-to-all-done.1
  53.6 7.2 %all-to-all-start.2 = ((bf16[8,512,128]{2,1,0:T(8,128)(2,1)}), bf16[8,512,128]{2,1,0:T(8,128)(2,1)S(1)}, u32[]{:S(2)}, u32[]{:S(2)}) async-start(bf16[8,512,128]{2,1,0:T(8,128)(2,1)} %get-tuple-element.10), calls=%async_computation.2 | async-start | bytes 2097152 | tf_op jit(solution)/shard_map/all_to_all | solution.py:240
  60.9 1.1 fusion.4
  62.0 0.3 collective-permute-start.11
  62.3 2.9 %collective-permute-start.12 = (bf16[512,256]{1,0:T(8,128)(2,1)S(1)}, bf16[512,256]{1,0:T(8,128)(2,1)S(1)}, u32[]{:S(2)}, u32[]{:S(2)}) collective-permute-start(bf16[512,256]{1,0:T(8,128)(2,1)S(1)} %get-tuple-element.12.w0), channel_id=1, source_target_pairs={{128,0},{192,64},{0,128},{64,192},{129,1},{193,65},{1,129},{65,193... | collective-permute-start | bytes 786440 | tf_op jit(solution)/shard_map/ppermute | solution.py:164
  65.2 1.5 %collective-permute-start.15 = (bf16[512,256]{1,0:T(8,128)(2,1)S(1)}, bf16[512,256]{1,0:T(8,128)(2,1)S(1)}, u32[]{:S(2)}, u32[]{:S(2)}) collective-permute-start(bf16[512,256]{1,0:T(8,128)(2,1)S(1)} %get-tuple-element.11.refs_0_), channel_id=1, source_target_pairs={{64,0},{128,64},{192,128},{0,192},{65,1},{129,65},{193,129},{1,193... | collective-permute-start | bytes 786440 | tf_op jit(solution)/shard_map/ppermute | solution.py:164
  66.7 0.5 collective-permute-start.16
  67.2 0.4 collective-permute-start.17
  67.6 5.4 %collective-permute-done.11.w1 = bf16[512,256]{1,0:T(8,128)(2,1)S(1)} collective-permute-done((bf16[512,256]{1,0:T(8,128)(2,1)S(1)}, bf16[512,256]{1,0:T(8,128)(2,1)S(1)}, u32[]{:S(2)}, u32[]{:S(2)}) %collective-permute-start.11) | collective-permute-done | bytes 262176 | tf_op jit(solution)/shard_map/ppermute | solution.py:164
  73.0 3.9 %collective-permute-start.13 = (bf16[512,256]{1,0:T(8,128)(2,1)S(1)}, bf16[512,256]{1,0:T(8,128)(2,1)S(1)}, u32[]{:S(2)}, u32[]{:S(2)}) collective-permute-start(bf16[512,256]{1,0:T(8,128)(2,1)S(1)} %get-tuple-element.12.w0), channel_id=1, source_target_pairs={{192,0},{0,64},{64,128},{128,192},{193,1},{1,65},{65,129},{129,193... | collective-permute-start | bytes 786440 | tf_op jit(solution)/shard_map/ppermute | solution.py:164
  76.9 5.6 %collective-permute-done.15.refs_1_ = bf16[512,256]{1,0:T(8,128)(2,1)S(1)} collective-permute-done((bf16[512,256]{1,0:T(8,128)(2,1)S(1)}, bf16[512,256]{1,0:T(8,128)(2,1)S(1)}, u32[]{:S(2)}, u32[]{:S(2)}) %collective-permute-start.15) | collective-permute-done | bytes 262176 | tf_op jit(solution)/shard_map/ppermute | solution.py:164
  82.5 0.0 collective-permute-start.19
  82.5 0.0 collective-permute-done.16.refs_2_
  82.5 0.5 collective-permute-start.20
  83.0 0.0 collective-permute-done.17.refs_3_
  83.0 0.1 collective-permute-start.21
  83.1 4.9 %collective-permute-done.13.w3 = bf16[512,256]{1,0:T(8,128)(2,1)S(1)} collective-permute-done((bf16[512,256]{1,0:T(8,128)(2,1)S(1)}, bf16[512,256]{1,0:T(8,128)(2,1)S(1)}, u32[]{:S(2)}, u32[]{:S(2)}) %collective-permute-start.13) | collective-permute-done | bytes 262176 | tf_op jit(solution)/shard_map/ppermute | solution.py:164
  88.0 2.6 %q_proj.1.q = bf16[4,512,128]{2,1,0:T(8,128)(2,1)S(1)} custom-call(s32[5]{0:T(128)S(1)} %stack.73.ids, bf16[512,2048]{1,0:T(8,128)(2,1)} %get-tuple-element.8.normed, bf16[512,256]{1,0:T(8,128)(2,1)S(1)} %get-tuple-element.12.w0, bf16[512,256]{1,0:T(8,128)(2,1)S(1)} %collective-permute-done.11.w1, bf16[512,256]{1,0:T(8,128)(2,1)S(1)} %collective-permute-done.12.w2, ...), custom_call_target="tpu_custom_call" | custom-call | tf_op jit(solution)/shard_map/q_proj/pallas_call | solution.py:242
  90.6 0.0 all-to-all-done.2.recv
  90.7 0.0 copy-start.2
  90.7 0.9 copy-done.2
  91.6 17.0 %attention.1 = bf16[2,256,256]{2,1,0:T(8,128)(2,1)S(1)} custom-call(s32[5]{0:T(128)S(1)} %stack.73.ids, f32[8]{0:T(128)S(1)} %copy-done.3, bf16[4,512,128]{2,1,0:T(8,128)(2,1)S(1)} %q_proj.1.q, bf16[512,128]{1,0:T(8,128)(2,1)S(1)} %pad_maximum_fusion.refs_15_.own_prefix, bf16[512,128]{1,0:T(8,128)(2,1)S(1)} %copy-done.2, ...), custom_call_target="tpu_custom_call" | custom-call | tf_op jit(solution)/shard_map/attention/pallas_call | solution.py:251
  108.6 0.1 collective-permute-start.14
  108.7 1.3 collective-permute-done.14.got
  110.0 1.9 %out_proj.1 = bf16[4,256,512]{2,1,0:T(8,128)(2,1)S(1)} custom-call(s32[5]{0:T(128)S(1)} %stack.73.ids, bf16[256,256]{1,0:T(8,128)(2,1)S(1)} %get-tuple-element.14.keep, bf16[256,256]{1,0:T(8,128)(2,1)S(1)} %collective-permute-done.14.got, bf16[512,256]{1,0:T(8,128)(2,1)S(1)} %get-tuple-element.11.refs_0_, ...), custom_call_target="tpu_custom_call" | custom-call | tf_op jit(solution)/shard_map/out_proj/pallas_call | solution.py:270
  111.9 20.0 %all_to_all.20 = bf16[4,256,512]{2,1,0:T(8,128)(2,1)S(1)} all-to-all(bf16[4,256,512]{2,1,0:T(8,128)(2,1)S(1)} %out_proj.1), channel_id=1, replica_groups=mesh['grp'=4,'z'=8,'core'=2,'mdl'=4] {'mdl'}, dimensions={0} | all-to-all | bytes 2097152 | tf_op jit(solution)/shard_map/all_to_all | solution.py:278
  131.9 0.9 reduce_sum.12
  (29 shorter events, 0.1 us)
Async XLA Ops:
  0.0 24.0 %copy-start.5 = (bf16[1,256,128]{2,1,0:T(8,128)(2,1)S(1)}, bf16[1,256,128]{2,1,0:T(8,128)(2,1)}, u32[]{:S(2)}) copy-start(bf16[1,256,128]{2,1,0:T(8,128)(2,1)} %param.18) | copy-start | bytes 196612
  0.0 24.1 %copy-start.4 = (bf16[1,256,128]{2,1,0:T(8,128)(2,1)S(1)}, bf16[1,256,128]{2,1,0:T(8,128)(2,1)}, u32[]{:S(2)}) copy-start(bf16[1,256,128]{2,1,0:T(8,128)(2,1)} %param.19) | copy-start | bytes 196612
  0.0 25.1 %copy-start = (bf16[1,256,512]{2,1,0:T(8,128)(2,1)S(1)}, bf16[1,256,512]{2,1,0:T(8,128)(2,1)}, u32[]{:S(2)}) copy-start(bf16[1,256,512]{2,1,0:T(8,128)(2,1)} %param.10) | copy-start | bytes 786436
  1.6 16.0 %all-to-all-start = ((bf16[16,32,128]{2,1,0:T(8,128)(2,1)}), bf16[16,32,128]{2,1,0:T(8,128)(2,1)S(1)}, u32[]{:S(2)}, u32[]{:S(2)}) async-start(bf16[16,32,128]{2,1,0:T(8,128)(2,1)} %bitcast.9), calls=%async_computation | async-start | bytes 262144 | tf_op jit(solution)/shard_map/all_to_all | solution.py:202
  18.5 27.0 %copy-start.7 = (bf16[2048]{0:T(1024)(128)(2,1)S(1)}, bf16[2048]{0:T(1024)(128)(2,1)}, u32[]{:S(2)}) copy-start(bf16[2048]{0:T(1024)(128)(2,1)} %param.12) | copy-start | bytes 12292
  18.5 35.2 %all-to-all-start.1 = ((bf16[16,32,512]{2,1,0:T(8,128)(2,1)}), bf16[16,32,512]{2,1,0:T(8,128)(2,1)}, u32[]{:S(2)}, u32[]{:S(2)}) async-start(bf16[16,32,512]{2,1,0:T(8,128)(2,1)} %bitcast.25), calls=%async_computation.1 | async-start | bytes 1048576 | tf_op jit(solution)/shard_map/all_to_all | solution.py:202
  24.9 4.8 %collective-permute-start.10 = (bf16[256,128]{1,0:T(8,128)(2,1)S(1)}, bf16[256,128]{1,0:T(8,128)(2,1)S(1)}, u32[]{:S(2)}, u32[]{:S(2)}) collective-permute-start(bf16[256,128]{1,0:T(8,128)(2,1)S(1)} %get-tuple-element.16), channel_id=1, source_target_pairs={{0,4},{4,0},{1,5},{5,1},{2,6},{6,2},{3,7},{7,3},{8,12},{12,8},{9,1... | collective-permute-start | bytes 196616 | tf_op jit(solution)/shard_map/ppermute | solution.py:169
  25.1 14.7 %collective-permute-start = (bf16[256,512]{1,0:T(8,128)(2,1)S(1)}, bf16[256,512]{1,0:T(8,128)(2,1)S(1)}, u32[]{:S(2)}, u32[]{:S(2)}) collective-permute-start(bf16[256,512]{1,0:T(8,128)(2,1)S(1)} %bitcast.50), channel_id=1, source_target_pairs={{1,0},{2,1},{3,2},{0,3},{5,4},{6,5},{7,6},{4,7},{9,8},{10,9},{11,1... | collective-permute-start | bytes 786440 | tf_op jit(solution)/shard_map/ppermute | solution.py:164
  28.1 14.7 %collective-permute-start.1 = (bf16[256,512]{1,0:T(8,128)(2,1)S(1)}, bf16[256,512]{1,0:T(8,128)(2,1)S(1)}, u32[]{:S(2)}, u32[]{:S(2)}) collective-permute-start(bf16[256,512]{1,0:T(8,128)(2,1)S(1)} %bitcast.51), channel_id=1, source_target_pairs={{2,0},{3,1},{0,2},{1,3},{6,4},{7,5},{4,6},{5,7},{10,8},{11,9},{8,1... | collective-permute-start | bytes 786440 | tf_op jit(solution)/shard_map/ppermute | solution.py:164
  28.8 14.8 %collective-permute-start.2 = (bf16[256,512]{1,0:T(8,128)(2,1)S(1)}, bf16[256,512]{1,0:T(8,128)(2,1)S(1)}, u32[]{:S(2)}, u32[]{:S(2)}) collective-permute-start(bf16[256,512]{1,0:T(8,128)(2,1)S(1)} %bitcast.52), channel_id=1, source_target_pairs={{3,0},{0,1},{1,2},{2,3},{7,4},{4,5},{5,6},{6,7},{11,8},{8,9},{9,10... | collective-permute-start | bytes 786440 | tf_op jit(solution)/shard_map/ppermute | solution.py:164
  29.7 13.8 %collective-permute-start.3 = (bf16[256,512]{1,0:T(8,128)(2,1)S(1)}, bf16[256,512]{1,0:T(8,128)(2,1)S(1)}, u32[]{:S(2)}, u32[]{:S(2)}) collective-permute-start(bf16[256,512]{1,0:T(8,128)(2,1)S(1)} %bitcast.53), channel_id=1, source_target_pairs={{0,4},{4,0},{1,5},{5,1},{2,6},{6,2},{3,7},{7,3},{8,12},{12,8},{9,1... | collective-permute-start | bytes 786440 | tf_op jit(solution)/shard_map/ppermute | solution.py:169
  29.7 15.4 %copy-start.6 = (bf16[256,128]{1,0:T(8,128)(2,1)}, bf16[256,128]{1,0:T(8,128)(2,1)S(1)}, u32[]{:S(2)}) copy-start(bf16[256,128]{1,0:T(8,128)(2,1)S(1)} %collective-permute-done.10) | copy-start | bytes 196612
  29.7 14.3 %collective-permute-start.7 = (bf16[512,128]{1,0:T(8,128)(2,1)S(1)}, bf16[512,128]{1,0:T(8,128)(2,1)S(1)}, u32[]{:S(2)}, u32[]{:S(2)}) collective-permute-start(bf16[512,128]{1,0:T(8,128)(2,1)S(1)} %bitcast.46), channel_id=1, source_target_pairs={{64,0},{128,64},{192,128},{0,192},{65,1},{129,65},{193,129},{1,193... | collective-permute-start | bytes 393224 | tf_op jit(solution)/shard_map/ppermute | solution.py:164
  39.8 7.6 %collective-permute-start.8 = (bf16[512,128]{1,0:T(8,128)(2,1)S(1)}, bf16[512,128]{1,0:T(8,128)(2,1)S(1)}, u32[]{:S(2)}, u32[]{:S(2)}) collective-permute-start(bf16[512,128]{1,0:T(8,128)(2,1)S(1)} %bitcast.47), channel_id=1, source_target_pairs={{128,0},{192,64},{0,128},{64,192},{129,1},{193,65},{1,129},{65,193... | collective-permute-start | bytes 393224 | tf_op jit(solution)/shard_map/ppermute | solution.py:164
  42.8 6.6 %collective-permute-start.9 = (bf16[512,128]{1,0:T(8,128)(2,1)S(1)}, bf16[512,128]{1,0:T(8,128)(2,1)S(1)}, u32[]{:S(2)}, u32[]{:S(2)}) collective-permute-start(bf16[512,128]{1,0:T(8,128)(2,1)S(1)} %bitcast.48), channel_id=1, source_target_pairs={{192,0},{0,64},{64,128},{128,192},{193,1},{1,65},{65,129},{129,193... | collective-permute-start | bytes 393224 | tf_op jit(solution)/shard_map/ppermute | solution.py:164
  43.5 5.9 %collective-permute-start.4 = (bf16[256,512]{1,0:T(8,128)(2,1)S(1)}, bf16[256,512]{1,0:T(8,128)(2,1)S(1)}, u32[]{:S(2)}, u32[]{:S(2)}) collective-permute-start(bf16[256,512]{1,0:T(8,128)(2,1)S(1)} %collective-permute-done.refs_1_), channel_id=1, source_target_pairs={{0,4},{4,0},{1,5},{5,1},{2,6},{6,2},{3,7},{7,3},{8,12},{12,8},{9,1... | collective-permute-start | bytes 786440 | tf_op jit(solution)/shard_map/ppermute | solution.py:169
  43.5 5.9 %collective-permute-start.5 = (bf16[256,512]{1,0:T(8,128)(2,1)S(1)}, bf16[256,512]{1,0:T(8,128)(2,1)S(1)}, u32[]{:S(2)}, u32[]{:S(2)}) collective-permute-start(bf16[256,512]{1,0:T(8,128)(2,1)S(1)} %collective-permute-done.1.refs_2_), channel_id=1, source_target_pairs={{0,4},{4,0},{1,5},{5,1},{2,6},{6,2},{3,7},{7,3},{8,12},{12,8},{9,1... | collective-permute-start | bytes 786440 | tf_op jit(solution)/shard_map/ppermute | solution.py:169
  44.0 5.4 %collective-permute-start.6 = (bf16[256,512]{1,0:T(8,128)(2,1)S(1)}, bf16[256,512]{1,0:T(8,128)(2,1)S(1)}, u32[]{:S(2)}, u32[]{:S(2)}) collective-permute-start(bf16[256,512]{1,0:T(8,128)(2,1)S(1)} %collective-permute-done.2.refs_3_), channel_id=1, source_target_pairs={{0,4},{4,0},{1,5},{5,1},{2,6},{6,2},{3,7},{7,3},{8,12},{12,8},{9,1... | collective-permute-start | bytes 786440 | tf_op jit(solution)/shard_map/ppermute | solution.py:169
  53.0 0.7 copy-start.1
  53.6 37.0 %all-to-all-start.2 = ((bf16[8,512,128]{2,1,0:T(8,128)(2,1)}), bf16[8,512,128]{2,1,0:T(8,128)(2,1)S(1)}, u32[]{:S(2)}, u32[]{:S(2)}) async-start(bf16[8,512,128]{2,1,0:T(8,128)(2,1)} %get-tuple-element.10), calls=%async_computation.2 | async-start | bytes 2097152 | tf_op jit(solution)/shard_map/all_to_all | solution.py:240
  62.0 11.0 %collective-permute-start.11 = (bf16[512,256]{1,0:T(8,128)(2,1)S(1)}, bf16[512,256]{1,0:T(8,128)(2,1)S(1)}, u32[]{:S(2)}, u32[]{:S(2)}) collective-permute-start(bf16[512,256]{1,0:T(8,128)(2,1)S(1)} %get-tuple-element.12.w0), channel_id=1, source_target_pairs={{64,0},{128,64},{192,128},{0,192},{65,1},{129,65},{193,129},{1,193... | collective-permute-start | bytes 786440 | tf_op jit(solution)/shard_map/ppermute | solution.py:164
  62.3 14.6 %collective-permute-start.12 = (bf16[512,256]{1,0:T(8,128)(2,1)S(1)}, bf16[512,256]{1,0:T(8,128)(2,1)S(1)}, u32[]{:S(2)}, u32[]{:S(2)}) collective-permute-start(bf16[512,256]{1,0:T(8,128)(2,1)S(1)} %get-tuple-element.12.w0), channel_id=1, source_target_pairs={{128,0},{192,64},{0,128},{64,192},{129,1},{193,65},{1,129},{65,193... | collective-permute-start | bytes 786440 | tf_op jit(solution)/shard_map/ppermute | solution.py:164
  65.2 17.3 %collective-permute-start.15 = (bf16[512,256]{1,0:T(8,128)(2,1)S(1)}, bf16[512,256]{1,0:T(8,128)(2,1)S(1)}, u32[]{:S(2)}, u32[]{:S(2)}) collective-permute-start(bf16[512,256]{1,0:T(8,128)(2,1)S(1)} %get-tuple-element.11.refs_0_), channel_id=1, source_target_pairs={{64,0},{128,64},{192,128},{0,192},{65,1},{129,65},{193,129},{1,193... | collective-permute-start | bytes 786440 | tf_op jit(solution)/shard_map/ppermute | solution.py:164
  66.7 15.8 %collective-permute-start.16 = (bf16[512,256]{1,0:T(8,128)(2,1)S(1)}, bf16[512,256]{1,0:T(8,128)(2,1)S(1)}, u32[]{:S(2)}, u32[]{:S(2)}) collective-permute-start(bf16[512,256]{1,0:T(8,128)(2,1)S(1)} %get-tuple-element.11.refs_0_), channel_id=1, source_target_pairs={{128,0},{192,64},{0,128},{64,192},{129,1},{193,65},{1,129},{65,193... | collective-permute-start | bytes 786440 | tf_op jit(solution)/shard_map/ppermute | solution.py:164
  67.2 15.8 %collective-permute-start.17 = (bf16[512,256]{1,0:T(8,128)(2,1)S(1)}, bf16[512,256]{1,0:T(8,128)(2,1)S(1)}, u32[]{:S(2)}, u32[]{:S(2)}) collective-permute-start(bf16[512,256]{1,0:T(8,128)(2,1)S(1)} %get-tuple-element.11.refs_0_), channel_id=1, source_target_pairs={{192,0},{0,64},{64,128},{128,192},{193,1},{1,65},{65,129},{129,193... | collective-permute-start | bytes 786440 | tf_op jit(solution)/shard_map/ppermute | solution.py:164
  73.0 15.0 %collective-permute-start.13 = (bf16[512,256]{1,0:T(8,128)(2,1)S(1)}, bf16[512,256]{1,0:T(8,128)(2,1)S(1)}, u32[]{:S(2)}, u32[]{:S(2)}) collective-permute-start(bf16[512,256]{1,0:T(8,128)(2,1)S(1)} %get-tuple-element.12.w0), channel_id=1, source_target_pairs={{192,0},{0,64},{64,128},{128,192},{193,1},{1,65},{65,129},{129,193... | collective-permute-start | bytes 786440 | tf_op jit(solution)/shard_map/ppermute | solution.py:164
  76.9 31.8 %collective-permute-start.18 = (bf16[512,256]{1,0:T(8,128)(2,1)S(1)}, bf16[512,256]{1,0:T(8,128)(2,1)S(1)}, u32[]{:S(2)}, u32[]{:S(2)}) collective-permute-start(bf16[512,256]{1,0:T(8,128)(2,1)S(1)} %get-tuple-element.11.refs_0_), channel_id=1, source_target_pairs={{0,4},{4,0},{1,5},{5,1},{2,6},{6,2},{3,7},{7,3},{8,12},{12,8},{9,1... | collective-permute-start | bytes 786440 | tf_op jit(solution)/shard_map/ppermute | solution.py:169
  82.5 26.2 %collective-permute-start.19 = (bf16[512,256]{1,0:T(8,128)(2,1)S(1)}, bf16[512,256]{1,0:T(8,128)(2,1)}, u32[]{:S(2)}, u32[]{:S(2)}) collective-permute-start(bf16[512,256]{1,0:T(8,128)(2,1)S(1)} %collective-permute-done.15.refs_1_), channel_id=1, source_target_pairs={{0,4},{4,0},{1,5},{5,1},{2,6},{6,2},{3,7},{7,3},{8,12},{12,8},{9,1... | collective-permute-start | bytes 786440 | tf_op jit(solution)/shard_map/ppermute | solution.py:169
  82.5 26.2 %collective-permute-start.20 = (bf16[512,256]{1,0:T(8,128)(2,1)S(1)}, bf16[512,256]{1,0:T(8,128)(2,1)}, u32[]{:S(2)}, u32[]{:S(2)}) collective-permute-start(bf16[512,256]{1,0:T(8,128)(2,1)S(1)} %collective-permute-done.16.refs_2_), channel_id=1, source_target_pairs={{0,4},{4,0},{1,5},{5,1},{2,6},{6,2},{3,7},{7,3},{8,12},{12,8},{9,1... | collective-permute-start | bytes 786440 | tf_op jit(solution)/shard_map/ppermute | solution.py:169
  83.0 25.7 %collective-permute-start.21 = (bf16[512,256]{1,0:T(8,128)(2,1)S(1)}, bf16[512,256]{1,0:T(8,128)(2,1)}, u32[]{:S(2)}, u32[]{:S(2)}) collective-permute-start(bf16[512,256]{1,0:T(8,128)(2,1)S(1)} %collective-permute-done.17.refs_3_), channel_id=1, source_target_pairs={{0,4},{4,0},{1,5},{5,1},{2,6},{6,2},{3,7},{7,3},{8,12},{12,8},{9,1... | collective-permute-start | bytes 786440 | tf_op jit(solution)/shard_map/ppermute | solution.py:169
  88.0 2.7 %copy-start.3 = (f32[8]{0:T(128)S(1)}, f32[8]{0:T(128)}, u32[]{:S(2)}) copy-start(f32[8]{0:T(128)} %sinks.1) | copy-start | bytes 100
  90.7 0.9 copy-start.2
  108.6 1.4 %collective-permute-start.14 = (bf16[256,256]{1,0:T(8,128)(2,1)S(1)}, bf16[256,256]{1,0:T(8,128)(2,1)S(1)}, u32[]{:S(2)}, u32[]{:S(2)}) collective-permute-start(bf16[256,256]{1,0:T(8,128)(2,1)S(1)} %get-tuple-element.13), channel_id=1, source_target_pairs={{0,4},{4,0},{1,5},{5,1},{2,6},{6,2},{3,7},{7,3},{8,12},{12,8},{9,1... | collective-permute-start | bytes 393224 | tf_op jit(solution)/shard_map/ppermute | solution.py:169

commit v2 on v1

v2 whole, which is shorter than its diff:
```python
import functools

import jax
import jax.numpy as jnp
import numpy as np
from jax import lax
from jax.experimental import pallas as pl
from jax.experimental.pallas import tpu as pltpu
from jax.sharding import Mesh
from jax.sharding import PartitionSpec as P

HD = 64
SCORE_SCALE = 0.015625
EPSILON = 1e-05
LOG_THETA = 16.11809565095832
LOG2E = 1.4426950408889634
BF16 = jnp.bfloat16
F32 = jnp.float32
VMEM_LIMIT = 48 * 1024 * 1024
VMEM_ALL = 63_400_000

AWAY = (1, 7, 2, 6, 3, 5, 4)
NEAR = 4

NT = (((1,), (1,)), ((), ()))


def params(semantics=None, limit=VMEM_LIMIT):
    return pltpu.CompilerParams(vmem_limit_bytes=limit, dimension_semantics=semantics)


def vspec():
    return pl.BlockSpec(memory_space=pltpu.VMEM)


def sspec():
    return pl.BlockSpec(memory_space=pltpu.SMEM)


def half_turn(x):
    width = x.shape[1]
    lane = lax.broadcasted_iota(jnp.int32, x.shape, 1) % HD
    up = pltpu.roll(x, width - HD // 2, 1)
    down = pltpu.roll(x, HD // 2, 1)
    return jnp.where(lane < HD // 2, -up, down)


def rotary_tables(first, step, count):
    frequency = np.exp(-LOG_THETA * 2.0 * np.arange(HD // 2) / HD).astype(np.float32)

    def table(position):
        angles = position[:, None].astype(np.float64) * frequency[None, :].astype(np.float64)
        cos, sin = np.cos(angles), np.sin(angles)
        return np.concatenate([cos, cos, sin, sin], axis=1).astype(np.float32)

    return table(first + step * np.arange(count)), table(np.arange(step))


def split_kernel(ids, wq, wk, wv, wo, pk, pv, fan, p_keep, p_send):
    core = ids[3]

    def halves(*refs):
        low = [r[:, : r.shape[1] // 2] for r in refs]
        high = [r[:, r.shape[1] // 2 :] for r in refs]
        return jnp.concatenate(low, axis=1), jnp.concatenate(high, axis=1)

    for c, half in enumerate(halves(wk, wv, wq, wo)):
        for d in range(fan.shape[0] // 2):
            fan[2 * d + c] = half
    low, high = halves(pk, pv)

    @pl.when(core == 0)
    def _():
        p_keep[...] = low
        p_send[...] = high

    @pl.when(core != 0)
    def _():
        p_keep[...] = high
        p_send[...] = low


def rotary(x, coarse, fine):
    low = lax.broadcasted_iota(jnp.int32, fine.shape, 1) < HD
    low1 = low[:1]

    def pair(t, low):
        other = pltpu.roll(t, HD, 1)
        return jnp.where(low, t, other), jnp.where(low, other, t)

    cos_a, sin_a = pair(coarse, low1)
    cos_b, sin_b = pair(fine, low)
    cos = cos_a * cos_b - sin_a * sin_b
    sin = sin_a * cos_b + cos_a * sin_b
    return x * cos + half_turn(x) * sin


def norm_kernel(ids, *refs):
    hid, gain, normed = refs[0:8], refs[8], refs[9]
    mdl = ids[0]
    rows, cols = hid[0].shape
    count = 4
    for side in range(2):
        total = jnp.zeros((rows, 1), F32)
        for k in range(count):
            part = hid[side * count + k][...].astype(F32)
            total = total + jnp.sum(part * part, axis=1, keepdims=True)
        scale = lax.rsqrt(total / (cols * count) + EPSILON)
        for k in range(count):
            at = pl.multiple_of(lax.rem(mdl + k, count) * cols, cols)
            part = hid[side * count + k][...].astype(F32)
            part = part * scale * gain[:, pl.ds(at, cols)].astype(F32)
            normed[side * rows : (side + 1) * rows, pl.ds(at, cols)] = part.astype(BF16)


def kv_kernel(ids, normed, w0, w1, w2, w3, coarse, fine, p_keep, p_got, own_new, own_prefix, *sends):
    grp, zed, core = ids[1], ids[2], ids[3]
    depth = w0.shape[0]
    rows = p_keep.shape[0]
    acc = None
    for k, w in enumerate((w0, w1, w2, w3)):
        at = pl.multiple_of(lax.rem(grp + k, 4) * depth, depth)
        part = jnp.dot(normed[:, pl.ds(at, depth)], w[...], preferred_element_type=F32)
        acc = part if acc is None else acc + part
    lane = lax.broadcasted_iota(jnp.int32, (rows, 2 * HD), 1)
    turn = coarse[pl.ds(zed, 1), :]
    for side in range(2):
        cut = slice(side * rows, (side + 1) * rows)
        at = pl.multiple_of(lax.rem(side + core, 2) * rows, rows)
        x = acc[cut]
        x = jnp.where(lane < HD, rotary(x, turn, fine[pl.ds(at, rows), :]), x).astype(BF16)
        prefix = (p_keep, p_got)[side][...]
        own_new[cut, :] = x
        own_prefix[cut, :] = prefix
        for away, send in zip(AWAY, sends):
            @pl.when(zed >= away)
            def _(send=send, cut=cut, prefix=prefix):
                send[cut, :] = prefix

            @pl.when(zed < away)
            def _(send=send, cut=cut, x=x):
                send[cut, :] = x


def q_kernel(ids, normed, w0, w1, w2, w3, coarse, fine, q, w_o):
    grp, zed, core = ids[1], ids[2], ids[3]
    depth = w0.shape[0]
    rows = normed.shape[0] // 2
    lane = lax.broadcasted_iota(jnp.int32, (rows, 2 * HD), 1)
    turn = coarse[pl.ds(zed, 1), :]
    weights = (w0, w1, w2, w3)
    for k, w in enumerate(weights):
        w_o[k * depth : (k + 1) * depth, :] = w[:, 4 * HD :]
    for side in range(2):
        cut = slice(side * rows, (side + 1) * rows)
        at = pl.multiple_of(lax.rem(side + core, 2) * rows, rows)
        acc = None
        for k, w in enumerate(weights):
            cols = pl.ds(pl.multiple_of(lax.rem(grp + k, 4) * depth, depth), depth)
            part = jnp.dot(normed[cut, cols], w[:, : 4 * HD], preferred_element_type=F32)
            acc = part if acc is None else acc + part
        for pair in range(2):
            both = rotary(
                acc[:, pair * 2 * HD : (pair + 1) * 2 * HD], turn, fine[pl.ds(at, rows), :]
            )
            both = both.astype(BF16).astype(F32) * SCORE_SCALE
            q[2 * pair, cut, :] = jnp.where(lane < HD, both, 0.0).astype(BF16)
            q[2 * pair + 1, cut, :] = jnp.where(
                lane < HD, pltpu.roll(both, HD, 1), 0.0
            ).astype(BF16)


def ones_and_values(block):
    lane = lax.broadcasted_iota(jnp.int32, block.shape, 1)
    return jnp.where(lane < HD, 1.0, block[...].astype(F32)).astype(BF16)


def attend(scores, top, acc, vals):
    shift = top * LOG2E
    for s, v in zip(scores, vals):
        p = jnp.exp2(s * LOG2E - shift).astype(BF16)
        acc = acc + jnp.dot(p, v[...], preferred_element_type=F32)
    return acc


def first_kernel(ids, sinks, q, own_prefix, own_new, *refs):
    count = len(AWAY[:NEAR])
    blocks, (state, vals) = refs[:count], refs[count:]
    core = ids[3]
    half, pair = pl.program_id(0), pl.program_id(1)
    block, rows = own_new.shape[0], q.shape[1]

    @pl.when((half == 0) & (pair == 0))
    def _():
        for j, b in enumerate((own_prefix, own_new) + tuple(blocks)):
            vals[j] = ones_and_values(b)

    row = lax.broadcasted_iota(jnp.int32, (rows, block), 0) + half * rows
    col = lax.broadcasted_iota(jnp.int32, (rows, block), 1)
    swing = core * (block // 2)
    new_side = lax.rem(col + swing, block) <= lax.rem(row + swing, block)
    for i in range(2):
        queries = q[i]
        sink = sinks[core * 4 + pair * 2 + i]
        scores = [
            lax.dot_general(queries, b[...], NT, preferred_element_type=F32) for b in blocks
        ]
        before = lax.dot_general(queries, own_prefix[...], NT, preferred_element_type=F32)
        after = lax.dot_general(queries, own_new[...], NT, preferred_element_type=F32)
        diagonal = jnp.where(new_side, after, before)
        top = diagonal
        for s in scores:
            top = jnp.maximum(top, s)
        top = jnp.maximum(jnp.max(top, axis=1, keepdims=True), sink)
        shift = top * LOG2E
        p = jnp.exp2(diagonal * LOG2E - shift)
        acc = jnp.dot(
            jnp.where(new_side, 0.0, p).astype(BF16), vals[0], preferred_element_type=F32
        ) + jnp.dot(jnp.where(new_side, p, 0.0).astype(BF16), vals[1], preferred_element_type=F32)
        acc = attend(scores, top, acc, [vals.at[2 + j] for j in range(count)])
        lane = lax.broadcasted_iota(jnp.int32, acc.shape, 1)
        acc = jnp.where(lane < HD, acc + jnp.exp2(sink * LOG2E - shift), acc)
        state[i] = jnp.where(lane < 1, top, acc)


def update(queries, blocks, vals, acc):
    scores = [lax.dot_general(queries, b[...], NT, preferred_element_type=F32) for b in blocks]
    old = acc[:, :1]
    lane = lax.broadcasted_iota(jnp.int32, acc.shape, 1)
    acc = jnp.where(lane < 1, acc[:, 1:2], acc)
    top = scores[0]
    for s in scores[1:]:
        top = jnp.maximum(top, s)
    top = jnp.maximum(jnp.max(top, axis=1, keepdims=True), old)
    acc = acc * jnp.exp2((old - top) * LOG2E)
    return top, attend(scores, top, acc, vals)


def second_kernel(ids, q, state, *refs):
    count = len(AWAY[NEAR:])
    blocks, (out, vals) = refs[:count], refs[count:]
    zed, core, length = ids[2], ids[3], ids[4]
    half, pair = pl.program_id(0), pl.program_id(1)
    rows = q.shape[1]
    block = blocks[0].shape[0]

    @pl.when((half == 0) & (pair == 0))
    def _():
        for j, b in enumerate(blocks):
            vals[j] = ones_and_values(b)

    done = []
    for i in range(2):
        done.append(update(q[i], blocks, [vals.at[j] for j in range(count)], state[i])[1])
    one, two = done
    low = lax.broadcasted_iota(jnp.int32, one.shape, 1) < HD
    numer = jnp.where(low, pltpu.roll(one, HD, 1), two)
    denom = jnp.where(low, one, pltpu.roll(two, HD, 1))
    pos = lax.broadcasted_iota(jnp.int32, one.shape, 0) + half * rows
    pos = lax.rem(pos + core * (block // 2), block) + zed * block
    out[0] = jnp.where(pos < length, numer / denom, 0.0).astype(BF16)


def out_kernel(ids, keep, got, mine, theirs, *outs):
    mdl, grp = ids[0], ids[1]
    feats = outs[0].shape[1]
    for k in range(4):
        at = pl.ds(pl.multiple_of(lax.rem(mdl + k + 4 - grp, 4) * feats, feats), feats)
        part = lax.dot_general(keep[...], mine[at, :], NT, preferred_element_type=F32)
        part = part + lax.dot_general(got[...], theirs[at, :], NT, preferred_element_type=F32)
        outs[k][...] = part.astype(BF16)


def around(x, axis, size):
    got = {k: lax.ppermute(x, axis, [((i + k) % size, i) for i in range(size)]) for k in (1, 3, 2)}
    return [x, got[1], got[2], got[3]]


def swap(x):
    return lax.ppermute(x, "core", [(0, 1), (1, 0)])


def on_device(
    hidden_in,
    suffix_len,
    norm_gain,
    w_query,
    w_key,
    w_value,
    w_out,
    sink_logits,
    prefix_keys,
    prefix_values,
):
    grp, zed, core, mdl = (lax.axis_index(a) for a in ("grp", "z", "core", "mdl"))
    zsize = lax.axis_size("z")
    hidden = hidden_in[0]
    tok_rows, feats = hidden.shape
    chip_rows = 2 * tok_rows
    ids = jnp.stack([mdl, grp, zed, core, suffix_len[0]]).astype(jnp.int32)

    def shaped(*shape):
        return jax.ShapeDtypeStruct(shape, BF16)

    def call(body, name, outs, *args, scalars=1, limit=VMEM_LIMIT):
        whole = lambda x: pl.BlockSpec(x.shape, lambda i, n=len(x.shape): (0,) * n)
        traffic = sum(x.size * x.dtype.itemsize for x in (*args, *jax.tree.leaves(outs)))
        return pl.pallas_call(
            body,
            out_shape=outs,
            grid=(1,),
            in_specs=[sspec()] * scalars + [whole(x) for x in args[scalars:]],
            out_specs=jax.tree.map(whole, outs),
            compiler_params=params(("arbitrary",), limit),
            cost_estimate=pl.CostEstimate(
                flops=10**9, bytes_accessed=traffic, transcendentals=0
            ),
            name=name,
        )(*args)

    rows_in = w_query.shape[0]
    fan, p_keep, p_send = call(
        split_kernel,
        "split",
        (shaped(2 * zsize, rows_in, 10 * HD),) + (shaped(tok_rows, 2 * HD),) * 2,
        ids, w_query, w_key, w_value, w_out, prefix_keys[0], prefix_values[0],
        limit=VMEM_ALL,
    )
    hid = around(hidden, "mdl", 4)
    p_got = swap(p_send)

    depth = 2 * zsize * rows_in
    w_z = lax.all_to_all(fan, ("z", "core"), 0, 0, tiled=True).reshape(depth, 10 * HD)
    hid_other = [swap(h) for h in hid]
    w_z, *both = lax.optimization_barrier((w_z, *hid, *hid_other))
    hid, hid_other = both[:4], both[4:]
    w_kv = around(w_z[:, : 2 * HD], "grp", 4)
    rest, *w_kv = lax.optimization_barrier((w_z[:, 2 * HD :], *w_kv))
    w_qo = around(rest, "grp", 4)

    tables = rotary_tables(zsize * chip_rows, chip_rows, zsize)

    normed = call(
        norm_kernel,
        "norm",
        shaped(chip_rows, 4 * feats),
        ids, *hid, *hid_other, norm_gain.reshape(1, -1),
        limit=VMEM_ALL,
    )
    own_new, prefix, *sends = call(
        kv_kernel,
        "kv_proj",
        (shaped(chip_rows, 2 * HD),) * (2 + len(AWAY)),
        ids, normed, *w_kv, *tables, p_keep, p_got,
        limit=VMEM_ALL,
    )
    blocks = [
        lax.ppermute(x, "z", [(i, (i + zsize - k) % zsize) for i in range(zsize)])
        for k, x in zip(AWAY, sends)
    ]
    q, w_o = call(
        q_kernel,
        "q_proj",
        (shaped(4, chip_rows, 2 * HD), shaped(4 * depth, 4 * HD)),
        ids, normed, *w_qo, *tables,
    )
    w_theirs = swap(w_o)

    def work(count):
        pairs = count * 4 * chip_rows * chip_rows
        return pl.CostEstimate(flops=1024 * pairs, bytes_accessed=2**22, transcendentals=pairs)

    block_spec = pl.BlockSpec((chip_rows, 2 * HD), lambda i, j: (0, 0))
    heads_spec = pl.BlockSpec((2, tok_rows, 2 * HD), lambda i, j: (j, i, 0))
    state = pl.pallas_call(
        first_kernel,
        out_shape=jax.ShapeDtypeStruct((4, chip_rows, 2 * HD), F32),
        grid=(2, 2),
        in_specs=[sspec(), sspec(), heads_spec] + [block_spec] * (2 + NEAR),
        out_specs=heads_spec,
        scratch_shapes=[pltpu.VMEM((2 + NEAR, chip_rows, 2 * HD), BF16)],
        compiler_params=params(("arbitrary", "arbitrary")),
        cost_estimate=work(2 + NEAR),
        name="attention_near",
    )(ids, sink_logits, q, prefix, own_new, *blocks[:NEAR])
    mixed = pl.pallas_call(
        second_kernel,
        out_shape=jax.ShapeDtypeStruct((2, tok_rows, 4 * HD), BF16),
        grid=(2, 2),
        in_specs=[sspec()] + [heads_spec] * 2 + [block_spec] * (len(AWAY) - NEAR),
        out_specs=pl.BlockSpec((1, tok_rows, 2 * HD), lambda i, j: (i, 0, j)),
        scratch_shapes=[pltpu.VMEM((len(AWAY) - NEAR, chip_rows, 2 * HD), BF16)],
        compiler_params=params(("arbitrary", "arbitrary")),
        cost_estimate=work(len(AWAY) - NEAR),
        name="attention_far",
    )(ids, q, state, *blocks[NEAR:])

    got = swap(mixed[1])
    piece = jax.ShapeDtypeStruct((tok_rows, feats), BF16)
    parts = call(out_kernel, "out_proj", (piece,) * 4, ids, mixed[0], got, w_o, w_theirs)
    arrived = {
        k: lax.ppermute(parts[k], "mdl", [(i, (i + k) % 4) for i in range(4)]) for k in (2, 1, 3)
    }
    total = parts[0].astype(F32) + arrived[1].astype(F32)
    total = total + (arrived[2].astype(F32) + arrived[3].astype(F32))
    return total.astype(BF16)[None]


def solution(mesh):
    groups, toks, mdls = mesh.devices.shape
    cores = Mesh(
        mesh.devices.reshape(groups, toks // 2, 2, mdls), ("grp", "z", "core", "mdl")
    )
    tok = ("z", "core")
    placed = (
        P("grp", tok, "mdl"),
        P("grp"),
        P(),
        P(("grp",) + tok, "mdl"),
        P(("grp",) + tok, "mdl"),
        P(("grp",) + tok, "mdl"),
        P(("grp",) + tok, "mdl"),
        P("mdl"),
        P("grp", tok, "mdl"),
        P("grp", tok, "mdl"),
    )
    return jax.shard_map(
        on_device,
        mesh=cores,
        in_specs=placed,
        out_specs=P("grp", tok, "mdl"),
        check_vma=False,
    )
```

time: 133 us -> 124 us (0.932); the launches traced: 133 us -> 122 us
  blocking collectives: 20 us -> 0 us
  waiting for transfers between devices: 34.1 us -> 46.5 us
  Pallas kernels: 25.1 us -> 32.1 us
  local copies, waits for them, and re-layouts: 6.33 us -> 1.38 us
  starting transfers between devices: 43.5 us -> 39.9 us
  other arithmetic: 2.96 us -> 0.84 us
    all_to_all x1 -> x0, blocking collectives: 20 us -> none  [on_device(): parts = lax.all_to_all(partial_out, 'mdl', 0, 0)]
    ppermute x0 -> x10, starting transfers between devices: none -> 18.7 us  [the longest x7 16.5 us: on_device(): lax.ppermute(x, 'z', [(i, (i + zsize - k) % zsize) for i in range(zsize)])]
    ppermute x0 -> x10, waiting for transfers between devices: none -> 14.1 us  [the longest x3 14.1 us: on_device(): lax.ppermute(parts[k], 'mdl', [(i, (i + k) % 4) for i in range(4)])]
    all_to_all x3 -> x1, starting transfers between devices: 21.4 us -> 8.73 us  [on_device(): lax.all_to_all(fan, ('z', 'core'), 0, 0, tiled=True).reshape(depth, 10 * HD)]
    ppermute x12 -> x9, starting transfers between devices: 20.7 us -> 11.4 us  [around(): lax.ppermute(x, axis, [((i + k) % size, i) for i in range(size)])]
    pallas_call x4 -> x7, Pallas kernels: 25.1 us -> 32.1 us  [the longest x5 13.5 us: call(): pl.pallas_call(body, out_shape=outs, grid=(1,), in_specs=[sspec()] * scal...]
    all_to_all x3 -> x1, waiting for transfers between devices: 6.6 us -> 0.01 us  [on_device(): lax.all_to_all(fan, ('z', 'core'), 0, 0, tiled=True).reshape(depth, 10 * HD)]
    ppermute x12 -> x9, waiting for transfers between devices: 26.2 us -> 29.9 us  [around(): lax.ppermute(x, axis, [((i + k) % size, i) for i in range(size)])]
  transfers between devices with their start and end apart: 25 -> 27, of which waited for: 9 -> 12; matrix products, arithmetic and copies ran while one was open for 3% -> 1% of each run, Pallas kernels for 17% -> 24%
where the time goes in v2:
time: 124 us; the launch traced here: 122 us
  waiting for transfers between devices  46.5 us (38%)
  starting transfers between devices  39.9 us (32%)
  Pallas kernels  32.1 us (26%)
  local copies, waits for them, and re-layouts  1.38 us (1%)
    ppermute x9, waiting for transfers between devices, around(): lax.ppermute(x, axis, [((i + k) % size, i) for i in range(size)])  29.9 us
    ppermute x7, starting transfers between devices, on_device(): lax.ppermute(x, 'z', [(i, (i + zsize - k) % zsize) for i in range(zsize)])  16.5 us
    ppermute x3, waiting for transfers between devices, on_device(): lax.ppermute(parts[k], 'mdl', [(i, (i + k) % 4) for i in range(4)])  14.1 us
    pallas_call x5, Pallas kernels, call(): pl.pallas_call(body, out_shape=outs, grid=(1,), in_specs=[sspec()] * scal...  13.5 us
    ppermute x9, starting transfers between devices, around(): lax.ppermute(x, axis, [((i + k) % size, i) for i in range(size)])  11.4 us
    pallas_call x1, Pallas kernels, on_device(): pl.pallas_call(first_kernel, out_shape=jax.ShapeDtypeStruct((4, chip_rows...  10.7 us
    all_to_all x1, starting transfers between devices, on_device(): lax.all_to_all(fan, ('z', 'core'), 0, 0, tiled=True).reshape(depth, 10 * HD)  8.73 us
    pallas_call x1, Pallas kernels, on_device(): pl.pallas_call(second_kernel, out_shape=jax.ShapeDtypeStruct((2, tok_rows...  7.9 us
  transfers between devices with their start and end apart: 27, of which 12 were waited for; matrix products, arithmetic and copies ran while one was open for 1% of the time, Pallas kernels for 24%

profile of v2, /device:TPU:32, one launch (start us, length us, event | category | flops | bytes accessed | tf_op | source)
XLA Modules:
  0.0 121.7 jit_solution(17181972526525491715)
XLA Ops:
  0.7 0.6 stack.19.ids
  1.3 2.0 %split.1 = (bf16[16,32,640]{2,1,0:T(8,128)(2,1)}, bf16[256,128]{1,0:T(8,128)(2,1)}, bf16[256,128]{1,0:T(8,128)(2,1)}) custom-call(s32[5]{0:T(128)} %stack.19.ids, bf16[32,512]{1,0:T(8,128)(2,1)} %wq.1, bf16[32,128]{1,0:T(8,128)(2,1)} %wk.1, bf16[32,128]{1,0:T(8,128)(2,1)} %wv.1, bf16[32,512]{1,0:T(8,128)(2,1)} %wo.1, bf16[256,128]{1,0:T(8,128)(2,1)} %bitcast.21, ...), custom_call_target="tpu_custom_call" | custom-call | flops 1000000000 | bytes 999444 | tf_op jit(solution)/shard_map/split/pallas_call | solution.py:308
  3.3 8.7 %all-to-all-start = ((bf16[16,32,640]{2,1,0:T(8,128)(2,1)}), bf16[16,32,640]{2,1,0:T(8,128)(2,1)S(1)}, u32[]{:S(2)}, u32[]{:S(2)}) async-start(bf16[16,32,640]{2,1,0:T(8,128)(2,1)} %get-tuple-element.37), calls=%async_computation | async-start | bytes 1310720 | tf_op jit(solution)/shard_map/all_to_all | solution.py:333
  12.0 3.1 %collective-permute-start = (bf16[256,512]{1,0:T(8,128)(2,1)S(1)}, bf16[256,512]{1,0:T(8,128)(2,1)S(1)}, u32[]{:S(2)}, u32[]{:S(2)}) collective-permute-start(bf16[256,512]{1,0:T(8,128)(2,1)S(1)} %bitcast.17), channel_id=1, source_target_pairs={{1,0},{2,1},{3,2},{0,3},{5,4},{6,5},{7,6},{4,7},{9,8},{10,9},{11,1... | collective-permute-start | bytes 786440 | tf_op jit(solution)/shard_map/ppermute | solution.py:275
  15.1 0.6 collective-permute-start.1
  15.7 1.0 collective-permute-start.2
  16.7 0.0 collective-permute-start.3
  16.7 9.9 %collective-permute-done.refs_1_ = bf16[256,512]{1,0:T(8,128)(2,1)S(1)} collective-permute-done((bf16[256,512]{1,0:T(8,128)(2,1)S(1)}, bf16[256,512]{1,0:T(8,128)(2,1)S(1)}, u32[]{:S(2)}, u32[]{:S(2)}) %collective-permute-start) | collective-permute-done | bytes 262176 | tf_op jit(solution)/shard_map/ppermute | solution.py:275
  26.6 0.0 collective-permute-start.4
  26.6 0.0 collective-permute-done.1.refs_2_
  26.6 0.5 collective-permute-start.5
  27.1 3.2 %collective-permute-done.2.refs_3_ = bf16[256,512]{1,0:T(8,128)(2,1)S(1)} collective-permute-done((bf16[256,512]{1,0:T(8,128)(2,1)S(1)}, bf16[256,512]{1,0:T(8,128)(2,1)S(1)}, u32[]{:S(2)}, u32[]{:S(2)}) %collective-permute-start.2) | collective-permute-done | bytes 262176 | tf_op jit(solution)/shard_map/ppermute | solution.py:275
  30.3 0.0 collective-permute-start.6
  30.3 0.0 collective-permute-done.3.refs_4_
  30.3 0.0 collective-permute-done.4.refs_5_
  30.4 0.0 collective-permute-done.5.refs_6_
  30.4 1.5 %collective-permute-done.6.refs_7_ = bf16[256,512]{1,0:T(8,128)(2,1)S(1)} collective-permute-done((bf16[256,512]{1,0:T(8,128)(2,1)S(1)}, bf16[256,512]{1,0:T(8,128)(2,1)S(1)}, u32[]{:S(2)}, u32[]{:S(2)}) %collective-permute-start.6) | collective-permute-done | bytes 262176 | tf_op jit(solution)/shard_map/ppermute | solution.py:280
  31.9 0.0 all-to-all-done
  31.9 2.8 %collective-permute-start.7 = (bf16[512,128]{1,0:T(8,128)(2,1)S(1)}, bf16[512,128]{1,0:T(8,128)(2,1)S(1)}, u32[]{:S(2)}, u32[]{:S(2)}) collective-permute-start(bf16[512,128]{1,0:T(8,128)(2,1)S(1)} %slice.13.w0), channel_id=1, source_target_pairs={{64,0},{128,64},{192,128},{0,192},{65,1},{129,65},{193,129},{1,193... | collective-permute-start | bytes 393224 | tf_op jit(solution)/shard_map/ppermute | solution.py:275
  34.7 0.8 collective-permute-start.8
  35.5 0.9 collective-permute-start.9
  36.4 4.2 %collective-permute-done.7.w1 = bf16[512,128]{1,0:T(8,128)(2,1)S(1)} collective-permute-done((bf16[512,128]{1,0:T(8,128)(2,1)S(1)}, bf16[512,128]{1,0:T(8,128)(2,1)S(1)}, u32[]{:S(2)}, u32[]{:S(2)}) %collective-permute-start.7) | collective-permute-done | bytes 131104 | tf_op jit(solution)/shard_map/ppermute | solution.py:275
  40.6 2.0 %collective-permute-done.8.w2 = bf16[512,128]{1,0:T(8,128)(2,1)S(1)} collective-permute-done((bf16[512,128]{1,0:T(8,128)(2,1)S(1)}, bf16[512,128]{1,0:T(8,128)(2,1)S(1)}, u32[]{:S(2)}, u32[]{:S(2)}) %collective-permute-start.8) | collective-permute-done | bytes 131104 | tf_op jit(solution)/shard_map/ppermute | solution.py:275
  42.6 1.7 %collective-permute-done.9.w3 = bf16[512,128]{1,0:T(8,128)(2,1)S(1)} collective-permute-done((bf16[512,128]{1,0:T(8,128)(2,1)S(1)}, bf16[512,128]{1,0:T(8,128)(2,1)S(1)}, u32[]{:S(2)}, u32[]{:S(2)}) %collective-permute-start.9) | collective-permute-done | bytes 131104 | tf_op jit(solution)/shard_map/ppermute | solution.py:275
  44.3 0.6 collective-permute-start.10
  44.9 0.8 collective-permute-start.11
  45.7 0.9 collective-permute-start.12
  46.5 0.0 collective-permute-start.13
  46.5 0.6 reshape.7.refs_8_
  47.2 3.8 %norm.1.normed = bf16[512,2048]{1,0:T(8,128)(2,1)} custom-call(s32[5]{0:T(128)} %stack.19.ids, bf16[256,512]{1,0:T(8,128)(2,1)} %bitcast.16, bf16[256,512]{1,0:T(8,128)(2,1)} %copy-done.8, bf16[256,512]{1,0:T(8,128)(2,1)} %copy-done.9, bf16[256,512]{1,0:T(8,128)(2,1)} %copy-done.10, bf16[256,512]{1,0:T(8,128)(2,1)} %copy-done.11, ...), custom_call_target="tpu_custom_call" | custom-call | flops 1000000000 | bytes 4198420 | tf_op jit(solution)/shard_map/norm/pallas_call | solution.py:308
  51.0 0.0 copy-start.3
  51.0 0.0 collective-permute-done.13.p_got
  51.0 4.1 %kv_proj.1 = (bf16[512,128]{1,0:T(8,128)(2,1)}, bf16[512,128]{1,0:T(8,128)(2,1)}, bf16[512,128]{1,0:T(8,128)(2,1)}, bf16[512,128]{1,0:T(8,128)(2,1)}, bf16[512,1...) custom-call(s32[5]{0:T(128)} %stack.19.ids, ...), custom_call_target="tpu_custom_call" | custom-call | flops 1000000000 | bytes 4198420 | tf_op jit(solution)/shard_map/kv_proj/pallas_call | solution.py:308
  55.1 0.7 collective-permute-start.14
  55.8 1.5 %collective-permute-start.15 = (bf16[512,128]{1,0:T(8,128)(2,1)}, bf16[512,128]{1,0:T(8,128)(2,1)S(1)}, u32[]{:S(2)}, u32[]{:S(2)}) collective-permute-start(bf16[512,128]{1,0:T(8,128)(2,1)} %get-tuple-element.58), channel_id=1, source_target_pairs={{0,8},{8,16},{16,24},{24,32},{32,40},{40,48},{48,56},{56,0},{1,9},... | collective-permute-start | bytes 393224 | tf_op jit(solution)/shard_map/ppermute | solution.py:358
  57.3 1.8 %collective-permute-done.10.w1 = bf16[512,512]{1,0:T(8,128)(2,1)S(1)} collective-permute-done((bf16[512,512]{1,0:T(8,128)(2,1)S(1)}, bf16[512,512]{1,0:T(8,128)(2,1)S(1)}, u32[]{:S(2)}, u32[]{:S(2)}) %collective-permute-start.10) | collective-permute-done | bytes 524320 | tf_op jit(solution)/shard_map/ppermute | solution.py:275
  59.1 2.7 %collective-permute-start.16 = (bf16[512,128]{1,0:T(8,128)(2,1)}, bf16[512,128]{1,0:T(8,128)(2,1)S(1)}, u32[]{:S(2)}, u32[]{:S(2)}) collective-permute-start(bf16[512,128]{1,0:T(8,128)(2,1)} %get-tuple-element.59), channel_id=1, source_target_pairs={{0,48},{8,56},{16,0},{24,8},{32,16},{40,24},{48,32},{56,40},{1,49}... | collective-permute-start | bytes 393224 | tf_op jit(solution)/shard_map/ppermute | solution.py:358
  61.8 0.0 collective-permute-done.11.w2
  61.8 2.0 %collective-permute-start.17 = (bf16[512,128]{1,0:T(8,128)(2,1)}, bf16[512,128]{1,0:T(8,128)(2,1)S(1)}, u32[]{:S(2)}, u32[]{:S(2)}) collective-permute-start(bf16[512,128]{1,0:T(8,128)(2,1)} %get-tuple-element.60), channel_id=1, source_target_pairs={{0,16},{8,24},{16,32},{24,40},{32,48},{40,56},{48,0},{56,8},{1,17}... | collective-permute-start | bytes 393224 | tf_op jit(solution)/shard_map/ppermute | solution.py:358
  63.7 7.3 %collective-permute-done.12.w3 = bf16[512,512]{1,0:T(8,128)(2,1)} collective-permute-done((bf16[512,512]{1,0:T(8,128)(2,1)S(1)}, bf16[512,512]{1,0:T(8,128)(2,1)}, u32[]{:S(2)}, u32[]{:S(2)}) %collective-permute-start.12) | collective-permute-done | bytes 524320 | tf_op jit(solution)/shard_map/ppermute | solution.py:275
  71.0 3.7 %collective-permute-start.18 = (bf16[512,128]{1,0:T(8,128)(2,1)}, bf16[512,128]{1,0:T(8,128)(2,1)S(1)}, u32[]{:S(2)}, u32[]{:S(2)}) collective-permute-start(bf16[512,128]{1,0:T(8,128)(2,1)} %get-tuple-element.61), channel_id=1, source_target_pairs={{0,40},{8,48},{16,56},{24,0},{32,8},{40,16},{48,24},{56,32},{1,41}... | collective-permute-start | bytes 393224 | tf_op jit(solution)/shard_map/ppermute | solution.py:358
  74.7 2.4 %q_proj.1 = (bf16[4,512,128]{2,1,0:T(8,128)(2,1)S(1)}, bf16[2048,256]{1,0:T(8,128)(2,1)S(1)}) custom-call(s32[5]{0:T(128)S(1)} %copy-done.2, bf16[512,2048]{1,0:T(8,128)(2,1)S(1)} %copy-done, bf16[512,512]{1,0:T(8,128)(2,1)S(1)} %slice.12.w0, bf16[512,512]{1,0:T(8,128)(2,1)S(1)} %collective-permute-done.10.w1, bf16[512,512]{1,0:T(8,128)(2,1)} %collective-permute-done.11.w2, ...), custom_call_target="tpu_custom_call" | custom-call | flops 1000000000 | bytes 6033428 | tf_op jit(solution)/shard_map/q_proj/pallas_call | solution.py:308
  77.0 0.0 collective-permute-done.14.refs_0_
  77.1 1.5 %collective-permute-start.19 = (bf16[512,128]{1,0:T(8,128)(2,1)S(1)}, bf16[512,128]{1,0:T(8,128)(2,1)S(1)}, u32[]{:S(2)}, u32[]{:S(2)}) collective-permute-start(bf16[512,128]{1,0:T(8,128)(2,1)S(1)} %copy-done.18), channel_id=1, source_target_pairs={{0,24},{8,32},{16,40},{24,48},{32,56},{40,0},{48,8},{56,16},{1,25}... | collective-permute-start | bytes 393224 | tf_op jit(solution)/shard_map/ppermute | solution.py:358
  78.6 0.0 collective-permute-done.15.refs_1_
  78.6 4.5 %collective-permute-start.20 = (bf16[512,128]{1,0:T(8,128)(2,1)S(1)}, bf16[512,128]{1,0:T(8,128)(2,1)S(1)}, u32[]{:S(2)}, u32[]{:S(2)}) collective-permute-start(bf16[512,128]{1,0:T(8,128)(2,1)S(1)} %copy-done.17), channel_id=1, source_target_pairs={{0,32},{8,40},{16,48},{24,56},{32,0},{40,8},{48,16},{56,24},{1,33}... | collective-permute-start | bytes 393224 | tf_op jit(solution)/shard_map/ppermute | solution.py:358
  83.1 0.0 collective-permute-done.16.refs_2_
  83.1 0.0 collective-permute-start.22
  83.1 0.0 collective-permute-done.17.refs_3_
  83.1 10.7 %attention_near.1.state = f32[4,512,128]{2,1,0:T(8,128)S(1)} custom-call(s32[5]{0:T(128)S(1)} %copy-done.2, f32[8]{0:T(128)S(1)} %copy-done.4, bf16[4,512,128]{2,1,0:T(8,128)(2,1)S(1)} %get-tuple-element.48.q, bf16[512,128]{1,0:T(8,128)(2,1)S(1)} %copy-done.6, bf16[512,128]{1,0:T(8,128)(2,1)S(1)} %copy-done.5, ...), custom_call_target="tpu_custom_call" | custom-call | flops 6442450944 | bytes 4194304 | tf_op jit(solution)/shard_map/attention_near/pallas_call | solution.py:375
  93.8 0.0 collective-permute-done.18.refs_0_
  93.8 0.0 collective-permute-done.20.refs_2_
  93.8 7.9 %attention_far.1 = bf16[2,256,256]{2,1,0:T(8,128)(2,1)S(1)} custom-call(s32[5]{0:T(128)S(1)} %copy-done.2, bf16[4,512,128]{2,1,0:T(8,128)(2,1)S(1)} %get-tuple-element.48.q, f32[4,512,128]{2,1,0:T(8,128)S(1)} %attention_near.1.state, bf16[512,128]{1,0:T(8,128)(2,1)S(1)} %collective-permute-done.18.refs_0_, ...), custom_call_target="tpu_custom_call" | custom-call | flops 3221225472 | bytes 4194304 | tf_op jit(solution)/shard_map/attention_far/pallas_call | solution.py:386
  101.7 0.6 collective-permute-start.21
  102.3 1.0 collective-permute-done.21.got
  103.3 0.0 collective-permute-done.22.theirs
  103.3 1.3 %out_proj.1 = (bf16[256,512]{1,0:T(8,128)(2,1)S(1)}, bf16[256,512]{1,0:T(8,128)(2,1)S(1)}, bf16[256,512]{1,0:T(8,128)(2,1)S(1)}, bf16[256,512]{1,0:T(8,128)(2,1)S(1)}) custom-call(s32[5]{0:T(128)S(1)} %copy-done.2, bf16[256,256]{1,0:T(8,128)(2,1)S(1)} %get-tuple-element.70.keep, bf16[256,256]{1,0:T(8,128)(2,1)S(1)} %collective-permute-done.21.got, ...), custom_call_target="tpu_custom_call" | custom-call | flops 1000000000 | bytes 3407892 | tf_op jit(solution)/shard_map/out_proj/pallas_call | solution.py:308
  104.6 0.8 collective-permute-start.25
  105.4 0.5 collective-permute-start.24
  105.9 0.8 collective-permute-start.23
  106.8 7.1 %collective-permute-done.25 = bf16[256,512]{1,0:T(8,128)(2,1)S(1)} collective-permute-done((bf16[256,512]{1,0:T(8,128)(2,1)S(1)}, bf16[256,512]{1,0:T(8,128)(2,1)S(1)}, u32[]{:S(2)}, u32[]{:S(2)}) %collective-permute-start.25) | collective-permute-done | bytes 262176 | tf_op jit(solution)/shard_map/ppermute | solution.py:402
  113.8 2.3 %collective-permute-done.24 = bf16[256,512]{1,0:T(8,128)(2,1)S(1)} collective-permute-done((bf16[256,512]{1,0:T(8,128)(2,1)S(1)}, bf16[256,512]{1,0:T(8,128)(2,1)S(1)}, u32[]{:S(2)}, u32[]{:S(2)}) %collective-permute-start.24) | collective-permute-done | bytes 262176 | tf_op jit(solution)/shard_map/ppermute | solution.py:402
  116.2 4.7 %collective-permute-done.23 = bf16[256,512]{1,0:T(8,128)(2,1)S(1)} collective-permute-done((bf16[256,512]{1,0:T(8,128)(2,1)S(1)}, bf16[256,512]{1,0:T(8,128)(2,1)S(1)}, u32[]{:S(2)}, u32[]{:S(2)}) %collective-permute-start.23) | collective-permute-done | bytes 262176 | tf_op jit(solution)/shard_map/ppermute | solution.py:402
  120.9 0.8 fusion
  (49 shorter events, 0.2 us)
Async XLA Ops:
  1.3 10.7 %copy-start.7 = (bf16[1,256,512]{2,1,0:T(8,128)(2,1)S(1)}, bf16[1,256,512]{2,1,0:T(8,128)(2,1)}, u32[]{:S(2)}) copy-start(bf16[1,256,512]{2,1,0:T(8,128)(2,1)} %param.12) | copy-start | bytes 786436
  3.3 43.2 %copy-start.22 = (bf16[256,128]{1,0:T(8,128)(2,1)S(1)}, bf16[256,128]{1,0:T(8,128)(2,1)}, u32[]{:S(2)}) copy-start(bf16[256,128]{1,0:T(8,128)(2,1)} %get-tuple-element.54) | copy-start | bytes 196612
  3.3 43.2 %copy-start.16 = (bf16[2048]{0:T(1024)(128)(2,1)S(1)}, bf16[2048]{0:T(1024)(128)(2,1)}, u32[]{:S(2)}) copy-start(bf16[2048]{0:T(1024)(128)(2,1)} %param.14) | copy-start | bytes 12292
  3.3 28.6 %all-to-all-start = ((bf16[16,32,640]{2,1,0:T(8,128)(2,1)}), bf16[16,32,640]{2,1,0:T(8,128)(2,1)S(1)}, u32[]{:S(2)}, u32[]{:S(2)}) async-start(bf16[16,32,640]{2,1,0:T(8,128)(2,1)} %get-tuple-element.37), calls=%async_computation | async-start | bytes 1310720 | tf_op jit(solution)/shard_map/all_to_all | solution.py:333
  12.0 14.6 %collective-permute-start = (bf16[256,512]{1,0:T(8,128)(2,1)S(1)}, bf16[256,512]{1,0:T(8,128)(2,1)S(1)}, u32[]{:S(2)}, u32[]{:S(2)}) collective-permute-start(bf16[256,512]{1,0:T(8,128)(2,1)S(1)} %bitcast.17), channel_id=1, source_target_pairs={{1,0},{2,1},{3,2},{0,3},{5,4},{6,5},{7,6},{4,7},{9,8},{10,9},{11,1... | collective-permute-start | bytes 786440 | tf_op jit(solution)/shard_map/ppermute | solution.py:275
  15.1 11.5 %collective-permute-start.1 = (bf16[256,512]{1,0:T(8,128)(2,1)S(1)}, bf16[256,512]{1,0:T(8,128)(2,1)S(1)}, u32[]{:S(2)}, u32[]{:S(2)}) collective-permute-start(bf16[256,512]{1,0:T(8,128)(2,1)S(1)} %bitcast.18), channel_id=1, source_target_pairs={{2,0},{3,1},{0,2},{1,3},{6,4},{7,5},{4,6},{5,7},{10,8},{11,9},{8,1... | collective-permute-start | bytes 786440 | tf_op jit(solution)/shard_map/ppermute | solution.py:275
  15.7 14.6 %collective-permute-start.2 = (bf16[256,512]{1,0:T(8,128)(2,1)S(1)}, bf16[256,512]{1,0:T(8,128)(2,1)S(1)}, u32[]{:S(2)}, u32[]{:S(2)}) collective-permute-start(bf16[256,512]{1,0:T(8,128)(2,1)S(1)} %bitcast.19), channel_id=1, source_target_pairs={{3,0},{0,1},{1,2},{2,3},{7,4},{4,5},{5,6},{6,7},{11,8},{8,9},{9,10... | collective-permute-start | bytes 786440 | tf_op jit(solution)/shard_map/ppermute | solution.py:275
  16.7 13.6 %collective-permute-start.3 = (bf16[256,512]{1,0:T(8,128)(2,1)S(1)}, bf16[256,512]{1,0:T(8,128)(2,1)S(1)}, u32[]{:S(2)}, u32[]{:S(2)}) collective-permute-start(bf16[256,512]{1,0:T(8,128)(2,1)S(1)} %bitcast.20), channel_id=1, source_target_pairs={{0,4},{4,0},{1,5},{5,1},{2,6},{6,2},{3,7},{7,3},{8,12},{12,8},{9,1... | collective-permute-start | bytes 786440 | tf_op jit(solution)/shard_map/ppermute | solution.py:280
  26.6 20.5 %copy-start.8 = (bf16[256,512]{1,0:T(8,128)(2,1)}, bf16[256,512]{1,0:T(8,128)(2,1)S(1)}, u32[]{:S(2)}) copy-start(bf16[256,512]{1,0:T(8,128)(2,1)S(1)} %collective-permute-done.refs_1_) | copy-start | bytes 786436
  26.6 3.7 %collective-permute-start.4 = (bf16[256,512]{1,0:T(8,128)(2,1)S(1)}, bf16[256,512]{1,0:T(8,128)(2,1)S(1)}, u32[]{:S(2)}, u32[]{:S(2)}) collective-permute-start(bf16[256,512]{1,0:T(8,128)(2,1)S(1)} %collective-permute-done.refs_1_), channel_id=1, source_target_pairs={{0,4},{4,0},{1,5},{5,1},{2,6},{6,2},{3,7},{7,3},{8,12},{12,8},{9,1... | collective-permute-start | bytes 786440 | tf_op jit(solution)/shard_map/ppermute | solution.py:280
  26.6 20.5 %copy-start.9 = (bf16[256,512]{1,0:T(8,128)(2,1)}, bf16[256,512]{1,0:T(8,128)(2,1)S(1)}, u32[]{:S(2)}) copy-start(bf16[256,512]{1,0:T(8,128)(2,1)S(1)} %collective-permute-done.1.refs_2_) | copy-start | bytes 786436
  26.6 3.7 %collective-permute-start.5 = (bf16[256,512]{1,0:T(8,128)(2,1)S(1)}, bf16[256,512]{1,0:T(8,128)(2,1)S(1)}, u32[]{:S(2)}, u32[]{:S(2)}) collective-permute-start(bf16[256,512]{1,0:T(8,128)(2,1)S(1)} %collective-permute-done.1.refs_2_), channel_id=1, source_target_pairs={{0,4},{4,0},{1,5},{5,1},{2,6},{6,2},{3,7},{7,3},{8,12},{12,8},{9,1... | collective-permute-start | bytes 786440 | tf_op jit(solution)/shard_map/ppermute | solution.py:280
  30.3 16.8 %copy-start.10 = (bf16[256,512]{1,0:T(8,128)(2,1)}, bf16[256,512]{1,0:T(8,128)(2,1)S(1)}, u32[]{:S(2)}) copy-start(bf16[256,512]{1,0:T(8,128)(2,1)S(1)} %collective-permute-done.2.refs_3_) | copy-start | bytes 786436
  30.3 1.5 %collective-permute-start.6 = (bf16[256,512]{1,0:T(8,128)(2,1)S(1)}, bf16[256,512]{1,0:T(8,128)(2,1)S(1)}, u32[]{:S(2)}, u32[]{:S(2)}) collective-permute-start(bf16[256,512]{1,0:T(8,128)(2,1)S(1)} %collective-permute-done.2.refs_3_), channel_id=1, source_target_pairs={{0,4},{4,0},{1,5},{5,1},{2,6},{6,2},{3,7},{7,3},{8,12},{12,8},{9,1... | collective-permute-start | bytes 786440 | tf_op jit(solution)/shard_map/ppermute | solution.py:280
  30.3 16.8 %copy-start.11 = (bf16[256,512]{1,0:T(8,128)(2,1)}, bf16[256,512]{1,0:T(8,128)(2,1)S(1)}, u32[]{:S(2)}) copy-start(bf16[256,512]{1,0:T(8,128)(2,1)S(1)} %collective-permute-done.3.refs_4_) | copy-start | bytes 786436
  30.3 16.8 %copy-start.12 = (bf16[256,512]{1,0:T(8,128)(2,1)}, bf16[256,512]{1,0:T(8,128)(2,1)S(1)}, u32[]{:S(2)}) copy-start(bf16[256,512]{1,0:T(8,128)(2,1)S(1)} %collective-permute-done.4.refs_5_) | copy-start | bytes 786436
  30.4 16.8 %copy-start.13 = (bf16[256,512]{1,0:T(8,128)(2,1)}, bf16[256,512]{1,0:T(8,128)(2,1)S(1)}, u32[]{:S(2)}) copy-start(bf16[256,512]{1,0:T(8,128)(2,1)S(1)} %collective-permute-done.5.refs_6_) | copy-start | bytes 786436
  31.9 15.3 %copy-start.14 = (bf16[256,512]{1,0:T(8,128)(2,1)}, bf16[256,512]{1,0:T(8,128)(2,1)S(1)}, u32[]{:S(2)}) copy-start(bf16[256,512]{1,0:T(8,128)(2,1)S(1)} %collective-permute-done.6.refs_7_) | copy-start | bytes 786436
  31.9 19.1 %copy-start.15 = (bf16[512,128]{1,0:T(8,128)(2,1)}, bf16[512,128]{1,0:T(8,128)(2,1)S(1)}, u32[]{:S(2)}) copy-start(bf16[512,128]{1,0:T(8,128)(2,1)S(1)} %slice.13.w0) | copy-start | bytes 393220
  31.9 8.7 %collective-permute-start.7 = (bf16[512,128]{1,0:T(8,128)(2,1)S(1)}, bf16[512,128]{1,0:T(8,128)(2,1)S(1)}, u32[]{:S(2)}, u32[]{:S(2)}) collective-permute-start(bf16[512,128]{1,0:T(8,128)(2,1)S(1)} %slice.13.w0), channel_id=1, source_target_pairs={{64,0},{128,64},{192,128},{0,192},{65,1},{129,65},{193,129},{1,193... | collective-permute-start | bytes 393224 | tf_op jit(solution)/shard_map/ppermute | solution.py:275
  34.7 7.9 %collective-permute-start.8 = (bf16[512,128]{1,0:T(8,128)(2,1)S(1)}, bf16[512,128]{1,0:T(8,128)(2,1)S(1)}, u32[]{:S(2)}, u32[]{:S(2)}) collective-permute-start(bf16[512,128]{1,0:T(8,128)(2,1)S(1)} %slice.13.w0), channel_id=1, source_target_pairs={{128,0},{192,64},{0,128},{64,192},{129,1},{193,65},{1,129},{65,193... | collective-permute-start | bytes 393224 | tf_op jit(solution)/shard_map/ppermute | solution.py:275
  35.5 8.8 %collective-permute-start.9 = (bf16[512,128]{1,0:T(8,128)(2,1)S(1)}, bf16[512,128]{1,0:T(8,128)(2,1)S(1)}, u32[]{:S(2)}, u32[]{:S(2)}) collective-permute-start(bf16[512,128]{1,0:T(8,128)(2,1)S(1)} %slice.13.w0), channel_id=1, source_target_pairs={{192,0},{0,64},{64,128},{128,192},{193,1},{1,65},{65,129},{129,193... | collective-permute-start | bytes 393224 | tf_op jit(solution)/shard_map/ppermute | solution.py:275
  40.6 6.6 %copy-start.19 = (bf16[512,128]{1,0:T(8,128)(2,1)}, bf16[512,128]{1,0:T(8,128)(2,1)S(1)}, u32[]{:S(2)}) copy-start(bf16[512,128]{1,0:T(8,128)(2,1)S(1)} %collective-permute-done.7.w1) | copy-start | bytes 393220
  42.6 4.6 %copy-start.20 = (bf16[512,128]{1,0:T(8,128)(2,1)}, bf16[512,128]{1,0:T(8,128)(2,1)S(1)}, u32[]{:S(2)}) copy-start(bf16[512,128]{1,0:T(8,128)(2,1)S(1)} %collective-permute-done.8.w2) | copy-start | bytes 393220
  44.3 2.9 %copy-start.21 = (bf16[512,128]{1,0:T(8,128)(2,1)}, bf16[512,128]{1,0:T(8,128)(2,1)S(1)}, u32[]{:S(2)}) copy-start(bf16[512,128]{1,0:T(8,128)(2,1)S(1)} %collective-permute-done.9.w3) | copy-start | bytes 393220
  44.3 14.8 %collective-permute-start.10 = (bf16[512,512]{1,0:T(8,128)(2,1)S(1)}, bf16[512,512]{1,0:T(8,128)(2,1)S(1)}, u32[]{:S(2)}, u32[]{:S(2)}) collective-permute-start(bf16[512,512]{1,0:T(8,128)(2,1)S(1)} %slice.12.w0), channel_id=1, source_target_pairs={{64,0},{128,64},{192,128},{0,192},{65,1},{129,65},{193,129},{1,193... | collective-permute-start | bytes 1572872 | tf_op jit(solution)/shard_map/ppermute | solution.py:275
  44.9 16.9 %collective-permute-start.11 = (bf16[512,512]{1,0:T(8,128)(2,1)S(1)}, bf16[512,512]{1,0:T(8,128)(2,1)}, u32[]{:S(2)}, u32[]{:S(2)}) collective-permute-start(bf16[512,512]{1,0:T(8,128)(2,1)S(1)} %slice.12.w0), channel_id=1, source_target_pairs={{128,0},{192,64},{0,128},{64,192},{129,1},{193,65},{1,129},{65,193... | collective-permute-start | bytes 1572872 | tf_op jit(solution)/shard_map/ppermute | solution.py:275
  45.7 25.3 %collective-permute-start.12 = (bf16[512,512]{1,0:T(8,128)(2,1)S(1)}, bf16[512,512]{1,0:T(8,128)(2,1)}, u32[]{:S(2)}, u32[]{:S(2)}) collective-permute-start(bf16[512,512]{1,0:T(8,128)(2,1)S(1)} %slice.12.w0), channel_id=1, source_target_pairs={{192,0},{0,64},{64,128},{128,192},{193,1},{1,65},{65,129},{129,193... | collective-permute-start | bytes 1572872 | tf_op jit(solution)/shard_map/ppermute | solution.py:275
  46.5 4.5 %collective-permute-start.13 = (bf16[256,128]{1,0:T(8,128)(2,1)S(1)}, bf16[256,128]{1,0:T(8,128)(2,1)}, u32[]{:S(2)}, u32[]{:S(2)}) collective-permute-start(bf16[256,128]{1,0:T(8,128)(2,1)S(1)} %copy-done.22), channel_id=1, source_target_pairs={{0,4},{4,0},{1,5},{5,1},{2,6},{6,2},{3,7},{7,3},{8,12},{12,8},{9,1... | collective-permute-start | bytes 196616 | tf_op jit(solution)/shard_map/ppermute | solution.py:280
  51.0 23.7 %copy-start = (bf16[512,2048]{1,0:T(8,128)(2,1)S(1)}, bf16[512,2048]{1,0:T(8,128)(2,1)}, u32[]{:S(2)}) copy-start(bf16[512,2048]{1,0:T(8,128)(2,1)} %norm.1.normed) | copy-start | bytes 6291460
  51.0 23.7 %copy-start.1 = (f32[512,128]{1,0:T(8,128)S(1)}, f32[512,128]{1,0:T(8,128)}, u32[]{:S(2)}) copy-start(f32[512,128]{1,0:T(8,128)} %constant.22.clone.fine) | copy-start | bytes 786436
  51.0 23.7 %copy-start.2 = (s32[5]{0:T(128)S(1)}, s32[5]{0:T(128)}, u32[]{:S(2)}) copy-start(s32[5]{0:T(128)} %stack.19.ids) | copy-start | bytes 64
  51.0 23.6 %copy-start.3 = (f32[8,128]{1,0:T(8,128)S(1)}, f32[8,128]{1,0:T(8,128)}, u32[]{:S(2)}) copy-start(f32[8,128]{1,0:T(8,128)} %constant.21.clone.coarse) | copy-start | bytes 12292
  55.1 21.9 %collective-permute-start.14 = (bf16[512,128]{1,0:T(8,128)(2,1)}, bf16[512,128]{1,0:T(8,128)(2,1)S(1)}, u32[]{:S(2)}, u32[]{:S(2)}) collective-permute-start(bf16[512,128]{1,0:T(8,128)(2,1)} %get-tuple-element.57), channel_id=1, source_target_pairs={{0,56},{8,0},{16,8},{24,16},{32,24},{40,32},{48,40},{56,48},{1,57}... | collective-permute-start | bytes 393224 | tf_op jit(solution)/shard_map/ppermute | solution.py:358
  55.8 22.7 %collective-permute-start.15 = (bf16[512,128]{1,0:T(8,128)(2,1)}, bf16[512,128]{1,0:T(8,128)(2,1)S(1)}, u32[]{:S(2)}, u32[]{:S(2)}) collective-permute-start(bf16[512,128]{1,0:T(8,128)(2,1)} %get-tuple-element.58), channel_id=1, source_target_pairs={{0,8},{8,16},{16,24},{24,32},{32,40},{40,48},{48,56},{56,0},{1,9},... | collective-permute-start | bytes 393224 | tf_op jit(solution)/shard_map/ppermute | solution.py:358
  59.1 24.0 %collective-permute-start.16 = (bf16[512,128]{1,0:T(8,128)(2,1)}, bf16[512,128]{1,0:T(8,128)(2,1)S(1)}, u32[]{:S(2)}, u32[]{:S(2)}) collective-permute-start(bf16[512,128]{1,0:T(8,128)(2,1)} %get-tuple-element.59), channel_id=1, source_target_pairs={{0,48},{8,56},{16,0},{24,8},{32,16},{40,24},{48,32},{56,40},{1,49}... | collective-permute-start | bytes 393224 | tf_op jit(solution)/shard_map/ppermute | solution.py:358
  61.8 21.3 %collective-permute-start.17 = (bf16[512,128]{1,0:T(8,128)(2,1)}, bf16[512,128]{1,0:T(8,128)(2,1)S(1)}, u32[]{:S(2)}, u32[]{:S(2)}) collective-permute-start(bf16[512,128]{1,0:T(8,128)(2,1)} %get-tuple-element.60), channel_id=1, source_target_pairs={{0,16},{8,24},{16,32},{24,40},{32,48},{40,56},{48,0},{56,8},{1,17}... | collective-permute-start | bytes 393224 | tf_op jit(solution)/shard_map/ppermute | solution.py:358
  71.0 6.1 %copy-start.18 = (bf16[512,128]{1,0:T(8,128)(2,1)S(1)}, bf16[512,128]{1,0:T(8,128)(2,1)}, u32[]{:S(2)}) copy-start(bf16[512,128]{1,0:T(8,128)(2,1)} %get-tuple-element.62) | copy-start | bytes 393220
  71.0 7.6 %copy-start.17 = (bf16[512,128]{1,0:T(8,128)(2,1)S(1)}, bf16[512,128]{1,0:T(8,128)(2,1)}, u32[]{:S(2)}) copy-start(bf16[512,128]{1,0:T(8,128)(2,1)} %get-tuple-element.63) | copy-start | bytes 393220
  71.0 12.1 %copy-start.4 = (f32[8]{0:T(128)S(1)}, f32[8]{0:T(128)}, u32[]{:S(2)}) copy-start(f32[8]{0:T(128)} %sinks.1) | copy-start | bytes 100
  71.0 12.1 %copy-start.5 = (bf16[512,128]{1,0:T(8,128)(2,1)S(1)}, bf16[512,128]{1,0:T(8,128)(2,1)}, u32[]{:S(2)}) copy-start(bf16[512,128]{1,0:T(8,128)(2,1)} %get-tuple-element.56.own_new) | copy-start | bytes 393220
  71.0 12.1 %copy-start.6 = (bf16[512,128]{1,0:T(8,128)(2,1)S(1)}, bf16[512,128]{1,0:T(8,128)(2,1)}, u32[]{:S(2)}) copy-start(bf16[512,128]{1,0:T(8,128)(2,1)} %get-tuple-element.55.own_prefix) | copy-start | bytes 393220
  71.0 22.8 %collective-permute-start.18 = (bf16[512,128]{1,0:T(8,128)(2,1)}, bf16[512,128]{1,0:T(8,128)(2,1)S(1)}, u32[]{:S(2)}, u32[]{:S(2)}) collective-permute-start(bf16[512,128]{1,0:T(8,128)(2,1)} %get-tuple-element.61), channel_id=1, source_target_pairs={{0,40},{8,48},{16,56},{24,0},{32,8},{40,16},{48,24},{56,32},{1,41}... | collective-permute-start | bytes 393224 | tf_op jit(solution)/shard_map/ppermute | solution.py:358
  77.1 16.7 %collective-permute-start.19 = (bf16[512,128]{1,0:T(8,128)(2,1)S(1)}, bf16[512,128]{1,0:T(8,128)(2,1)S(1)}, u32[]{:S(2)}, u32[]{:S(2)}) collective-permute-start(bf16[512,128]{1,0:T(8,128)(2,1)S(1)} %copy-done.18), channel_id=1, source_target_pairs={{0,24},{8,32},{16,40},{24,48},{32,56},{40,0},{48,8},{56,16},{1,25}... | collective-permute-start | bytes 393224 | tf_op jit(solution)/shard_map/ppermute | solution.py:358
  78.6 15.2 %collective-permute-start.20 = (bf16[512,128]{1,0:T(8,128)(2,1)S(1)}, bf16[512,128]{1,0:T(8,128)(2,1)S(1)}, u32[]{:S(2)}, u32[]{:S(2)}) collective-permute-start(bf16[512,128]{1,0:T(8,128)(2,1)S(1)} %copy-done.17), channel_id=1, source_target_pairs={{0,32},{8,40},{16,48},{24,56},{32,0},{40,8},{48,16},{56,24},{1,33}... | collective-permute-start | bytes 393224 | tf_op jit(solution)/shard_map/ppermute | solution.py:358
  83.1 20.2 %collective-permute-start.22 = (bf16[2048,256]{1,0:T(8,128)(2,1)S(1)}, bf16[2048,256]{1,0:T(8,128)(2,1)S(1)}, u32[]{:S(2)}, u32[]{:S(2)}) collective-permute-start(bf16[2048,256]{1,0:T(8,128)(2,1)S(1)} %get-tuple-element.64.mine), channel_id=1, source_target_pairs={{0,4},{4,0},{1,5},{5,1},{2,6},{6,2},{3,7},{7,3},{8,12},{12,8},{9,1... | collective-permute-start | bytes 3145736 | tf_op jit(solution)/shard_map/ppermute | solution.py:280
  101.7 1.6 %collective-permute-start.21 = (bf16[256,256]{1,0:T(8,128)(2,1)S(1)}, bf16[256,256]{1,0:T(8,128)(2,1)S(1)}, u32[]{:S(2)}, u32[]{:S(2)}) collective-permute-start(bf16[256,256]{1,0:T(8,128)(2,1)S(1)} %get-tuple-element.69), channel_id=1, source_target_pairs={{0,4},{4,0},{1,5},{5,1},{2,6},{6,2},{3,7},{7,3},{8,12},{12,8},{9,1... | collective-permute-start | bytes 393224 | tf_op jit(solution)/shard_map/ppermute | solution.py:280
  104.6 9.2 %collective-permute-start.25 = (bf16[256,512]{1,0:T(8,128)(2,1)S(1)}, bf16[256,512]{1,0:T(8,128)(2,1)S(1)}, u32[]{:S(2)}, u32[]{:S(2)}) collective-permute-start(bf16[256,512]{1,0:T(8,128)(2,1)S(1)} %get-tuple-element.68), channel_id=1, source_target_pairs={{0,3},{1,0},{2,1},{3,2},{4,7},{5,4},{6,5},{7,6},{8,11},{9,8},{10,9... | collective-permute-start | bytes 786440 | tf_op jit(solution)/shard_map/ppermute | solution.py:402
  105.4 10.7 %collective-permute-start.24 = (bf16[256,512]{1,0:T(8,128)(2,1)S(1)}, bf16[256,512]{1,0:T(8,128)(2,1)S(1)}, u32[]{:S(2)}, u32[]{:S(2)}) collective-permute-start(bf16[256,512]{1,0:T(8,128)(2,1)S(1)} %get-tuple-element.67), channel_id=1, source_target_pairs={{0,2},{1,3},{2,0},{3,1},{4,6},{5,7},{6,4},{7,5},{8,10},{9,11},{10,... | collective-permute-start | bytes 786440 | tf_op jit(solution)/shard_map/ppermute | solution.py:402
  105.9 14.9 %collective-permute-start.23 = (bf16[256,512]{1,0:T(8,128)(2,1)S(1)}, bf16[256,512]{1,0:T(8,128)(2,1)S(1)}, u32[]{:S(2)}, u32[]{:S(2)}) collective-permute-start(bf16[256,512]{1,0:T(8,128)(2,1)S(1)} %get-tuple-element.66), channel_id=1, source_target_pairs={{0,1},{1,2},{2,3},{3,0},{4,5},{5,6},{6,7},{7,4},{8,9},{9,10},{10,1... | collective-permute-start | bytes 786440 | tf_op jit(solution)/shard_map/ppermute | solution.py:402

commit v3 on v2

--- a/solution.py
+++ b/solution.py
@@ -142,22 +142,19 @@
                 send[cut, :] = x
 
 
-def q_kernel(ids, normed, w0, w1, w2, w3, coarse, fine, q, w_o):
+def q_kernel(ids, normed, w0, w1, w2, w3, coarse, fine, q):
     grp, zed, core = ids[1], ids[2], ids[3]
     depth = w0.shape[0]
     rows = normed.shape[0] // 2
     lane = lax.broadcasted_iota(jnp.int32, (rows, 2 * HD), 1)
     turn = coarse[pl.ds(zed, 1), :]
-    weights = (w0, w1, w2, w3)
-    for k, w in enumerate(weights):
-        w_o[k * depth : (k + 1) * depth, :] = w[:, 4 * HD :]
     for side in range(2):
         cut = slice(side * rows, (side + 1) * rows)
         at = pl.multiple_of(lax.rem(side + core, 2) * rows, rows)
         acc = None
-        for k, w in enumerate(weights):
+        for k, w in enumerate((w0, w1, w2, w3)):
             cols = pl.ds(pl.multiple_of(lax.rem(grp + k, 4) * depth, depth), depth)
-            part = jnp.dot(normed[cut, cols], w[:, : 4 * HD], preferred_element_type=F32)
+            part = jnp.dot(normed[cut, cols], w[...], preferred_element_type=F32)
             acc = part if acc is None else acc + part
         for pair in range(2):
             both = rotary(
@@ -261,14 +258,15 @@
     out[0] = jnp.where(pos < length, numer / denom, 0.0).astype(BF16)
 
 
-def out_kernel(ids, keep, got, mine, theirs, *outs):
+def out_kernel(ids, keep, got, *refs):
     mdl, grp = ids[0], ids[1]
-    feats = outs[0].shape[1]
+    mine, theirs, outs, held = refs[0:4], refs[4:8], refs[8:12], refs[12]
     for k in range(4):
-        at = pl.ds(pl.multiple_of(lax.rem(mdl + k + 4 - grp, 4) * feats, feats), feats)
-        part = lax.dot_general(keep[...], mine[at, :], NT, preferred_element_type=F32)
-        part = part + lax.dot_general(got[...], theirs[at, :], NT, preferred_element_type=F32)
-        outs[k][...] = part.astype(BF16)
+        part = lax.dot_general(keep[...], mine[k][...], NT, preferred_element_type=F32)
+        part = part + lax.dot_general(got[...], theirs[k][...], NT, preferred_element_type=F32)
+        held[lax.rem(grp + k + 4 - mdl, 4)] = part.astype(BF16)
+    for k in range(4):
+        outs[k][...] = held[k]
 
 
 def around(x, axis, size):
@@ -302,7 +300,7 @@
     def shaped(*shape):
         return jax.ShapeDtypeStruct(shape, BF16)
 
-    def call(body, name, outs, *args, scalars=1, limit=VMEM_LIMIT):
+    def call(body, name, outs, *args, scalars=1, limit=VMEM_LIMIT, scratch=()):
         whole = lambda x: pl.BlockSpec(x.shape, lambda i, n=len(x.shape): (0,) * n)
         traffic = sum(x.size * x.dtype.itemsize for x in (*args, *jax.tree.leaves(outs)))
         return pl.pallas_call(
@@ -311,6 +309,7 @@
             grid=(1,),
             in_specs=[sspec()] * scalars + [whole(x) for x in args[scalars:]],
             out_specs=jax.tree.map(whole, outs),
+            scratch_shapes=scratch,
             compiler_params=params(("arbitrary",), limit),
             cost_estimate=pl.CostEstimate(
                 flops=10**9, bytes_accessed=traffic, transcendentals=0
@@ -335,8 +334,6 @@
     w_z, *both = lax.optimization_barrier((w_z, *hid, *hid_other))
     hid, hid_other = both[:4], both[4:]
     w_kv = around(w_z[:, : 2 * HD], "grp", 4)
-    rest, *w_kv = lax.optimization_barrier((w_z[:, 2 * HD :], *w_kv))
-    w_qo = around(rest, "grp", 4)
 
     tables = rotary_tables(zsize * chip_rows, chip_rows, zsize)
 
@@ -358,14 +355,12 @@
         lax.ppermute(x, "z", [(i, (i + zsize - k) % zsize) for i in range(zsize)])
         for k, x in zip(AWAY, sends)
     ]
-    q, w_o = call(
-        q_kernel,
-        "q_proj",
-        (shaped(4, chip_rows, 2 * HD), shaped(4 * depth, 4 * HD)),
-        ids, normed, *w_qo, *tables,
-    )
-    w_theirs = swap(w_o)
-
+    w_q, own_new = lax.optimization_barrier((w_z[:, 2 * HD : 6 * HD], own_new))
+    w_q = around(w_q, "grp", 4)
+    w_q[1], *blocks[:NEAR] = lax.optimization_barrier((w_q[1], *blocks[:NEAR]))
+    q = call(
+        q_kernel, "q_proj", shaped(4, chip_rows, 2 * HD), ids, normed, *w_q, *tables
+    )
     def work(count):
         pairs = count * 4 * chip_rows * chip_rows
         return pl.CostEstimate(flops=1024 * pairs, bytes_accessed=2**22, transcendentals=pairs)
@@ -383,6 +378,8 @@
         cost_estimate=work(2 + NEAR),
         name="attention_near",
     )(ids, sink_logits, q, prefix, own_new, *blocks[:NEAR])
+    state, w_o = lax.optimization_barrier((state, w_z[:, 6 * HD :]))
+    w_o = around(w_o, "grp", 4)
     mixed = pl.pallas_call(
         second_kernel,
         out_shape=jax.ShapeDtypeStruct((2, tok_rows, 4 * HD), BF16),
@@ -395,9 +392,17 @@
         name="attention_far",
     )(ids, q, state, *blocks[NEAR:])
 
+    mixed, *w_o = lax.optimization_barrier((mixed, *w_o))
     got = swap(mixed[1])
+    w_theirs = [swap(w) for w in w_o]
     piece = jax.ShapeDtypeStruct((tok_rows, feats), BF16)
-    parts = call(out_kernel, "out_proj", (piece,) * 4, ids, mixed[0], got, w_o, w_theirs)
+    parts = call(
+        out_kernel,
+        "out_proj",
+        (piece,) * 4,
+        ids, mixed[0], got, *w_o, *w_theirs,
+        scratch=[pltpu.VMEM((4, tok_rows, feats), BF16)],
+    )
     arrived = {
         k: lax.ppermute(parts[k], "mdl", [(i, (i + k) % 4) for i in range(4)]) for k in (2, 1, 3)
     }

time: 124 us -> 120 us (0.968)
  waiting for transfers between devices: 46.5 us -> 38.8 us
  starting transfers between devices: 39.9 us -> 44.5 us
    ppermute x9 -> x12, waiting for transfers between devices: 29.9 us -> 17.7 us  [around(): lax.ppermute(x, axis, [((i + k) % size, i) for i in range(size)])]
    ppermute x7, waiting for transfers between devices: 0.02 us -> 5.79 us  [on_device(): lax.ppermute(x, 'z', [(i, (i + zsize - k) % zsize) for i in range(zsize)])]
    ppermute x9 -> x12, starting transfers between devices: 11.4 us -> 14.9 us  [around(): lax.ppermute(x, axis, [((i + k) % size, i) for i in range(size)])]
    ppermute x3, waiting for transfers between devices: 14.1 us -> 12.1 us  [on_device(): lax.ppermute(parts[k], 'mdl', [(i, (i + k) % 4) for i in range(4)])]
    ppermute x3, starting transfers between devices: 2.14 us -> 3.75 us  [on_device(): lax.ppermute(parts[k], 'mdl', [(i, (i + k) % 4) for i in range(4)])]
    ppermute x7 -> x10, waiting for transfers between devices: 2.48 us -> 3.2 us  [swap(): return lax.ppermute(x, 'core', [(0, 1), (1, 0)])]
  transfers between devices with their start and end apart: 27 -> 33, of which waited for: 12 -> 11; matrix products, arithmetic and copies ran while one was open for 1% -> 1% of each run, Pallas kernels for 24% -> 20%
where the time goes in v3:
time: 120 us; the launch traced here: 119 us
  starting transfers between devices  44.5 us (37%)
  waiting for transfers between devices  38.8 us (32%)
  Pallas kernels  31.5 us (26%)
  local copies, waits for them, and re-layouts  2.07 us (2%)
    ppermute x12, waiting for transfers between devices, around(): lax.ppermute(x, axis, [((i + k) % size, i) for i in range(size)])  17.7 us
    ppermute x7, starting transfers between devices, on_device(): lax.ppermute(x, 'z', [(i, (i + zsize - k) % zsize) for i in range(zsize)])  15.6 us
    ppermute x12, starting transfers between devices, around(): lax.ppermute(x, axis, [((i + k) % size, i) for i in range(size)])  14.9 us
    pallas_call x5, Pallas kernels, call(): pl.pallas_call(body, out_shape=outs, grid=(1,), in_specs=[sspec()] * scal...  12.9 us
    ppermute x3, waiting for transfers between devices, on_device(): lax.ppermute(parts[k], 'mdl', [(i, (i + k) % 4) for i in range(4)])  12.1 us
    pallas_call x1, Pallas kernels, on_device(): pl.pallas_call(first_kernel, out_shape=jax.ShapeDtypeStruct((4, chip_rows...  10.7 us
    all_to_all x1, starting transfers between devices, on_device(): lax.all_to_all(fan, ('z', 'core'), 0, 0, tiled=True).reshape(depth, 10 * HD)  8.59 us
    pallas_call x1, Pallas kernels, on_device(): pl.pallas_call(second_kernel, out_shape=jax.ShapeDtypeStruct((2, tok_rows...  7.87 us
  transfers between devices with their start and end apart: 33, of which 11 were waited for; matrix products, arithmetic and copies ran while one was open for 1% of the time, Pallas kernels for 20%

profile of v3, /device:TPU:32, one launch (start us, length us, event | category | flops | bytes accessed | tf_op | source)
XLA Modules:
  0.0 118.6 jit_solution(14326604350900296149)
XLA Ops:
  0.7 0.7 stack.19.ids
  1.3 2.0 %split.1 = (bf16[16,32,640]{2,1,0:T(8,128)(2,1)}, bf16[256,128]{1,0:T(8,128)(2,1)}, bf16[256,128]{1,0:T(8,128)(2,1)}) custom-call(s32[5]{0:T(128)} %stack.19.ids, bf16[32,512]{1,0:T(8,128)(2,1)} %wq.1, bf16[32,128]{1,0:T(8,128)(2,1)} %wk.1, bf16[32,128]{1,0:T(8,128)(2,1)} %wv.1, bf16[32,512]{1,0:T(8,128)(2,1)} %wo.1, bf16[256,128]{1,0:T(8,128)(2,1)} %bitcast.21, ...), custom_call_target="tpu_custom_call" | custom-call | flops 1000000000 | bytes 999444 | tf_op jit(solution)/shard_map/split/pallas_call | solution.py:306
  3.4 8.6 %all-to-all-start = ((bf16[16,32,640]{2,1,0:T(8,128)(2,1)}), bf16[16,32,640]{2,1,0:T(8,128)(2,1)S(1)}, u32[]{:S(2)}, u32[]{:S(2)}) async-start(bf16[16,32,640]{2,1,0:T(8,128)(2,1)} %get-tuple-element.44), calls=%async_computation | async-start | bytes 1310720 | tf_op jit(solution)/shard_map/all_to_all | solution.py:332
  11.9 3.1 %collective-permute-start = (bf16[256,512]{1,0:T(8,128)(2,1)S(1)}, bf16[256,512]{1,0:T(8,128)(2,1)S(1)}, u32[]{:S(2)}, u32[]{:S(2)}) collective-permute-start(bf16[256,512]{1,0:T(8,128)(2,1)S(1)} %bitcast.17), channel_id=1, source_target_pairs={{1,0},{2,1},{3,2},{0,3},{5,4},{6,5},{7,6},{4,7},{9,8},{10,9},{11,1... | collective-permute-start | bytes 786440 | tf_op jit(solution)/shard_map/ppermute | solution.py:273
  15.0 0.6 collective-permute-start.1
  15.7 1.0 collective-permute-start.2
  16.6 0.0 collective-permute-start.3
  16.6 9.9 %collective-permute-done.refs_1_ = bf16[256,512]{1,0:T(8,128)(2,1)S(1)} collective-permute-done((bf16[256,512]{1,0:T(8,128)(2,1)S(1)}, bf16[256,512]{1,0:T(8,128)(2,1)S(1)}, u32[]{:S(2)}, u32[]{:S(2)}) %collective-permute-start) | collective-permute-done | bytes 262176 | tf_op jit(solution)/shard_map/ppermute | solution.py:273
  26.5 0.5 collective-permute-start.5
  27.0 3.2 %collective-permute-done.2.refs_3_ = bf16[256,512]{1,0:T(8,128)(2,1)S(1)} collective-permute-done((bf16[256,512]{1,0:T(8,128)(2,1)S(1)}, bf16[256,512]{1,0:T(8,128)(2,1)S(1)}, u32[]{:S(2)}, u32[]{:S(2)}) %collective-permute-start.2) | collective-permute-done | bytes 262176 | tf_op jit(solution)/shard_map/ppermute | solution.py:273
  30.2 0.0 collective-permute-start.6
  30.3 0.0 collective-permute-done.3.refs_4_
  30.3 0.0 collective-permute-done.5.refs_6_
  30.3 1.5 %collective-permute-done.6.refs_7_ = bf16[256,512]{1,0:T(8,128)(2,1)S(1)} collective-permute-done((bf16[256,512]{1,0:T(8,128)(2,1)S(1)}, bf16[256,512]{1,0:T(8,128)(2,1)S(1)}, u32[]{:S(2)}, u32[]{:S(2)}) %collective-permute-start.6) | collective-permute-done | bytes 262176 | tf_op jit(solution)/shard_map/ppermute | solution.py:278
  31.8 0.0 all-to-all-done
  31.8 2.8 %collective-permute-start.7 = (bf16[512,128]{1,0:T(8,128)(2,1)S(1)}, bf16[512,128]{1,0:T(8,128)(2,1)S(1)}, u32[]{:S(2)}, u32[]{:S(2)}) collective-permute-start(bf16[512,128]{1,0:T(8,128)(2,1)S(1)} %slice.16.w0), channel_id=1, source_target_pairs={{64,0},{128,64},{192,128},{0,192},{65,1},{129,65},{193,129},{1,193... | collective-permute-start | bytes 393224 | tf_op jit(solution)/shard_map/ppermute | solution.py:273
  34.6 0.8 collective-permute-start.8
  35.4 0.9 collective-permute-start.9
  36.3 0.0 collective-permute-start.10
  36.3 0.6 reshape.7.refs_8_
  37.0 3.8 %norm.1.normed = bf16[512,2048]{1,0:T(8,128)(2,1)} custom-call(s32[5]{0:T(128)} %stack.19.ids, bf16[256,512]{1,0:T(8,128)(2,1)} %bitcast.16, bf16[256,512]{1,0:T(8,128)(2,1)} %copy-done.8, bf16[256,512]{1,0:T(8,128)(2,1)} %copy-done.9, bf16[256,512]{1,0:T(8,128)(2,1)} %copy-done.10, bf16[256,512]{1,0:T(8,128)(2,1)} %copy-done.11, ...), custom_call_target="tpu_custom_call" | custom-call | flops 1000000000 | bytes 4198420 | tf_op jit(solution)/shard_map/norm/pallas_call | solution.py:306
  40.8 0.0 collective-permute-done.10.p_got
  40.8 0.0 collective-permute-done.7.w1
  40.8 0.0 copy-start.17
  40.8 1.7 %collective-permute-done.8.w2 = bf16[512,128]{1,0:T(8,128)(2,1)S(1)} collective-permute-done((bf16[512,128]{1,0:T(8,128)(2,1)S(1)}, bf16[512,128]{1,0:T(8,128)(2,1)S(1)}, u32[]{:S(2)}, u32[]{:S(2)}) %collective-permute-start.8) | collective-permute-done | bytes 131104 | tf_op jit(solution)/shard_map/ppermute | solution.py:273
  42.5 1.7 %collective-permute-done.9.w3 = bf16[512,128]{1,0:T(8,128)(2,1)S(1)} collective-permute-done((bf16[512,128]{1,0:T(8,128)(2,1)S(1)}, bf16[512,128]{1,0:T(8,128)(2,1)S(1)}, u32[]{:S(2)}, u32[]{:S(2)}) %collective-permute-start.9) | collective-permute-done | bytes 131104 | tf_op jit(solution)/shard_map/ppermute | solution.py:273
  44.2 0.6 copy-done.19
  44.9 4.1 %kv_proj.1 = (bf16[512,128]{1,0:T(8,128)(2,1)}, bf16[512,128]{1,0:T(8,128)(2,1)}, bf16[512,128]{1,0:T(8,128)(2,1)}, bf16[512,128]{1,0:T(8,128)(2,1)}, bf16[512,1...) custom-call(s32[5]{0:T(128)} %stack.19.ids, ...), custom_call_target="tpu_custom_call" | custom-call | flops 1000000000 | bytes 4198420 | tf_op jit(solution)/shard_map/kv_proj/pallas_call | solution.py:306
  49.0 0.5 collective-permute-start.12
  49.6 0.0 copy-start.4
  49.6 1.6 %collective-permute-start.13 = (bf16[512,128]{1,0:T(8,128)(2,1)}, bf16[512,128]{1,0:T(8,128)(2,1)S(1)}, u32[]{:S(2)}, u32[]{:S(2)}) collective-permute-start(bf16[512,128]{1,0:T(8,128)(2,1)} %get-tuple-element.59), channel_id=1, source_target_pairs={{0,8},{8,16},{16,24},{24,32},{32,40},{40,48},{48,56},{56,0},{1,9},... | collective-permute-start | bytes 393224 | tf_op jit(solution)/shard_map/ppermute | solution.py:355
  51.2 0.6 collective-permute-start.11
  51.8 0.8 collective-permute-start.16
  52.6 0.9 collective-permute-start.17
  53.4 1.2 %collective-permute-done.12.refs_0_ = bf16[512,128]{1,0:T(8,128)(2,1)S(1)} collective-permute-done((bf16[512,128]{1,0:T(8,128)(2,1)}, bf16[512,128]{1,0:T(8,128)(2,1)S(1)}, u32[]{:S(2)}, u32[]{:S(2)}) %collective-permute-start.12) | collective-permute-done | bytes 131104 | tf_op jit(solution)/shard_map/ppermute | solution.py:355
  54.6 3.9 %collective-permute-start.14 = (bf16[512,128]{1,0:T(8,128)(2,1)}, bf16[512,128]{1,0:T(8,128)(2,1)S(1)}, u32[]{:S(2)}, u32[]{:S(2)}) collective-permute-start(bf16[512,128]{1,0:T(8,128)(2,1)} %get-tuple-element.60), channel_id=1, source_target_pairs={{0,48},{8,56},{16,0},{24,8},{32,16},{40,24},{48,32},{56,40},{1,49}... | collective-permute-start | bytes 393224 | tf_op jit(solution)/shard_map/ppermute | solution.py:355
  58.6 0.0 collective-permute-done.13.refs_1_
  58.6 0.0 collective-permute-start.15
  58.6 4.5 %collective-permute-done.14.refs_2_ = bf16[512,128]{1,0:T(8,128)(2,1)S(1)} collective-permute-done((bf16[512,128]{1,0:T(8,128)(2,1)}, bf16[512,128]{1,0:T(8,128)(2,1)S(1)}, u32[]{:S(2)}, u32[]{:S(2)}) %collective-permute-start.14) | collective-permute-done | bytes 131104 | tf_op jit(solution)/shard_map/ppermute | solution.py:355
  63.1 4.9 %collective-permute-start.18 = (bf16[512,128]{1,0:T(8,128)(2,1)}, bf16[512,128]{1,0:T(8,128)(2,1)S(1)}, u32[]{:S(2)}, u32[]{:S(2)}) collective-permute-start(bf16[512,128]{1,0:T(8,128)(2,1)} %get-tuple-element.70), channel_id=1, source_target_pairs={{0,40},{8,48},{16,56},{24,0},{32,8},{40,16},{48,24},{56,32},{1,41}... | collective-permute-start | bytes 393224 | tf_op jit(solution)/shard_map/ppermute | solution.py:355
  68.0 0.0 collective-permute-done.15.refs_3_
  68.0 2.4 %collective-permute-start.19 = (bf16[512,128]{1,0:T(8,128)(2,1)}, bf16[512,128]{1,0:T(8,128)(2,1)S(1)}, u32[]{:S(2)}, u32[]{:S(2)}) collective-permute-start(bf16[512,128]{1,0:T(8,128)(2,1)} %get-tuple-element.71), channel_id=1, source_target_pairs={{0,24},{8,32},{16,40},{24,48},{32,56},{40,0},{48,8},{56,16},{1,25}... | collective-permute-start | bytes 393224 | tf_op jit(solution)/shard_map/ppermute | solution.py:355
  70.4 0.0 collective-permute-done.11.w1
  70.4 2.2 %collective-permute-start.20 = (bf16[512,128]{1,0:T(8,128)(2,1)}, bf16[512,128]{1,0:T(8,128)(2,1)S(1)}, u32[]{:S(2)}, u32[]{:S(2)}) collective-permute-start(bf16[512,128]{1,0:T(8,128)(2,1)} %get-tuple-element.72), channel_id=1, source_target_pairs={{0,32},{8,40},{16,48},{24,56},{32,0},{40,8},{48,16},{56,24},{1,33}... | collective-permute-start | bytes 393224 | tf_op jit(solution)/shard_map/ppermute | solution.py:355
  72.7 1.6 %q_proj.1.q = bf16[4,512,128]{2,1,0:T(8,128)(2,1)S(1)} custom-call(s32[5]{0:T(128)S(1)} %copy-done.2, bf16[512,2048]{1,0:T(8,128)(2,1)S(1)} %copy-done, bf16[512,256]{1,0:T(8,128)(2,1)S(1)} %get-tuple-element.57.w0, bf16[512,256]{1,0:T(8,128)(2,1)S(1)} %collective-permute-done.11.w1, bf16[512,256]{1,0:T(8,128)(2,1)S(1)} %collective-permute-done.16.w2, ...), custom_call_target="tpu_custom_call" | custom-call | flops 1000000000 | bytes 3936276 | tf_op jit(solution)/shard_map/q_proj/pallas_call | solution.py:306
  74.4 10.7 %attention_near.1.state = f32[4,512,128]{2,1,0:T(8,128)S(1)} custom-call(s32[5]{0:T(128)S(1)} %copy-done.2, f32[8]{0:T(128)S(1)} %copy-done.4, bf16[4,512,128]{2,1,0:T(8,128)(2,1)S(1)} %q_proj.1.q, bf16[512,128]{1,0:T(8,128)(2,1)S(1)} %copy-done.6, bf16[512,128]{1,0:T(8,128)(2,1)S(1)} %copy-done.5, bf16[512,128]{1,0:T(8,128)(2,1)S(1)} %collective-permute-done.12.refs_0_, ...), custom_call_target="tpu_custom_call" | custom-call | flops 6442450944 | bytes 4194304 | tf_op jit(solution)/shard_map/attention_near/pallas_call | solution.py:370
  85.1 1.2 collective-permute-start.21
  86.2 1.0 collective-permute-start.22
  87.2 1.3 %collective-permute-start.23 = (bf16[512,256]{1,0:T(8,128)(2,1)S(1)}, bf16[512,256]{1,0:T(8,128)(2,1)S(1)}, u32[]{:S(2)}, u32[]{:S(2)}) collective-permute-start(bf16[512,256]{1,0:T(8,128)(2,1)S(1)} %get-tuple-element.75.refs_0_), channel_id=1, source_target_pairs={{192,0},{0,64},{64,128},{128,192},{193,1},{1,65},{65,129},{129,193... | collective-permute-start | bytes 786440 | tf_op jit(solution)/shard_map/ppermute | solution.py:273
  88.6 7.9 %attention_far.1 = bf16[2,256,256]{2,1,0:T(8,128)(2,1)S(1)} custom-call(s32[5]{0:T(128)S(1)} %copy-done.2, bf16[4,512,128]{2,1,0:T(8,128)(2,1)S(1)} %q_proj.1.q, f32[4,512,128]{2,1,0:T(8,128)S(1)} %attention_near.1.state, bf16[512,128]{1,0:T(8,128)(2,1)S(1)} %collective-permute-done.18.refs_0_, bf16[512,128]{1,0:T(8,128)(2,1)S(1)} %collective-permute-done.19.refs_1_, ...), custom_call_target="tpu_custom_call" | custom-call | flops 3221225472 | bytes 4194304 | tf_op jit(solution)/shard_map/attention_far/pallas_call | solution.py:383
  96.5 1.2 %collective-permute-done.23.refs_3_ = bf16[512,256]{1,0:T(8,128)(2,1)S(1)} collective-permute-done((bf16[512,256]{1,0:T(8,128)(2,1)S(1)}, bf16[512,256]{1,0:T(8,128)(2,1)S(1)}, u32[]{:S(2)}, u32[]{:S(2)}) %collective-permute-start.23) | collective-permute-done | bytes 262176 | tf_op jit(solution)/shard_map/ppermute | solution.py:273
  97.7 0.0 collective-permute-start.25
  97.7 0.5 collective-permute-start.26
  98.2 0.0 collective-permute-start.27
  98.2 0.5 collective-permute-start.28
  98.7 0.1 collective-permute-start.24
  98.8 1.7 %collective-permute-done.24.got = bf16[256,256]{1,0:T(8,128)(2,1)S(1)} collective-permute-done((bf16[256,256]{1,0:T(8,128)(2,1)S(1)}, bf16[256,256]{1,0:T(8,128)(2,1)S(1)}, u32[]{:S(2)}, u32[]{:S(2)}) %collective-permute-start.24) | collective-permute-done | bytes 131104 | tf_op jit(solution)/shard_map/ppermute | solution.py:278
  100.6 1.3 %out_proj.1 = (bf16[256,512]{1,0:T(8,128)(2,1)S(1)}, bf16[256,512]{1,0:T(8,128)(2,1)S(1)}, bf16[256,512]{1,0:T(8,128)(2,1)S(1)}, bf16[256,512]{1,0:T(8,128)(2,1)S(1)}) custom-call(s32[5]{0:T(128)S(1)} %copy-done.2, bf16[256,256]{1,0:T(8,128)(2,1)S(1)} %get-tuple-element.86.keep, bf16[256,256]{1,0:T(8,128)(2,1)S(1)} %collective-permute-done.24.got, ...), custom_call_target="tpu_custom_call" | custom-call | flops 1000000000 | bytes 3407892 | tf_op jit(solution)/shard_map/out_proj/pallas_call | solution.py:306
  101.9 0.1 collective-permute-start.29
  102.0 2.2 %collective-permute-start.30 = (bf16[256,512]{1,0:T(8,128)(2,1)S(1)}, bf16[256,512]{1,0:T(8,128)(2,1)S(1)}, u32[]{:S(2)}, u32[]{:S(2)}) collective-permute-start(bf16[256,512]{1,0:T(8,128)(2,1)S(1)} %get-tuple-element.81), channel_id=1, source_target_pairs={{0,2},{1,3},{2,0},{3,1},{4,6},{5,7},{6,4},{7,5},{8,10},{9,11},{10,... | collective-permute-start | bytes 786440 | tf_op jit(solution)/shard_map/ppermute | solution.py:407
  104.2 1.4 %collective-permute-start.31 = (bf16[256,512]{1,0:T(8,128)(2,1)S(1)}, bf16[256,512]{1,0:T(8,128)(2,1)S(1)}, u32[]{:S(2)}, u32[]{:S(2)}) collective-permute-start(bf16[256,512]{1,0:T(8,128)(2,1)S(1)} %get-tuple-element.82), channel_id=1, source_target_pairs={{0,3},{1,0},{2,1},{3,2},{4,7},{5,4},{6,5},{7,6},{8,11},{9,8},{10,9... | collective-permute-start | bytes 786440 | tf_op jit(solution)/shard_map/ppermute | solution.py:407
  105.7 11.5 %collective-permute-done.29 = bf16[256,512]{1,0:T(8,128)(2,1)S(1)} collective-permute-done((bf16[256,512]{1,0:T(8,128)(2,1)S(1)}, bf16[256,512]{1,0:T(8,128)(2,1)S(1)}, u32[]{:S(2)}, u32[]{:S(2)}) %collective-permute-start.29) | collective-permute-done | bytes 262176 | tf_op jit(solution)/shard_map/ppermute | solution.py:407
  117.2 0.6 collective-permute-done.31
  117.8 0.8 fusion
  (57 shorter events, 0.2 us)
Async XLA Ops:
  1.3 10.6 %copy-start.7 = (bf16[1,256,512]{2,1,0:T(8,128)(2,1)S(1)}, bf16[1,256,512]{2,1,0:T(8,128)(2,1)}, u32[]{:S(2)}) copy-start(bf16[1,256,512]{2,1,0:T(8,128)(2,1)} %param.12) | copy-start | bytes 786436
  1.3 35.0 %copy-start.16 = (bf16[2048]{0:T(1024)(128)(2,1)S(1)}, bf16[2048]{0:T(1024)(128)(2,1)}, u32[]{:S(2)}) copy-start(bf16[2048]{0:T(1024)(128)(2,1)} %param.14) | copy-start | bytes 12292
  3.4 28.4 %all-to-all-start = ((bf16[16,32,640]{2,1,0:T(8,128)(2,1)}), bf16[16,32,640]{2,1,0:T(8,128)(2,1)S(1)}, u32[]{:S(2)}, u32[]{:S(2)}) async-start(bf16[16,32,640]{2,1,0:T(8,128)(2,1)} %get-tuple-element.44), calls=%async_computation | async-start | bytes 1310720 | tf_op jit(solution)/shard_map/all_to_all | solution.py:332
  11.9 14.6 %collective-permute-start = (bf16[256,512]{1,0:T(8,128)(2,1)S(1)}, bf16[256,512]{1,0:T(8,128)(2,1)S(1)}, u32[]{:S(2)}, u32[]{:S(2)}) collective-permute-start(bf16[256,512]{1,0:T(8,128)(2,1)S(1)} %bitcast.17), channel_id=1, source_target_pairs={{1,0},{2,1},{3,2},{0,3},{5,4},{6,5},{7,6},{4,7},{9,8},{10,9},{11,1... | collective-permute-start | bytes 786440 | tf_op jit(solution)/shard_map/ppermute | solution.py:273
  15.0 11.5 %collective-permute-start.1 = (bf16[256,512]{1,0:T(8,128)(2,1)S(1)}, bf16[256,512]{1,0:T(8,128)(2,1)S(1)}, u32[]{:S(2)}, u32[]{:S(2)}) collective-permute-start(bf16[256,512]{1,0:T(8,128)(2,1)S(1)} %bitcast.18), channel_id=1, source_target_pairs={{2,0},{3,1},{0,2},{1,3},{6,4},{7,5},{4,6},{5,7},{10,8},{11,9},{8,1... | collective-permute-start | bytes 786440 | tf_op jit(solution)/shard_map/ppermute | solution.py:273
  15.7 14.6 %collective-permute-start.2 = (bf16[256,512]{1,0:T(8,128)(2,1)S(1)}, bf16[256,512]{1,0:T(8,128)(2,1)S(1)}, u32[]{:S(2)}, u32[]{:S(2)}) collective-permute-start(bf16[256,512]{1,0:T(8,128)(2,1)S(1)} %bitcast.19), channel_id=1, source_target_pairs={{3,0},{0,1},{1,2},{2,3},{7,4},{4,5},{5,6},{6,7},{11,8},{8,9},{9,10... | collective-permute-start | bytes 786440 | tf_op jit(solution)/shard_map/ppermute | solution.py:273
  16.6 13.6 %collective-permute-start.3 = (bf16[256,512]{1,0:T(8,128)(2,1)S(1)}, bf16[256,512]{1,0:T(8,128)(2,1)S(1)}, u32[]{:S(2)}, u32[]{:S(2)}) collective-permute-start(bf16[256,512]{1,0:T(8,128)(2,1)S(1)} %bitcast.20), channel_id=1, source_target_pairs={{0,4},{4,0},{1,5},{5,1},{2,6},{6,2},{3,7},{7,3},{8,12},{12,8},{9,1... | collective-permute-start | bytes 786440 | tf_op jit(solution)/shard_map/ppermute | solution.py:278
  26.5 10.4 %copy-start.8 = (bf16[256,512]{1,0:T(8,128)(2,1)}, bf16[256,512]{1,0:T(8,128)(2,1)S(1)}, u32[]{:S(2)}) copy-start(bf16[256,512]{1,0:T(8,128)(2,1)S(1)} %collective-permute-done.refs_1_) | copy-start | bytes 786436
  26.5 3.7 %collective-permute-start.4 = (bf16[256,512]{1,0:T(8,128)(2,1)S(1)}, bf16[256,512]{1,0:T(8,128)(2,1)S(1)}, u32[]{:S(2)}, u32[]{:S(2)}) collective-permute-start(bf16[256,512]{1,0:T(8,128)(2,1)S(1)} %collective-permute-done.refs_1_), channel_id=1, source_target_pairs={{0,4},{4,0},{1,5},{5,1},{2,6},{6,2},{3,7},{7,3},{8,12},{12,8},{9,1... | collective-permute-start | bytes 786440 | tf_op jit(solution)/shard_map/ppermute | solution.py:278
  26.5 10.4 %copy-start.9 = (bf16[256,512]{1,0:T(8,128)(2,1)}, bf16[256,512]{1,0:T(8,128)(2,1)S(1)}, u32[]{:S(2)}) copy-start(bf16[256,512]{1,0:T(8,128)(2,1)S(1)} %collective-permute-done.1.refs_2_) | copy-start | bytes 786436
  26.5 3.7 %collective-permute-start.5 = (bf16[256,512]{1,0:T(8,128)(2,1)S(1)}, bf16[256,512]{1,0:T(8,128)(2,1)S(1)}, u32[]{:S(2)}, u32[]{:S(2)}) collective-permute-start(bf16[256,512]{1,0:T(8,128)(2,1)S(1)} %collective-permute-done.1.refs_2_), channel_id=1, source_target_pairs={{0,4},{4,0},{1,5},{5,1},{2,6},{6,2},{3,7},{7,3},{8,12},{12,8},{9,1... | collective-permute-start | bytes 786440 | tf_op jit(solution)/shard_map/ppermute | solution.py:278
  30.2 6.7 %copy-start.10 = (bf16[256,512]{1,0:T(8,128)(2,1)}, bf16[256,512]{1,0:T(8,128)(2,1)S(1)}, u32[]{:S(2)}) copy-start(bf16[256,512]{1,0:T(8,128)(2,1)S(1)} %collective-permute-done.2.refs_3_) | copy-start | bytes 786436
  30.2 1.5 %collective-permute-start.6 = (bf16[256,512]{1,0:T(8,128)(2,1)S(1)}, bf16[256,512]{1,0:T(8,128)(2,1)S(1)}, u32[]{:S(2)}, u32[]{:S(2)}) collective-permute-start(bf16[256,512]{1,0:T(8,128)(2,1)S(1)} %collective-permute-done.2.refs_3_), channel_id=1, source_target_pairs={{0,4},{4,0},{1,5},{5,1},{2,6},{6,2},{3,7},{7,3},{8,12},{12,8},{9,1... | collective-permute-start | bytes 786440 | tf_op jit(solution)/shard_map/ppermute | solution.py:278
  30.3 6.7 %copy-start.11 = (bf16[256,512]{1,0:T(8,128)(2,1)}, bf16[256,512]{1,0:T(8,128)(2,1)S(1)}, u32[]{:S(2)}) copy-start(bf16[256,512]{1,0:T(8,128)(2,1)S(1)} %collective-permute-done.3.refs_4_) | copy-start | bytes 786436
  30.3 6.7 %copy-start.12 = (bf16[256,512]{1,0:T(8,128)(2,1)}, bf16[256,512]{1,0:T(8,128)(2,1)S(1)}, u32[]{:S(2)}) copy-start(bf16[256,512]{1,0:T(8,128)(2,1)S(1)} %collective-permute-done.4.refs_5_) | copy-start | bytes 786436
  30.3 6.7 %copy-start.13 = (bf16[256,512]{1,0:T(8,128)(2,1)}, bf16[256,512]{1,0:T(8,128)(2,1)S(1)}, u32[]{:S(2)}) copy-start(bf16[256,512]{1,0:T(8,128)(2,1)S(1)} %collective-permute-done.5.refs_6_) | copy-start | bytes 786436
  31.8 5.2 %copy-start.14 = (bf16[256,512]{1,0:T(8,128)(2,1)}, bf16[256,512]{1,0:T(8,128)(2,1)S(1)}, u32[]{:S(2)}) copy-start(bf16[256,512]{1,0:T(8,128)(2,1)S(1)} %collective-permute-done.6.refs_7_) | copy-start | bytes 786436
  31.8 9.0 %copy-start.15 = (bf16[512,128]{1,0:T(8,128)(2,1)}, bf16[512,128]{1,0:T(8,128)(2,1)S(1)}, u32[]{:S(2)}) copy-start(bf16[512,128]{1,0:T(8,128)(2,1)S(1)} %slice.16.w0) | copy-start | bytes 393220
  31.8 9.0 %collective-permute-start.7 = (bf16[512,128]{1,0:T(8,128)(2,1)S(1)}, bf16[512,128]{1,0:T(8,128)(2,1)S(1)}, u32[]{:S(2)}, u32[]{:S(2)}) collective-permute-start(bf16[512,128]{1,0:T(8,128)(2,1)S(1)} %slice.16.w0), channel_id=1, source_target_pairs={{64,0},{128,64},{192,128},{0,192},{65,1},{129,65},{193,129},{1,193... | collective-permute-start | bytes 393224 | tf_op jit(solution)/shard_map/ppermute | solution.py:273
  34.6 7.9 %collective-permute-start.8 = (bf16[512,128]{1,0:T(8,128)(2,1)S(1)}, bf16[512,128]{1,0:T(8,128)(2,1)S(1)}, u32[]{:S(2)}, u32[]{:S(2)}) collective-permute-start(bf16[512,128]{1,0:T(8,128)(2,1)S(1)} %slice.16.w0), channel_id=1, source_target_pairs={{128,0},{192,64},{0,128},{64,192},{129,1},{193,65},{1,129},{65,193... | collective-permute-start | bytes 393224 | tf_op jit(solution)/shard_map/ppermute | solution.py:273
  35.4 8.8 %collective-permute-start.9 = (bf16[512,128]{1,0:T(8,128)(2,1)S(1)}, bf16[512,128]{1,0:T(8,128)(2,1)S(1)}, u32[]{:S(2)}, u32[]{:S(2)}) collective-permute-start(bf16[512,128]{1,0:T(8,128)(2,1)S(1)} %slice.16.w0), channel_id=1, source_target_pairs={{192,0},{0,64},{64,128},{128,192},{193,1},{1,65},{65,129},{129,193... | collective-permute-start | bytes 393224 | tf_op jit(solution)/shard_map/ppermute | solution.py:273
  36.3 4.5 %collective-permute-start.10 = (bf16[256,128]{1,0:T(8,128)(2,1)}, bf16[256,128]{1,0:T(8,128)(2,1)S(1)}, u32[]{:S(2)}, u32[]{:S(2)}) collective-permute-start(bf16[256,128]{1,0:T(8,128)(2,1)} %get-tuple-element.55), channel_id=1, source_target_pairs={{0,4},{4,0},{1,5},{5,1},{2,6},{6,2},{3,7},{7,3},{8,12},{12,8},{9,1... | collective-permute-start | bytes 196616 | tf_op jit(solution)/shard_map/ppermute | solution.py:278
  40.8 3.4 %copy-start.20 = (bf16[256,128]{1,0:T(8,128)(2,1)}, bf16[256,128]{1,0:T(8,128)(2,1)S(1)}, u32[]{:S(2)}) copy-start(bf16[256,128]{1,0:T(8,128)(2,1)S(1)} %collective-permute-done.10.p_got) | copy-start | bytes 196612
  40.8 3.4 %copy-start.17 = (bf16[512,128]{1,0:T(8,128)(2,1)}, bf16[512,128]{1,0:T(8,128)(2,1)S(1)}, u32[]{:S(2)}) copy-start(bf16[512,128]{1,0:T(8,128)(2,1)S(1)} %collective-permute-done.7.w1) | copy-start | bytes 393220
  42.5 1.7 %copy-start.18 = (bf16[512,128]{1,0:T(8,128)(2,1)}, bf16[512,128]{1,0:T(8,128)(2,1)S(1)}, u32[]{:S(2)}) copy-start(bf16[512,128]{1,0:T(8,128)(2,1)S(1)} %collective-permute-done.8.w2) | copy-start | bytes 393220
  44.2 0.7 copy-start.19
  44.9 27.8 %copy-start = (bf16[512,2048]{1,0:T(8,128)(2,1)S(1)}, bf16[512,2048]{1,0:T(8,128)(2,1)}, u32[]{:S(2)}) copy-start(bf16[512,2048]{1,0:T(8,128)(2,1)} %norm.1.normed) | copy-start | bytes 6291460
  44.9 27.8 %copy-start.1 = (f32[512,128]{1,0:T(8,128)S(1)}, f32[512,128]{1,0:T(8,128)}, u32[]{:S(2)}) copy-start(f32[512,128]{1,0:T(8,128)} %constant.22.clone.fine) | copy-start | bytes 786436
  44.9 27.8 %copy-start.2 = (s32[5]{0:T(128)S(1)}, s32[5]{0:T(128)}, u32[]{:S(2)}) copy-start(s32[5]{0:T(128)} %stack.19.ids) | copy-start | bytes 64
  44.9 27.8 %copy-start.3 = (f32[8,128]{1,0:T(8,128)S(1)}, f32[8,128]{1,0:T(8,128)}, u32[]{:S(2)}) copy-start(f32[8,128]{1,0:T(8,128)} %constant.21.clone.coarse) | copy-start | bytes 12292
  49.0 5.6 %collective-permute-start.12 = (bf16[512,128]{1,0:T(8,128)(2,1)}, bf16[512,128]{1,0:T(8,128)(2,1)S(1)}, u32[]{:S(2)}, u32[]{:S(2)}) collective-permute-start(bf16[512,128]{1,0:T(8,128)(2,1)} %get-tuple-element.58), channel_id=1, source_target_pairs={{0,56},{8,0},{16,8},{24,16},{32,24},{40,32},{48,40},{56,48},{1,57}... | collective-permute-start | bytes 393224 | tf_op jit(solution)/shard_map/ppermute | solution.py:355
  49.6 24.7 %copy-start.4 = (f32[8]{0:T(128)S(1)}, f32[8]{0:T(128)}, u32[]{:S(2)}) copy-start(f32[8]{0:T(128)} %sinks.1) | copy-start | bytes 100
  49.6 24.7 %copy-start.5 = (bf16[512,128]{1,0:T(8,128)(2,1)S(1)}, bf16[512,128]{1,0:T(8,128)(2,1)}, u32[]{:S(2)}) copy-start(bf16[512,128]{1,0:T(8,128)(2,1)} %get-tuple-element.64.own_new) | copy-start | bytes 393220
  49.6 24.7 %copy-start.6 = (bf16[512,128]{1,0:T(8,128)(2,1)S(1)}, bf16[512,128]{1,0:T(8,128)(2,1)}, u32[]{:S(2)}) copy-start(bf16[512,128]{1,0:T(8,128)(2,1)} %get-tuple-element.63.own_prefix) | copy-start | bytes 393220
  49.6 9.0 %collective-permute-start.13 = (bf16[512,128]{1,0:T(8,128)(2,1)}, bf16[512,128]{1,0:T(8,128)(2,1)S(1)}, u32[]{:S(2)}, u32[]{:S(2)}) collective-permute-start(bf16[512,128]{1,0:T(8,128)(2,1)} %get-tuple-element.59), channel_id=1, source_target_pairs={{0,8},{8,16},{16,24},{24,32},{32,40},{40,48},{48,56},{56,0},{1,9},... | collective-permute-start | bytes 393224 | tf_op jit(solution)/shard_map/ppermute | solution.py:355
  51.2 19.2 %collective-permute-start.11 = (bf16[512,256]{1,0:T(8,128)(2,1)S(1)}, bf16[512,256]{1,0:T(8,128)(2,1)S(1)}, u32[]{:S(2)}, u32[]{:S(2)}) collective-permute-start(bf16[512,256]{1,0:T(8,128)(2,1)S(1)} %get-tuple-element.57.w0), channel_id=1, source_target_pairs={{64,0},{128,64},{192,128},{0,192},{65,1},{129,65},{193,129},{1,193... | collective-permute-start | bytes 786440 | tf_op jit(solution)/shard_map/ppermute | solution.py:273
  51.8 20.9 %collective-permute-start.16 = (bf16[512,256]{1,0:T(8,128)(2,1)S(1)}, bf16[512,256]{1,0:T(8,128)(2,1)S(1)}, u32[]{:S(2)}, u32[]{:S(2)}) collective-permute-start(bf16[512,256]{1,0:T(8,128)(2,1)S(1)} %get-tuple-element.57.w0), channel_id=1, source_target_pairs={{128,0},{192,64},{0,128},{64,192},{129,1},{193,65},{1,129},{65,193... | collective-permute-start | bytes 786440 | tf_op jit(solution)/shard_map/ppermute | solution.py:273
  52.6 20.1 %collective-permute-start.17 = (bf16[512,256]{1,0:T(8,128)(2,1)S(1)}, bf16[512,256]{1,0:T(8,128)(2,1)S(1)}, u32[]{:S(2)}, u32[]{:S(2)}) collective-permute-start(bf16[512,256]{1,0:T(8,128)(2,1)S(1)} %get-tuple-element.57.w0), channel_id=1, source_target_pairs={{192,0},{0,64},{64,128},{128,192},{193,1},{1,65},{65,129},{129,193... | collective-permute-start | bytes 786440 | tf_op jit(solution)/shard_map/ppermute | solution.py:273
  54.6 8.5 %collective-permute-start.14 = (bf16[512,128]{1,0:T(8,128)(2,1)}, bf16[512,128]{1,0:T(8,128)(2,1)S(1)}, u32[]{:S(2)}, u32[]{:S(2)}) collective-permute-start(bf16[512,128]{1,0:T(8,128)(2,1)} %get-tuple-element.60), channel_id=1, source_target_pairs={{0,48},{8,56},{16,0},{24,8},{32,16},{40,24},{48,32},{56,40},{1,49}... | collective-permute-start | bytes 393224 | tf_op jit(solution)/shard_map/ppermute | solution.py:355
  58.6 9.4 %collective-permute-start.15 = (bf16[512,128]{1,0:T(8,128)(2,1)}, bf16[512,128]{1,0:T(8,128)(2,1)S(1)}, u32[]{:S(2)}, u32[]{:S(2)}) collective-permute-start(bf16[512,128]{1,0:T(8,128)(2,1)} %get-tuple-element.61), channel_id=1, source_target_pairs={{0,16},{8,24},{16,32},{24,40},{32,48},{40,56},{48,0},{56,8},{1,17}... | collective-permute-start | bytes 393224 | tf_op jit(solution)/shard_map/ppermute | solution.py:355
  63.1 24.1 %collective-permute-start.18 = (bf16[512,128]{1,0:T(8,128)(2,1)}, bf16[512,128]{1,0:T(8,128)(2,1)S(1)}, u32[]{:S(2)}, u32[]{:S(2)}) collective-permute-start(bf16[512,128]{1,0:T(8,128)(2,1)} %get-tuple-element.70), channel_id=1, source_target_pairs={{0,40},{8,48},{16,56},{24,0},{32,8},{40,16},{48,24},{56,32},{1,41}... | collective-permute-start | bytes 393224 | tf_op jit(solution)/shard_map/ppermute | solution.py:355
  68.0 20.6 %collective-permute-start.19 = (bf16[512,128]{1,0:T(8,128)(2,1)}, bf16[512,128]{1,0:T(8,128)(2,1)S(1)}, u32[]{:S(2)}, u32[]{:S(2)}) collective-permute-start(bf16[512,128]{1,0:T(8,128)(2,1)} %get-tuple-element.71), channel_id=1, source_target_pairs={{0,24},{8,32},{16,40},{24,48},{32,56},{40,0},{48,8},{56,16},{1,25}... | collective-permute-start | bytes 393224 | tf_op jit(solution)/shard_map/ppermute | solution.py:355
  70.4 18.1 %collective-permute-start.20 = (bf16[512,128]{1,0:T(8,128)(2,1)}, bf16[512,128]{1,0:T(8,128)(2,1)S(1)}, u32[]{:S(2)}, u32[]{:S(2)}) collective-permute-start(bf16[512,128]{1,0:T(8,128)(2,1)} %get-tuple-element.72), channel_id=1, source_target_pairs={{0,32},{8,40},{16,48},{24,56},{32,0},{40,8},{48,16},{56,24},{1,33}... | collective-permute-start | bytes 393224 | tf_op jit(solution)/shard_map/ppermute | solution.py:355
  85.1 11.4 %collective-permute-start.21 = (bf16[512,256]{1,0:T(8,128)(2,1)S(1)}, bf16[512,256]{1,0:T(8,128)(2,1)S(1)}, u32[]{:S(2)}, u32[]{:S(2)}) collective-permute-start(bf16[512,256]{1,0:T(8,128)(2,1)S(1)} %get-tuple-element.75.refs_0_), channel_id=1, source_target_pairs={{64,0},{128,64},{192,128},{0,192},{65,1},{129,65},{193,129},{1,193... | collective-permute-start | bytes 786440 | tf_op jit(solution)/shard_map/ppermute | solution.py:273
  86.2 10.2 %collective-permute-start.22 = (bf16[512,256]{1,0:T(8,128)(2,1)S(1)}, bf16[512,256]{1,0:T(8,128)(2,1)S(1)}, u32[]{:S(2)}, u32[]{:S(2)}) collective-permute-start(bf16[512,256]{1,0:T(8,128)(2,1)S(1)} %get-tuple-element.75.refs_0_), channel_id=1, source_target_pairs={{128,0},{192,64},{0,128},{64,192},{129,1},{193,65},{1,129},{65,193... | collective-permute-start | bytes 786440 | tf_op jit(solution)/shard_map/ppermute | solution.py:273
  87.2 10.5 %collective-permute-start.23 = (bf16[512,256]{1,0:T(8,128)(2,1)S(1)}, bf16[512,256]{1,0:T(8,128)(2,1)S(1)}, u32[]{:S(2)}, u32[]{:S(2)}) collective-permute-start(bf16[512,256]{1,0:T(8,128)(2,1)S(1)} %get-tuple-element.75.refs_0_), channel_id=1, source_target_pairs={{192,0},{0,64},{64,128},{128,192},{193,1},{1,65},{65,129},{129,193... | collective-permute-start | bytes 786440 | tf_op jit(solution)/shard_map/ppermute | solution.py:273
  97.7 2.9 %collective-permute-start.25 = (bf16[512,256]{1,0:T(8,128)(2,1)S(1)}, bf16[512,256]{1,0:T(8,128)(2,1)S(1)}, u32[]{:S(2)}, u32[]{:S(2)}) collective-permute-start(bf16[512,256]{1,0:T(8,128)(2,1)S(1)} %get-tuple-element.75.refs_0_), channel_id=1, source_target_pairs={{0,4},{4,0},{1,5},{5,1},{2,6},{6,2},{3,7},{7,3},{8,12},{12,8},{9,1... | collective-permute-start | bytes 786440 | tf_op jit(solution)/shard_map/ppermute | solution.py:278
  97.7 2.9 %collective-permute-start.26 = (bf16[512,256]{1,0:T(8,128)(2,1)S(1)}, bf16[512,256]{1,0:T(8,128)(2,1)S(1)}, u32[]{:S(2)}, u32[]{:S(2)}) collective-permute-start(bf16[512,256]{1,0:T(8,128)(2,1)S(1)} %collective-permute-done.21.refs_1_), channel_id=1, source_target_pairs={{0,4},{4,0},{1,5},{5,1},{2,6},{6,2},{3,7},{7,3},{8,12},{12,8},{9,1... | collective-permute-start | bytes 786440 | tf_op jit(solution)/shard_map/ppermute | solution.py:278
  98.2 2.3 %collective-permute-start.27 = (bf16[512,256]{1,0:T(8,128)(2,1)S(1)}, bf16[512,256]{1,0:T(8,128)(2,1)S(1)}, u32[]{:S(2)}, u32[]{:S(2)}) collective-permute-start(bf16[512,256]{1,0:T(8,128)(2,1)S(1)} %collective-permute-done.22.refs_2_), channel_id=1, source_target_pairs={{0,4},{4,0},{1,5},{5,1},{2,6},{6,2},{3,7},{7,3},{8,12},{12,8},{9,1... | collective-permute-start | bytes 786440 | tf_op jit(solution)/shard_map/ppermute | solution.py:278
  98.2 2.3 %collective-permute-start.28 = (bf16[512,256]{1,0:T(8,128)(2,1)S(1)}, bf16[512,256]{1,0:T(8,128)(2,1)S(1)}, u32[]{:S(2)}, u32[]{:S(2)}) collective-permute-start(bf16[512,256]{1,0:T(8,128)(2,1)S(1)} %collective-permute-done.23.refs_3_), channel_id=1, source_target_pairs={{0,4},{4,0},{1,5},{5,1},{2,6},{6,2},{3,7},{7,3},{8,12},{12,8},{9,1... | collective-permute-start | bytes 786440 | tf_op jit(solution)/shard_map/ppermute | solution.py:278
  98.7 1.8 %collective-permute-start.24 = (bf16[256,256]{1,0:T(8,128)(2,1)S(1)}, bf16[256,256]{1,0:T(8,128)(2,1)S(1)}, u32[]{:S(2)}, u32[]{:S(2)}) collective-permute-start(bf16[256,256]{1,0:T(8,128)(2,1)S(1)} %get-tuple-element.85), channel_id=1, source_target_pairs={{0,4},{4,0},{1,5},{5,1},{2,6},{6,2},{3,7},{7,3},{8,12},{12,8},{9,1... | collective-permute-start | bytes 393224 | tf_op jit(solution)/shard_map/ppermute | solution.py:278
  101.9 15.3 %collective-permute-start.29 = (bf16[256,512]{1,0:T(8,128)(2,1)S(1)}, bf16[256,512]{1,0:T(8,128)(2,1)S(1)}, u32[]{:S(2)}, u32[]{:S(2)}) collective-permute-start(bf16[256,512]{1,0:T(8,128)(2,1)S(1)} %get-tuple-element.80), channel_id=1, source_target_pairs={{0,1},{1,2},{2,3},{3,0},{4,5},{5,6},{6,7},{7,4},{8,9},{9,10},{10,1... | collective-permute-start | bytes 786440 | tf_op jit(solution)/shard_map/ppermute | solution.py:407
  102.0 15.2 %collective-permute-start.30 = (bf16[256,512]{1,0:T(8,128)(2,1)S(1)}, bf16[256,512]{1,0:T(8,128)(2,1)S(1)}, u32[]{:S(2)}, u32[]{:S(2)}) collective-permute-start(bf16[256,512]{1,0:T(8,128)(2,1)S(1)} %get-tuple-element.81), channel_id=1, source_target_pairs={{0,2},{1,3},{2,0},{3,1},{4,6},{5,7},{6,4},{7,5},{8,10},{9,11},{10,... | collective-permute-start | bytes 786440 | tf_op jit(solution)/shard_map/ppermute | solution.py:407
  104.2 13.6 %collective-permute-start.31 = (bf16[256,512]{1,0:T(8,128)(2,1)S(1)}, bf16[256,512]{1,0:T(8,128)(2,1)S(1)}, u32[]{:S(2)}, u32[]{:S(2)}) collective-permute-start(bf16[256,512]{1,0:T(8,128)(2,1)S(1)} %get-tuple-element.82), channel_id=1, source_target_pairs={{0,3},{1,0},{2,1},{3,2},{4,7},{5,4},{6,5},{7,6},{8,11},{9,8},{10,9... | collective-permute-start | bytes 786440 | tf_op jit(solution)/shard_map/ppermute | solution.py:407

commit v4 on v3

--- a/solution.py
+++ b/solution.py
@@ -115,6 +115,7 @@
 
 def kv_kernel(ids, normed, w0, w1, w2, w3, coarse, fine, p_keep, p_got, own_new, own_prefix, *sends):
     grp, zed, core = ids[1], ids[2], ids[3]
+    side = pl.program_id(0)
     depth = w0.shape[0]
     rows = p_keep.shape[0]
     acc = None
@@ -123,23 +124,27 @@
         part = jnp.dot(normed[:, pl.ds(at, depth)], w[...], preferred_element_type=F32)
         acc = part if acc is None else acc + part
     lane = lax.broadcasted_iota(jnp.int32, (rows, 2 * HD), 1)
-    turn = coarse[pl.ds(zed, 1), :]
-    for side in range(2):
-        cut = slice(side * rows, (side + 1) * rows)
-        at = pl.multiple_of(lax.rem(side + core, 2) * rows, rows)
-        x = acc[cut]
-        x = jnp.where(lane < HD, rotary(x, turn, fine[pl.ds(at, rows), :]), x).astype(BF16)
-        prefix = (p_keep, p_got)[side][...]
-        own_new[cut, :] = x
-        own_prefix[cut, :] = prefix
-        for away, send in zip(AWAY, sends):
-            @pl.when(zed >= away)
-            def _(send=send, cut=cut, prefix=prefix):
-                send[cut, :] = prefix
-
-            @pl.when(zed < away)
-            def _(send=send, cut=cut, x=x):
-                send[cut, :] = x
+    at = pl.multiple_of(lax.rem(side + core, 2) * rows, rows)
+    turned = rotary(acc, coarse[pl.ds(zed, 1), :], fine[pl.ds(at, rows), :])
+    x = jnp.where(lane < HD, turned, acc).astype(BF16)
+    own_new[...] = x
+
+    @pl.when(side == 0)
+    def _():
+        own_prefix[...] = p_keep[...]
+
+    @pl.when(side != 0)
+    def _():
+        own_prefix[...] = p_got[...]
+
+    for away, send in zip(AWAY, sends):
+        @pl.when(zed >= away)
+        def _(send=send):
+            send[...] = own_prefix[...]
+
+        @pl.when(zed < away)
+        def _(send=send):
+            send[...] = own_new[...]
 
 
 def q_kernel(ids, normed, w0, w1, w2, w3, coarse, fine, q):
@@ -182,7 +187,7 @@
 
 def first_kernel(ids, sinks, q, own_prefix, own_new, *refs):
     count = len(AWAY[:NEAR])
-    blocks, (state, vals) = refs[:count], refs[count:]
+    blocks, (state, vals, keys) = refs[:count], refs[count:]
     core = ids[3]
     half, pair = pl.program_id(0), pl.program_id(1)
     block, rows = own_new.shape[0], q.shape[1]
@@ -191,29 +196,41 @@
     def _():
         for j, b in enumerate((own_prefix, own_new) + tuple(blocks)):
             vals[j] = ones_and_values(b)
-
-    row = lax.broadcasted_iota(jnp.int32, (rows, block), 0) + half * rows
-    col = lax.broadcasted_iota(jnp.int32, (rows, block), 1)
-    swing = core * (block // 2)
-    new_side = lax.rem(col + swing, block) <= lax.rem(row + swing, block)
+        keys[0] = own_prefix[...]
+        keys[1] = own_new[...]
+
+    row = lax.broadcasted_iota(jnp.int32, (rows, rows), 0)
+    col = lax.broadcasted_iota(jnp.int32, (rows, rows), 1)
+    new_side = col <= row
+    same = pl.ds(pl.multiple_of(half * rows, rows), rows)
+    rest = pl.ds(pl.multiple_of((1 - half) * rows, rows), rows)
+    later = lax.rem(half + core, 2)
     for i in range(2):
         queries = q[i]
         sink = sinks[core * 4 + pair * 2 + i]
         scores = [
             lax.dot_general(queries, b[...], NT, preferred_element_type=F32) for b in blocks
         ]
-        before = lax.dot_general(queries, own_prefix[...], NT, preferred_element_type=F32)
-        after = lax.dot_general(queries, own_new[...], NT, preferred_element_type=F32)
+        before = lax.dot_general(queries, own_prefix[same, :], NT, preferred_element_type=F32)
+        after = lax.dot_general(queries, own_new[same, :], NT, preferred_element_type=F32)
         diagonal = jnp.where(new_side, after, before)
-        top = diagonal
+        across = lax.dot_general(queries, keys[later, rest, :], NT, preferred_element_type=F32)
+        top = jnp.maximum(diagonal, across)
         for s in scores:
-            top = jnp.maximum(top, s)
+            top = jnp.maximum(top, jnp.maximum(s[:, :rows], s[:, rows:]))
         top = jnp.maximum(jnp.max(top, axis=1, keepdims=True), sink)
         shift = top * LOG2E
         p = jnp.exp2(diagonal * LOG2E - shift)
         acc = jnp.dot(
-            jnp.where(new_side, 0.0, p).astype(BF16), vals[0], preferred_element_type=F32
-        ) + jnp.dot(jnp.where(new_side, p, 0.0).astype(BF16), vals[1], preferred_element_type=F32)
+            jnp.where(new_side, 0.0, p).astype(BF16), vals[0, same, :], preferred_element_type=F32
+        ) + jnp.dot(
+            jnp.where(new_side, p, 0.0).astype(BF16), vals[1, same, :], preferred_element_type=F32
+        )
+        acc = acc + jnp.dot(
+            jnp.exp2(across * LOG2E - shift).astype(BF16),
+            vals[later, rest, :],
+            preferred_element_type=F32,
+        )
         acc = attend(scores, top, acc, [vals.at[2 + j] for j in range(count)])
         lane = lax.broadcasted_iota(jnp.int32, acc.shape, 1)
         acc = jnp.where(lane < HD, acc + jnp.exp2(sink * LOG2E - shift), acc)
@@ -330,9 +347,8 @@
 
     depth = 2 * zsize * rows_in
     w_z = lax.all_to_all(fan, ("z", "core"), 0, 0, tiled=True).reshape(depth, 10 * HD)
+    w_z, *hid = lax.optimization_barrier((w_z, *hid))
     hid_other = [swap(h) for h in hid]
-    w_z, *both = lax.optimization_barrier((w_z, *hid, *hid_other))
-    hid, hid_other = both[:4], both[4:]
     w_kv = around(w_z[:, : 2 * HD], "grp", 4)
 
     tables = rotary_tables(zsize * chip_rows, chip_rows, zsize)
@@ -344,13 +360,21 @@
         ids, *hid, *hid_other, norm_gain.reshape(1, -1),
         limit=VMEM_ALL,
     )
-    own_new, prefix, *sends = call(
+    kv_args = (normed, *w_kv, *tables, p_keep, p_got)
+    half = lambda x: pl.BlockSpec((tok_rows, x.shape[1]), lambda i: (i, 0))
+    fixed = lambda x: pl.BlockSpec(x.shape, lambda i: (0, 0))
+    own_new, prefix, *sends = pl.pallas_call(
         kv_kernel,
-        "kv_proj",
-        (shaped(chip_rows, 2 * HD),) * (2 + len(AWAY)),
-        ids, normed, *w_kv, *tables, p_keep, p_got,
-        limit=VMEM_ALL,
-    )
+        out_shape=(shaped(chip_rows, 2 * HD),) * (2 + len(AWAY)),
+        grid=(2,),
+        in_specs=[sspec(), half(normed)] + [fixed(x) for x in kv_args[1:]],
+        out_specs=(half(p_keep),) * (2 + len(AWAY)),
+        compiler_params=params(("arbitrary",), VMEM_ALL),
+        cost_estimate=pl.CostEstimate(
+            flops=10**9, bytes_accessed=2**22, transcendentals=0
+        ),
+        name="kv_proj",
+    )(ids, *kv_args)
     blocks = [
         lax.ppermute(x, "z", [(i, (i + zsize - k) % zsize) for i in range(zsize)])
         for k, x in zip(AWAY, sends)
@@ -373,7 +397,10 @@
         grid=(2, 2),
         in_specs=[sspec(), sspec(), heads_spec] + [block_spec] * (2 + NEAR),
         out_specs=heads_spec,
-        scratch_shapes=[pltpu.VMEM((2 + NEAR, chip_rows, 2 * HD), BF16)],
+        scratch_shapes=[
+            pltpu.VMEM((2 + NEAR, chip_rows, 2 * HD), BF16),
+            pltpu.VMEM((2, chip_rows, 2 * HD), BF16),
+        ],
         compiler_params=params(("arbitrary", "arbitrary")),
         cost_estimate=work(2 + NEAR),
         name="attention_near",

time: 120 us -> 119 us (level)
  waiting for transfers between devices: 38.8 us -> 37.4 us
  local copies, waits for them, and re-layouts: 2.07 us -> 3.37 us
    pallas_call x5 -> x4, Pallas kernels: 12.9 us -> 8.78 us  [call(): pl.pallas_call(body, out_shape=outs, grid=(1,), in_specs=[sspec()] * scal...]
    pallas_call x0 -> x1, Pallas kernels: none -> 3.69 us  [on_device(): pl.pallas_call(kv_kernel, out_shape=(shaped(chip_rows, 2 * HD),) * (2 + l...]
    ppermute x7, starting transfers between devices: 15.6 us -> 13 us  [on_device(): lax.ppermute(x, 'z', [(i, (i + zsize - k) % zsize) for i in range(zsize)])]
    ppermute x7, waiting for transfers between devices: 5.79 us -> 8.18 us  [on_device(): lax.ppermute(x, 'z', [(i, (i + zsize - k) % zsize) for i in range(zsize)])]
    ppermute x3, starting transfers between devices: 3.75 us -> 5.7 us  [on_device(): lax.ppermute(parts[k], 'mdl', [(i, (i + k) % 4) for i in range(4)])]
    ppermute x3, waiting for transfers between devices: 12.1 us -> 10.6 us  [on_device(): lax.ppermute(parts[k], 'mdl', [(i, (i + k) % 4) for i in range(4)])]
    ppermute x10, waiting for transfers between devices: 3.2 us -> 1.73 us  [swap(): return lax.ppermute(x, 'core', [(0, 1), (1, 0)])]
    unnamed x42, local copies, waits for them, and re-layouts: 0.72 us -> 2.03 us
where the time goes in v4:
time: 119 us; the launch traced here: 118 us
  starting transfers between devices  44.6 us (37%)
  waiting for transfers between devices  37.4 us (31%)
  Pallas kernels  30.4 us (26%)
  local copies, waits for them, and re-layouts  3.37 us (3%)
    ppermute x12, waiting for transfers between devices, around(): lax.ppermute(x, axis, [((i + k) % size, i) for i in range(size)])  16.9 us
    ppermute x12, starting transfers between devices, around(): lax.ppermute(x, axis, [((i + k) % size, i) for i in range(size)])  15.1 us
    ppermute x7, starting transfers between devices, on_device(): lax.ppermute(x, 'z', [(i, (i + zsize - k) % zsize) for i in range(zsize)])  13 us
    ppermute x3, waiting for transfers between devices, on_device(): lax.ppermute(parts[k], 'mdl', [(i, (i + k) % 4) for i in range(4)])  10.6 us
    pallas_call x1, Pallas kernels, on_device(): pl.pallas_call(first_kernel, out_shape=jax.ShapeDtypeStruct((4, chip_rows...  10.1 us
    pallas_call x4, Pallas kernels, call(): pl.pallas_call(body, out_shape=outs, grid=(1,), in_specs=[sspec()] * scal...  8.78 us
    all_to_all x1, starting transfers between devices, on_device(): lax.all_to_all(fan, ('z', 'core'), 0, 0, tiled=True).reshape(depth, 10 * HD)  8.59 us
    ppermute x7, waiting for transfers between devices, on_device(): lax.ppermute(x, 'z', [(i, (i + zsize - k) % zsize) for i in range(zsize)])  8.18 us
  transfers between devices with their start and end apart: 33, of which 11 were waited for; matrix products, arithmetic and copies ran while one was open for 1% of the time, Pallas kernels for 20%

profile of v4, /device:TPU:32, one launch (start us, length us, event | category | flops | bytes accessed | tf_op | source)
XLA Modules:
  0.0 117.5 jit_solution(13310639771266576873)
XLA Ops:
  0.7 0.7 stack.19.ids
  1.3 2.0 %split.1 = (bf16[16,32,640]{2,1,0:T(8,128)(2,1)}, bf16[256,128]{1,0:T(8,128)(2,1)}, bf16[256,128]{1,0:T(8,128)(2,1)}) custom-call(s32[5]{0:T(128)} %stack.19.ids, bf16[32,512]{1,0:T(8,128)(2,1)} %wq.1, bf16[32,128]{1,0:T(8,128)(2,1)} %wk.1, bf16[32,128]{1,0:T(8,128)(2,1)} %wv.1, bf16[32,512]{1,0:T(8,128)(2,1)} %wo.1, bf16[256,128]{1,0:T(8,128)(2,1)} %bitcast.21, ...), custom_call_target="tpu_custom_call" | custom-call | flops 1000000000 | bytes 999444 | tf_op jit(solution)/shard_map/split/pallas_call | solution.py:323
  3.4 8.6 %all-to-all-start = ((bf16[16,32,640]{2,1,0:T(8,128)(2,1)}), bf16[16,32,640]{2,1,0:T(8,128)(2,1)S(1)}, u32[]{:S(2)}, u32[]{:S(2)}) async-start(bf16[16,32,640]{2,1,0:T(8,128)(2,1)} %get-tuple-element.40), calls=%async_computation | async-start | bytes 1310720 | tf_op jit(solution)/shard_map/all_to_all | solution.py:349
  11.9 3.1 %collective-permute-start = (bf16[256,512]{1,0:T(8,128)(2,1)S(1)}, bf16[256,512]{1,0:T(8,128)(2,1)S(1)}, u32[]{:S(2)}, u32[]{:S(2)}) collective-permute-start(bf16[256,512]{1,0:T(8,128)(2,1)S(1)} %bitcast.17), channel_id=1, source_target_pairs={{1,0},{2,1},{3,2},{0,3},{5,4},{6,5},{7,6},{4,7},{9,8},{10,9},{11,1... | collective-permute-start | bytes 786440 | tf_op jit(solution)/shard_map/ppermute | solution.py:290
  15.0 0.6 collective-permute-start.1
  15.7 1.0 collective-permute-start.2
  16.6 9.9 %collective-permute-done.refs_1_ = bf16[256,512]{1,0:T(8,128)(2,1)S(1)} collective-permute-done((bf16[256,512]{1,0:T(8,128)(2,1)S(1)}, bf16[256,512]{1,0:T(8,128)(2,1)S(1)}, u32[]{:S(2)}, u32[]{:S(2)}) %collective-permute-start) | collective-permute-done | bytes 262176 | tf_op jit(solution)/shard_map/ppermute | solution.py:290
  26.5 0.0 collective-permute-done.1.refs_2_
  26.5 3.7 %collective-permute-done.2.refs_3_ = bf16[256,512]{1,0:T(8,128)(2,1)S(1)} collective-permute-done((bf16[256,512]{1,0:T(8,128)(2,1)S(1)}, bf16[256,512]{1,0:T(8,128)(2,1)S(1)}, u32[]{:S(2)}, u32[]{:S(2)}) %collective-permute-start.2) | collective-permute-done | bytes 262176 | tf_op jit(solution)/shard_map/ppermute | solution.py:290
  30.2 0.0 collective-permute-start.3
  30.3 0.5 collective-permute-start.4
  30.8 0.1 collective-permute-start.5
  30.8 0.4 collective-permute-start.6
  31.3 2.8 %collective-permute-start.7 = (bf16[512,128]{1,0:T(8,128)(2,1)S(1)}, bf16[512,128]{1,0:T(8,128)(2,1)S(1)}, u32[]{:S(2)}, u32[]{:S(2)}) collective-permute-start(bf16[512,128]{1,0:T(8,128)(2,1)S(1)} %slice.16.w0), channel_id=1, source_target_pairs={{64,0},{128,64},{192,128},{0,192},{65,1},{129,65},{193,129},{1,193... | collective-permute-start | bytes 393224 | tf_op jit(solution)/shard_map/ppermute | solution.py:290
  34.1 0.0 collective-permute-done.3.refs_4_
  34.1 0.8 collective-permute-start.8
  34.9 0.0 collective-permute-done.4.refs_5_
  34.9 0.9 collective-permute-start.9
  35.8 0.6 reshape.7.refs_8_
  36.4 0.0 collective-permute-done.5.refs_6_
  36.4 0.0 collective-permute-start.10
  36.4 0.0 collective-permute-done.6.refs_7_
  36.5 0.6 copy-done.13
  37.1 0.7 copy-done.14
  37.8 3.8 %norm.1.normed = bf16[512,2048]{1,0:T(8,128)(2,1)} custom-call(s32[5]{0:T(128)} %stack.19.ids, bf16[256,512]{1,0:T(8,128)(2,1)} %bitcast.16, bf16[256,512]{1,0:T(8,128)(2,1)} %copy-done.8, bf16[256,512]{1,0:T(8,128)(2,1)} %copy-done.9, bf16[256,512]{1,0:T(8,128)(2,1)} %copy-done.10, bf16[256,512]{1,0:T(8,128)(2,1)} %copy-done.11, ...), custom_call_target="tpu_custom_call" | custom-call | flops 1000000000 | bytes 4198420 | tf_op jit(solution)/shard_map/norm/pallas_call | solution.py:323
  41.6 0.0 collective-permute-done.10.p_got
  41.6 0.0 copy-start.17
  41.7 0.4 collective-permute-done.8.w2
  42.0 1.6 %collective-permute-done.9.w3 = bf16[512,128]{1,0:T(8,128)(2,1)S(1)} collective-permute-done((bf16[512,128]{1,0:T(8,128)(2,1)S(1)}, bf16[512,128]{1,0:T(8,128)(2,1)S(1)}, u32[]{:S(2)}, u32[]{:S(2)}) %collective-permute-start.9) | collective-permute-done | bytes 131104 | tf_op jit(solution)/shard_map/ppermute | solution.py:290
  43.7 0.6 copy-done.19
  44.3 3.7 %kv_proj.1 = (bf16[512,128]{1,0:T(8,128)(2,1)}, bf16[512,128]{1,0:T(8,128)(2,1)}, bf16[512,128]{1,0:T(8,128)(2,1)}, bf16[512,128]{1,0:T(8,128)(2,1)}, bf16[512,1...) custom-call(s32[5]{0:T(128)} %stack.19.ids, ...), custom_call_target="tpu_custom_call" | custom-call | flops 1000000000 | bytes 4194304 | tf_op jit(solution)/shard_map/kv_proj/pallas_call | solution.py:366
  48.0 2.2 %collective-permute-start.12 = (bf16[512,128]{1,0:T(8,128)(2,1)}, bf16[512,128]{1,0:T(8,128)(2,1)S(1)}, u32[]{:S(2)}, u32[]{:S(2)}) collective-permute-start(bf16[512,128]{1,0:T(8,128)(2,1)} %get-tuple-element.50), channel_id=1, source_target_pairs={{0,56},{8,0},{16,8},{24,16},{32,24},{40,32},{48,40},{56,48},{1,57}... | collective-permute-start | bytes 393224 | tf_op jit(solution)/shard_map/ppermute | solution.py:379
  50.3 0.0 copy-start.4
  50.3 0.1 collective-permute-start.13
  50.4 0.7 collective-permute-start.11
  51.1 1.2 collective-permute-start.16
  52.2 0.6 collective-permute-start.17
  52.8 0.9 collective-permute-done.12.refs_0_
  53.7 3.9 %collective-permute-start.14 = (bf16[512,128]{1,0:T(8,128)(2,1)}, bf16[512,128]{1,0:T(8,128)(2,1)S(1)}, u32[]{:S(2)}, u32[]{:S(2)}) collective-permute-start(bf16[512,128]{1,0:T(8,128)(2,1)} %get-tuple-element.52), channel_id=1, source_target_pairs={{0,48},{8,56},{16,0},{24,8},{32,16},{40,24},{48,32},{56,40},{1,49}... | collective-permute-start | bytes 393224 | tf_op jit(solution)/shard_map/ppermute | solution.py:379
  57.6 0.0 collective-permute-done.13.refs_1_
  57.6 5.6 %collective-permute-done.14.refs_2_ = bf16[512,128]{1,0:T(8,128)(2,1)S(1)} collective-permute-done((bf16[512,128]{1,0:T(8,128)(2,1)}, bf16[512,128]{1,0:T(8,128)(2,1)S(1)}, u32[]{:S(2)}, u32[]{:S(2)}) %collective-permute-start.14) | collective-permute-done | bytes 131104 | tf_op jit(solution)/shard_map/ppermute | solution.py:379
  63.2 2.1 %collective-permute-start.18 = (bf16[512,128]{1,0:T(8,128)(2,1)}, bf16[512,128]{1,0:T(8,128)(2,1)S(1)}, u32[]{:S(2)}, u32[]{:S(2)}) collective-permute-start(bf16[512,128]{1,0:T(8,128)(2,1)} %get-tuple-element.62), channel_id=1, source_target_pairs={{0,40},{8,48},{16,56},{24,0},{32,8},{40,16},{48,24},{56,32},{1,41}... | collective-permute-start | bytes 393224 | tf_op jit(solution)/shard_map/ppermute | solution.py:379
  65.3 1.7 %collective-permute-done.15.refs_3_ = bf16[512,128]{1,0:T(8,128)(2,1)S(1)} collective-permute-done((bf16[512,128]{1,0:T(8,128)(2,1)}, bf16[512,128]{1,0:T(8,128)(2,1)S(1)}, u32[]{:S(2)}, u32[]{:S(2)}) %collective-permute-start.15) | collective-permute-done | bytes 131104 | tf_op jit(solution)/shard_map/ppermute | solution.py:379
  67.0 1.9 %collective-permute-start.19 = (bf16[512,128]{1,0:T(8,128)(2,1)}, bf16[512,128]{1,0:T(8,128)(2,1)S(1)}, u32[]{:S(2)}, u32[]{:S(2)}) collective-permute-start(bf16[512,128]{1,0:T(8,128)(2,1)} %get-tuple-element.63), channel_id=1, source_target_pairs={{0,24},{8,32},{16,40},{24,48},{32,56},{40,0},{48,8},{56,16},{1,25}... | collective-permute-start | bytes 393224 | tf_op jit(solution)/shard_map/ppermute | solution.py:379
  68.9 2.9 %collective-permute-start.20 = (bf16[512,128]{1,0:T(8,128)(2,1)}, bf16[512,128]{1,0:T(8,128)(2,1)S(1)}, u32[]{:S(2)}, u32[]{:S(2)}) collective-permute-start(bf16[512,128]{1,0:T(8,128)(2,1)} %get-tuple-element.64), channel_id=1, source_target_pairs={{0,32},{8,40},{16,48},{24,56},{32,0},{40,8},{48,16},{56,24},{1,33}... | collective-permute-start | bytes 393224 | tf_op jit(solution)/shard_map/ppermute | solution.py:379
  71.8 1.6 %q_proj.1.q = bf16[4,512,128]{2,1,0:T(8,128)(2,1)S(1)} custom-call(s32[5]{0:T(128)S(1)} %copy-done.2, bf16[512,2048]{1,0:T(8,128)(2,1)S(1)} %copy-done, bf16[512,256]{1,0:T(8,128)(2,1)S(1)} %get-tuple-element.49.w0, bf16[512,256]{1,0:T(8,128)(2,1)S(1)} %collective-permute-done.11.w1, bf16[512,256]{1,0:T(8,128)(2,1)S(1)} %collective-permute-done.16.w2, ...), custom_call_target="tpu_custom_call" | custom-call | flops 1000000000 | bytes 3936276 | tf_op jit(solution)/shard_map/q_proj/pallas_call | solution.py:323
  73.5 10.1 %attention_near.1.state = f32[4,512,128]{2,1,0:T(8,128)S(1)} custom-call(s32[5]{0:T(128)S(1)} %copy-done.2, f32[8]{0:T(128)S(1)} %copy-done.4, bf16[4,512,128]{2,1,0:T(8,128)(2,1)S(1)} %q_proj.1.q, bf16[512,128]{1,0:T(8,128)(2,1)S(1)} %copy-done.6, bf16[512,128]{1,0:T(8,128)(2,1)S(1)} %copy-done.5, bf16[512,128]{1,0:T(8,128)(2,1)S(1)} %collective-permute-done.12.refs_0_, ...), custom_call_target="tpu_custom_call" | custom-call | flops 6442450944 | bytes 4194304 | tf_op jit(solution)/shard_map/attention_near/pallas_call | solution.py:394
  83.5 0.9 collective-permute-start.21
  84.4 1.3 %collective-permute-start.22 = (bf16[512,256]{1,0:T(8,128)(2,1)S(1)}, bf16[512,256]{1,0:T(8,128)(2,1)S(1)}, u32[]{:S(2)}, u32[]{:S(2)}) collective-permute-start(bf16[512,256]{1,0:T(8,128)(2,1)S(1)} %get-tuple-element.67.refs_0_), channel_id=1, source_target_pairs={{128,0},{192,64},{0,128},{64,192},{129,1},{193,65},{1,129},{65,193... | collective-permute-start | bytes 786440 | tf_op jit(solution)/shard_map/ppermute | solution.py:290
  85.7 1.3 %collective-permute-start.23 = (bf16[512,256]{1,0:T(8,128)(2,1)S(1)}, bf16[512,256]{1,0:T(8,128)(2,1)S(1)}, u32[]{:S(2)}, u32[]{:S(2)}) collective-permute-start(bf16[512,256]{1,0:T(8,128)(2,1)S(1)} %get-tuple-element.67.refs_0_), channel_id=1, source_target_pairs={{192,0},{0,64},{64,128},{128,192},{193,1},{1,65},{65,129},{129,193... | collective-permute-start | bytes 786440 | tf_op jit(solution)/shard_map/ppermute | solution.py:290
  87.0 7.9 %attention_far.1 = bf16[2,256,256]{2,1,0:T(8,128)(2,1)S(1)} custom-call(s32[5]{0:T(128)S(1)} %copy-done.2, bf16[4,512,128]{2,1,0:T(8,128)(2,1)S(1)} %q_proj.1.q, f32[4,512,128]{2,1,0:T(8,128)S(1)} %attention_near.1.state, bf16[512,128]{1,0:T(8,128)(2,1)S(1)} %collective-permute-done.18.refs_0_, bf16[512,128]{1,0:T(8,128)(2,1)S(1)} %collective-permute-done.19.refs_1_, ...), custom_call_target="tpu_custom_call" | custom-call | flops 3221225472 | bytes 4194304 | tf_op jit(solution)/shard_map/attention_far/pallas_call | solution.py:410
  94.9 1.3 %collective-permute-done.23.refs_3_ = bf16[512,256]{1,0:T(8,128)(2,1)S(1)} collective-permute-done((bf16[512,256]{1,0:T(8,128)(2,1)S(1)}, bf16[512,256]{1,0:T(8,128)(2,1)S(1)}, u32[]{:S(2)}, u32[]{:S(2)}) %collective-permute-start.23) | collective-permute-done | bytes 262176 | tf_op jit(solution)/shard_map/ppermute | solution.py:290
  96.2 0.5 collective-permute-start.26
  96.7 0.0 collective-permute-start.27
  96.7 0.5 collective-permute-start.28
  97.2 0.1 collective-permute-start.24
  97.3 1.7 %collective-permute-done.24.got = bf16[256,256]{1,0:T(8,128)(2,1)S(1)} collective-permute-done((bf16[256,256]{1,0:T(8,128)(2,1)S(1)}, bf16[256,256]{1,0:T(8,128)(2,1)S(1)}, u32[]{:S(2)}, u32[]{:S(2)}) %collective-permute-start.24) | collective-permute-done | bytes 131104 | tf_op jit(solution)/shard_map/ppermute | solution.py:295
  99.1 1.3 %out_proj.1 = (bf16[256,512]{1,0:T(8,128)(2,1)S(1)}, bf16[256,512]{1,0:T(8,128)(2,1)S(1)}, bf16[256,512]{1,0:T(8,128)(2,1)S(1)}, bf16[256,512]{1,0:T(8,128)(2,1)S(1)}) custom-call(s32[5]{0:T(128)S(1)} %copy-done.2, bf16[256,256]{1,0:T(8,128)(2,1)S(1)} %get-tuple-element.78.keep, bf16[256,256]{1,0:T(8,128)(2,1)S(1)} %collective-permute-done.24.got, ...), custom_call_target="tpu_custom_call" | custom-call | flops 1000000000 | bytes 3407892 | tf_op jit(solution)/shard_map/out_proj/pallas_call | solution.py:323
  100.4 1.4 %collective-permute-start.29 = (bf16[256,512]{1,0:T(8,128)(2,1)S(1)}, bf16[256,512]{1,0:T(8,128)(2,1)S(1)}, u32[]{:S(2)}, u32[]{:S(2)}) collective-permute-start(bf16[256,512]{1,0:T(8,128)(2,1)S(1)} %get-tuple-element.72), channel_id=1, source_target_pairs={{0,1},{1,2},{2,3},{3,0},{4,5},{5,6},{6,7},{7,4},{8,9},{9,10},{10,1... | collective-permute-start | bytes 786440 | tf_op jit(solution)/shard_map/ppermute | solution.py:434
  101.8 2.9 %collective-permute-start.30 = (bf16[256,512]{1,0:T(8,128)(2,1)S(1)}, bf16[256,512]{1,0:T(8,128)(2,1)S(1)}, u32[]{:S(2)}, u32[]{:S(2)}) collective-permute-start(bf16[256,512]{1,0:T(8,128)(2,1)S(1)} %get-tuple-element.73), channel_id=1, source_target_pairs={{0,2},{1,3},{2,0},{3,1},{4,6},{5,7},{6,4},{7,5},{8,10},{9,11},{10,... | collective-permute-start | bytes 786440 | tf_op jit(solution)/shard_map/ppermute | solution.py:434
  104.8 1.3 %collective-permute-start.31 = (bf16[256,512]{1,0:T(8,128)(2,1)S(1)}, bf16[256,512]{1,0:T(8,128)(2,1)S(1)}, u32[]{:S(2)}, u32[]{:S(2)}) collective-permute-start(bf16[256,512]{1,0:T(8,128)(2,1)S(1)} %get-tuple-element.74), channel_id=1, source_target_pairs={{0,3},{1,0},{2,1},{3,2},{4,7},{5,4},{6,5},{7,6},{8,11},{9,8},{10,9... | collective-permute-start | bytes 786440 | tf_op jit(solution)/shard_map/ppermute | solution.py:434
  106.1 3.9 %collective-permute-done.29 = bf16[256,512]{1,0:T(8,128)(2,1)S(1)} collective-permute-done((bf16[256,512]{1,0:T(8,128)(2,1)S(1)}, bf16[256,512]{1,0:T(8,128)(2,1)S(1)}, u32[]{:S(2)}, u32[]{:S(2)}) %collective-permute-start.29) | collective-permute-done | bytes 262176 | tf_op jit(solution)/shard_map/ppermute | solution.py:434
  110.0 6.7 %collective-permute-done.30 = bf16[256,512]{1,0:T(8,128)(2,1)S(1)} collective-permute-done((bf16[256,512]{1,0:T(8,128)(2,1)S(1)}, bf16[256,512]{1,0:T(8,128)(2,1)S(1)}, u32[]{:S(2)}, u32[]{:S(2)}) %collective-permute-start.30) | collective-permute-done | bytes 262176 | tf_op jit(solution)/shard_map/ppermute | solution.py:434
  116.7 0.8 fusion
  (57 shorter events, 0.2 us)
Async XLA Ops:
  1.3 10.6 %copy-start.7 = (bf16[1,256,512]{2,1,0:T(8,128)(2,1)S(1)}, bf16[1,256,512]{2,1,0:T(8,128)(2,1)}, u32[]{:S(2)}) copy-start(bf16[1,256,512]{2,1,0:T(8,128)(2,1)} %param.12) | copy-start | bytes 786436
  1.3 34.5 %copy-start.16 = (bf16[2048]{0:T(1024)(128)(2,1)S(1)}, bf16[2048]{0:T(1024)(128)(2,1)}, u32[]{:S(2)}) copy-start(bf16[2048]{0:T(1024)(128)(2,1)} %param.14) | copy-start | bytes 12292
  3.4 26.9 %all-to-all-start = ((bf16[16,32,640]{2,1,0:T(8,128)(2,1)}), bf16[16,32,640]{2,1,0:T(8,128)(2,1)S(1)}, u32[]{:S(2)}, u32[]{:S(2)}) async-start(bf16[16,32,640]{2,1,0:T(8,128)(2,1)} %get-tuple-element.40), calls=%async_computation | async-start | bytes 1310720 | tf_op jit(solution)/shard_map/all_to_all | solution.py:349
  11.9 14.6 %collective-permute-start = (bf16[256,512]{1,0:T(8,128)(2,1)S(1)}, bf16[256,512]{1,0:T(8,128)(2,1)S(1)}, u32[]{:S(2)}, u32[]{:S(2)}) collective-permute-start(bf16[256,512]{1,0:T(8,128)(2,1)S(1)} %bitcast.17), channel_id=1, source_target_pairs={{1,0},{2,1},{3,2},{0,3},{5,4},{6,5},{7,6},{4,7},{9,8},{10,9},{11,1... | collective-permute-start | bytes 786440 | tf_op jit(solution)/shard_map/ppermute | solution.py:290
  15.0 11.5 %collective-permute-start.1 = (bf16[256,512]{1,0:T(8,128)(2,1)S(1)}, bf16[256,512]{1,0:T(8,128)(2,1)S(1)}, u32[]{:S(2)}, u32[]{:S(2)}) collective-permute-start(bf16[256,512]{1,0:T(8,128)(2,1)S(1)} %bitcast.18), channel_id=1, source_target_pairs={{2,0},{3,1},{0,2},{1,3},{6,4},{7,5},{4,6},{5,7},{10,8},{11,9},{8,1... | collective-permute-start | bytes 786440 | tf_op jit(solution)/shard_map/ppermute | solution.py:290
  15.7 14.6 %collective-permute-start.2 = (bf16[256,512]{1,0:T(8,128)(2,1)S(1)}, bf16[256,512]{1,0:T(8,128)(2,1)S(1)}, u32[]{:S(2)}, u32[]{:S(2)}) collective-permute-start(bf16[256,512]{1,0:T(8,128)(2,1)S(1)} %bitcast.19), channel_id=1, source_target_pairs={{3,0},{0,1},{1,2},{2,3},{7,4},{4,5},{5,6},{6,7},{11,8},{8,9},{9,10... | collective-permute-start | bytes 786440 | tf_op jit(solution)/shard_map/ppermute | solution.py:290
  26.5 9.9 %copy-start.8 = (bf16[256,512]{1,0:T(8,128)(2,1)}, bf16[256,512]{1,0:T(8,128)(2,1)S(1)}, u32[]{:S(2)}) copy-start(bf16[256,512]{1,0:T(8,128)(2,1)S(1)} %collective-permute-done.refs_1_) | copy-start | bytes 786436
  26.5 9.9 %copy-start.9 = (bf16[256,512]{1,0:T(8,128)(2,1)}, bf16[256,512]{1,0:T(8,128)(2,1)S(1)}, u32[]{:S(2)}) copy-start(bf16[256,512]{1,0:T(8,128)(2,1)S(1)} %collective-permute-done.1.refs_2_) | copy-start | bytes 786436
  30.2 6.2 %copy-start.10 = (bf16[256,512]{1,0:T(8,128)(2,1)}, bf16[256,512]{1,0:T(8,128)(2,1)S(1)}, u32[]{:S(2)}) copy-start(bf16[256,512]{1,0:T(8,128)(2,1)S(1)} %collective-permute-done.2.refs_3_) | copy-start | bytes 786436
  30.2 3.9 %collective-permute-start.3 = (bf16[256,512]{1,0:T(8,128)(2,1)S(1)}, bf16[256,512]{1,0:T(8,128)(2,1)S(1)}, u32[]{:S(2)}, u32[]{:S(2)}) collective-permute-start(bf16[256,512]{1,0:T(8,128)(2,1)S(1)} %bitcast.20), channel_id=1, source_target_pairs={{0,4},{4,0},{1,5},{5,1},{2,6},{6,2},{3,7},{7,3},{8,12},{12,8},{9,1... | collective-permute-start | bytes 786440 | tf_op jit(solution)/shard_map/ppermute | solution.py:295
  30.3 4.7 %collective-permute-start.4 = (bf16[256,512]{1,0:T(8,128)(2,1)S(1)}, bf16[256,512]{1,0:T(8,128)(2,1)S(1)}, u32[]{:S(2)}, u32[]{:S(2)}) collective-permute-start(bf16[256,512]{1,0:T(8,128)(2,1)S(1)} %collective-permute-done.refs_1_), channel_id=1, source_target_pairs={{0,4},{4,0},{1,5},{5,1},{2,6},{6,2},{3,7},{7,3},{8,12},{12,8},{9,1... | collective-permute-start | bytes 786440 | tf_op jit(solution)/shard_map/ppermute | solution.py:295
  30.8 5.7 %collective-permute-start.5 = (bf16[256,512]{1,0:T(8,128)(2,1)S(1)}, bf16[256,512]{1,0:T(8,128)(2,1)S(1)}, u32[]{:S(2)}, u32[]{:S(2)}) collective-permute-start(bf16[256,512]{1,0:T(8,128)(2,1)S(1)} %collective-permute-done.1.refs_2_), channel_id=1, source_target_pairs={{0,4},{4,0},{1,5},{5,1},{2,6},{6,2},{3,7},{7,3},{8,12},{12,8},{9,1... | collective-permute-start | bytes 786440 | tf_op jit(solution)/shard_map/ppermute | solution.py:295
  30.8 5.6 %collective-permute-start.6 = (bf16[256,512]{1,0:T(8,128)(2,1)S(1)}, bf16[256,512]{1,0:T(8,128)(2,1)S(1)}, u32[]{:S(2)}, u32[]{:S(2)}) collective-permute-start(bf16[256,512]{1,0:T(8,128)(2,1)S(1)} %collective-permute-done.2.refs_3_), channel_id=1, source_target_pairs={{0,4},{4,0},{1,5},{5,1},{2,6},{6,2},{3,7},{7,3},{8,12},{12,8},{9,1... | collective-permute-start | bytes 786440 | tf_op jit(solution)/shard_map/ppermute | solution.py:295
  31.3 12.4 %copy-start.15 = (bf16[512,128]{1,0:T(8,128)(2,1)}, bf16[512,128]{1,0:T(8,128)(2,1)S(1)}, u32[]{:S(2)}) copy-start(bf16[512,128]{1,0:T(8,128)(2,1)S(1)} %slice.16.w0) | copy-start | bytes 393220
  31.3 10.4 %collective-permute-start.7 = (bf16[512,128]{1,0:T(8,128)(2,1)S(1)}, bf16[512,128]{1,0:T(8,128)(2,1)S(1)}, u32[]{:S(2)}, u32[]{:S(2)}) collective-permute-start(bf16[512,128]{1,0:T(8,128)(2,1)S(1)} %slice.16.w0), channel_id=1, source_target_pairs={{64,0},{128,64},{192,128},{0,192},{65,1},{129,65},{193,129},{1,193... | collective-permute-start | bytes 393224 | tf_op jit(solution)/shard_map/ppermute | solution.py:290
  34.1 2.4 %copy-start.11 = (bf16[256,512]{1,0:T(8,128)(2,1)}, bf16[256,512]{1,0:T(8,128)(2,1)S(1)}, u32[]{:S(2)}) copy-start(bf16[256,512]{1,0:T(8,128)(2,1)S(1)} %collective-permute-done.3.refs_4_) | copy-start | bytes 786436
  34.1 7.9 %collective-permute-start.8 = (bf16[512,128]{1,0:T(8,128)(2,1)S(1)}, bf16[512,128]{1,0:T(8,128)(2,1)S(1)}, u32[]{:S(2)}, u32[]{:S(2)}) collective-permute-start(bf16[512,128]{1,0:T(8,128)(2,1)S(1)} %slice.16.w0), channel_id=1, source_target_pairs={{128,0},{192,64},{0,128},{64,192},{129,1},{193,65},{1,129},{65,193... | collective-permute-start | bytes 393224 | tf_op jit(solution)/shard_map/ppermute | solution.py:290
  34.9 1.6 %copy-start.12 = (bf16[256,512]{1,0:T(8,128)(2,1)}, bf16[256,512]{1,0:T(8,128)(2,1)S(1)}, u32[]{:S(2)}) copy-start(bf16[256,512]{1,0:T(8,128)(2,1)S(1)} %collective-permute-done.4.refs_5_) | copy-start | bytes 786436
  34.9 8.7 %collective-permute-start.9 = (bf16[512,128]{1,0:T(8,128)(2,1)S(1)}, bf16[512,128]{1,0:T(8,128)(2,1)S(1)}, u32[]{:S(2)}, u32[]{:S(2)}) collective-permute-start(bf16[512,128]{1,0:T(8,128)(2,1)S(1)} %slice.16.w0), channel_id=1, source_target_pairs={{192,0},{0,64},{64,128},{128,192},{193,1},{1,65},{65,129},{129,193... | collective-permute-start | bytes 393224 | tf_op jit(solution)/shard_map/ppermute | solution.py:290
  36.4 0.7 copy-start.13
  36.4 5.2 %collective-permute-start.10 = (bf16[256,128]{1,0:T(8,128)(2,1)}, bf16[256,128]{1,0:T(8,128)(2,1)S(1)}, u32[]{:S(2)}, u32[]{:S(2)}) collective-permute-start(bf16[256,128]{1,0:T(8,128)(2,1)} %get-tuple-element.47), channel_id=1, source_target_pairs={{0,4},{4,0},{1,5},{5,1},{2,6},{6,2},{3,7},{7,3},{8,12},{12,8},{9,1... | collective-permute-start | bytes 196616 | tf_op jit(solution)/shard_map/ppermute | solution.py:295
  37.1 0.7 copy-start.14
  41.6 2.0 %copy-start.20 = (bf16[256,128]{1,0:T(8,128)(2,1)}, bf16[256,128]{1,0:T(8,128)(2,1)S(1)}, u32[]{:S(2)}) copy-start(bf16[256,128]{1,0:T(8,128)(2,1)S(1)} %collective-permute-done.10.p_got) | copy-start | bytes 196612
  41.6 2.0 %copy-start.17 = (bf16[512,128]{1,0:T(8,128)(2,1)}, bf16[512,128]{1,0:T(8,128)(2,1)S(1)}, u32[]{:S(2)}) copy-start(bf16[512,128]{1,0:T(8,128)(2,1)S(1)} %collective-permute-done.7.w1) | copy-start | bytes 393220
  42.0 1.6 %copy-start.18 = (bf16[512,128]{1,0:T(8,128)(2,1)}, bf16[512,128]{1,0:T(8,128)(2,1)S(1)}, u32[]{:S(2)}) copy-start(bf16[512,128]{1,0:T(8,128)(2,1)S(1)} %collective-permute-done.8.w2) | copy-start | bytes 393220
  43.7 0.7 copy-start.19
  44.3 27.5 %copy-start = (bf16[512,2048]{1,0:T(8,128)(2,1)S(1)}, bf16[512,2048]{1,0:T(8,128)(2,1)}, u32[]{:S(2)}) copy-start(bf16[512,2048]{1,0:T(8,128)(2,1)} %norm.1.normed) | copy-start | bytes 6291460
  44.3 27.5 %copy-start.1 = (f32[512,128]{1,0:T(8,128)S(1)}, f32[512,128]{1,0:T(8,128)}, u32[]{:S(2)}) copy-start(f32[512,128]{1,0:T(8,128)} %constant.22.clone.fine) | copy-start | bytes 786436
  44.3 27.5 %copy-start.2 = (s32[5]{0:T(128)S(1)}, s32[5]{0:T(128)}, u32[]{:S(2)}) copy-start(s32[5]{0:T(128)} %stack.19.ids) | copy-start | bytes 64
  44.3 27.5 %copy-start.3 = (f32[8,128]{1,0:T(8,128)S(1)}, f32[8,128]{1,0:T(8,128)}, u32[]{:S(2)}) copy-start(f32[8,128]{1,0:T(8,128)} %constant.21.clone.coarse) | copy-start | bytes 12292
  48.0 5.7 %collective-permute-start.12 = (bf16[512,128]{1,0:T(8,128)(2,1)}, bf16[512,128]{1,0:T(8,128)(2,1)S(1)}, u32[]{:S(2)}, u32[]{:S(2)}) collective-permute-start(bf16[512,128]{1,0:T(8,128)(2,1)} %get-tuple-element.50), channel_id=1, source_target_pairs={{0,56},{8,0},{16,8},{24,16},{32,24},{40,32},{48,40},{56,48},{1,57}... | collective-permute-start | bytes 393224 | tf_op jit(solution)/shard_map/ppermute | solution.py:379
  50.3 23.2 %copy-start.4 = (f32[8]{0:T(128)S(1)}, f32[8]{0:T(128)}, u32[]{:S(2)}) copy-start(f32[8]{0:T(128)} %sinks.1) | copy-start | bytes 100
  50.3 23.2 %copy-start.5 = (bf16[512,128]{1,0:T(8,128)(2,1)S(1)}, bf16[512,128]{1,0:T(8,128)(2,1)}, u32[]{:S(2)}) copy-start(bf16[512,128]{1,0:T(8,128)(2,1)} %get-tuple-element.56.own_new) | copy-start | bytes 393220
  50.3 23.2 %copy-start.6 = (bf16[512,128]{1,0:T(8,128)(2,1)S(1)}, bf16[512,128]{1,0:T(8,128)(2,1)}, u32[]{:S(2)}) copy-start(bf16[512,128]{1,0:T(8,128)(2,1)} %get-tuple-element.55.own_prefix) | copy-start | bytes 393220
  50.3 7.3 %collective-permute-start.13 = (bf16[512,128]{1,0:T(8,128)(2,1)}, bf16[512,128]{1,0:T(8,128)(2,1)S(1)}, u32[]{:S(2)}, u32[]{:S(2)}) collective-permute-start(bf16[512,128]{1,0:T(8,128)(2,1)} %get-tuple-element.51), channel_id=1, source_target_pairs={{0,8},{8,16},{16,24},{24,32},{32,40},{40,48},{48,56},{56,0},{1,9},... | collective-permute-start | bytes 393224 | tf_op jit(solution)/shard_map/ppermute | solution.py:379
  50.4 18.5 %collective-permute-start.11 = (bf16[512,256]{1,0:T(8,128)(2,1)S(1)}, bf16[512,256]{1,0:T(8,128)(2,1)S(1)}, u32[]{:S(2)}, u32[]{:S(2)}) collective-permute-start(bf16[512,256]{1,0:T(8,128)(2,1)S(1)} %get-tuple-element.49.w0), channel_id=1, source_target_pairs={{64,0},{128,64},{192,128},{0,192},{65,1},{129,65},{193,129},{1,193... | collective-permute-start | bytes 786440 | tf_op jit(solution)/shard_map/ppermute | solution.py:290
  51.1 20.7 %collective-permute-start.16 = (bf16[512,256]{1,0:T(8,128)(2,1)S(1)}, bf16[512,256]{1,0:T(8,128)(2,1)S(1)}, u32[]{:S(2)}, u32[]{:S(2)}) collective-permute-start(bf16[512,256]{1,0:T(8,128)(2,1)S(1)} %get-tuple-element.49.w0), channel_id=1, source_target_pairs={{128,0},{192,64},{0,128},{64,192},{129,1},{193,65},{1,129},{65,193... | collective-permute-start | bytes 786440 | tf_op jit(solution)/shard_map/ppermute | solution.py:290
  52.2 19.6 %collective-permute-start.17 = (bf16[512,256]{1,0:T(8,128)(2,1)S(1)}, bf16[512,256]{1,0:T(8,128)(2,1)S(1)}, u32[]{:S(2)}, u32[]{:S(2)}) collective-permute-start(bf16[512,256]{1,0:T(8,128)(2,1)S(1)} %get-tuple-element.49.w0), channel_id=1, source_target_pairs={{192,0},{0,64},{64,128},{128,192},{193,1},{1,65},{65,129},{129,193... | collective-permute-start | bytes 786440 | tf_op jit(solution)/shard_map/ppermute | solution.py:290
  53.7 9.5 %collective-permute-start.14 = (bf16[512,128]{1,0:T(8,128)(2,1)}, bf16[512,128]{1,0:T(8,128)(2,1)S(1)}, u32[]{:S(2)}, u32[]{:S(2)}) collective-permute-start(bf16[512,128]{1,0:T(8,128)(2,1)} %get-tuple-element.52), channel_id=1, source_target_pairs={{0,48},{8,56},{16,0},{24,8},{32,16},{40,24},{48,32},{56,40},{1,49}... | collective-permute-start | bytes 393224 | tf_op jit(solution)/shard_map/ppermute | solution.py:379
  57.6 9.4 %collective-permute-start.15 = (bf16[512,128]{1,0:T(8,128)(2,1)}, bf16[512,128]{1,0:T(8,128)(2,1)S(1)}, u32[]{:S(2)}, u32[]{:S(2)}) collective-permute-start(bf16[512,128]{1,0:T(8,128)(2,1)} %get-tuple-element.53), channel_id=1, source_target_pairs={{0,16},{8,24},{16,32},{24,40},{32,48},{40,56},{48,0},{56,8},{1,17}... | collective-permute-start | bytes 393224 | tf_op jit(solution)/shard_map/ppermute | solution.py:379
  63.2 22.5 %collective-permute-start.18 = (bf16[512,128]{1,0:T(8,128)(2,1)}, bf16[512,128]{1,0:T(8,128)(2,1)S(1)}, u32[]{:S(2)}, u32[]{:S(2)}) collective-permute-start(bf16[512,128]{1,0:T(8,128)(2,1)} %get-tuple-element.62), channel_id=1, source_target_pairs={{0,40},{8,48},{16,56},{24,0},{32,8},{40,16},{48,24},{56,32},{1,41}... | collective-permute-start | bytes 393224 | tf_op jit(solution)/shard_map/ppermute | solution.py:379
  67.0 20.0 %collective-permute-start.19 = (bf16[512,128]{1,0:T(8,128)(2,1)}, bf16[512,128]{1,0:T(8,128)(2,1)S(1)}, u32[]{:S(2)}, u32[]{:S(2)}) collective-permute-start(bf16[512,128]{1,0:T(8,128)(2,1)} %get-tuple-element.63), channel_id=1, source_target_pairs={{0,24},{8,32},{16,40},{24,48},{32,56},{40,0},{48,8},{56,16},{1,25}... | collective-permute-start | bytes 393224 | tf_op jit(solution)/shard_map/ppermute | solution.py:379
  68.9 18.1 %collective-permute-start.20 = (bf16[512,128]{1,0:T(8,128)(2,1)}, bf16[512,128]{1,0:T(8,128)(2,1)S(1)}, u32[]{:S(2)}, u32[]{:S(2)}) collective-permute-start(bf16[512,128]{1,0:T(8,128)(2,1)} %get-tuple-element.64), channel_id=1, source_target_pairs={{0,32},{8,40},{16,48},{24,56},{32,0},{40,8},{48,16},{56,24},{1,33}... | collective-permute-start | bytes 393224 | tf_op jit(solution)/shard_map/ppermute | solution.py:379
  83.5 11.4 %collective-permute-start.21 = (bf16[512,256]{1,0:T(8,128)(2,1)S(1)}, bf16[512,256]{1,0:T(8,128)(2,1)S(1)}, u32[]{:S(2)}, u32[]{:S(2)}) collective-permute-start(bf16[512,256]{1,0:T(8,128)(2,1)S(1)} %get-tuple-element.67.refs_0_), channel_id=1, source_target_pairs={{64,0},{128,64},{192,128},{0,192},{65,1},{129,65},{193,129},{1,193... | collective-permute-start | bytes 786440 | tf_op jit(solution)/shard_map/ppermute | solution.py:290
  84.4 10.5 %collective-permute-start.22 = (bf16[512,256]{1,0:T(8,128)(2,1)S(1)}, bf16[512,256]{1,0:T(8,128)(2,1)S(1)}, u32[]{:S(2)}, u32[]{:S(2)}) collective-permute-start(bf16[512,256]{1,0:T(8,128)(2,1)S(1)} %get-tuple-element.67.refs_0_), channel_id=1, source_target_pairs={{128,0},{192,64},{0,128},{64,192},{129,1},{193,65},{1,129},{65,193... | collective-permute-start | bytes 786440 | tf_op jit(solution)/shard_map/ppermute | solution.py:290
  85.7 10.5 %collective-permute-start.23 = (bf16[512,256]{1,0:T(8,128)(2,1)S(1)}, bf16[512,256]{1,0:T(8,128)(2,1)S(1)}, u32[]{:S(2)}, u32[]{:S(2)}) collective-permute-start(bf16[512,256]{1,0:T(8,128)(2,1)S(1)} %get-tuple-element.67.refs_0_), channel_id=1, source_target_pairs={{192,0},{0,64},{64,128},{128,192},{193,1},{1,65},{65,129},{129,193... | collective-permute-start | bytes 786440 | tf_op jit(solution)/shard_map/ppermute | solution.py:290
  96.2 2.9 %collective-permute-start.25 = (bf16[512,256]{1,0:T(8,128)(2,1)S(1)}, bf16[512,256]{1,0:T(8,128)(2,1)S(1)}, u32[]{:S(2)}, u32[]{:S(2)}) collective-permute-start(bf16[512,256]{1,0:T(8,128)(2,1)S(1)} %get-tuple-element.67.refs_0_), channel_id=1, source_target_pairs={{0,4},{4,0},{1,5},{5,1},{2,6},{6,2},{3,7},{7,3},{8,12},{12,8},{9,1... | collective-permute-start | bytes 786440 | tf_op jit(solution)/shard_map/ppermute | solution.py:295
  96.2 2.9 %collective-permute-start.26 = (bf16[512,256]{1,0:T(8,128)(2,1)S(1)}, bf16[512,256]{1,0:T(8,128)(2,1)S(1)}, u32[]{:S(2)}, u32[]{:S(2)}) collective-permute-start(bf16[512,256]{1,0:T(8,128)(2,1)S(1)} %collective-permute-done.21.refs_1_), channel_id=1, source_target_pairs={{0,4},{4,0},{1,5},{5,1},{2,6},{6,2},{3,7},{7,3},{8,12},{12,8},{9,1... | collective-permute-start | bytes 786440 | tf_op jit(solution)/shard_map/ppermute | solution.py:295
  96.7 2.3 %collective-permute-start.27 = (bf16[512,256]{1,0:T(8,128)(2,1)S(1)}, bf16[512,256]{1,0:T(8,128)(2,1)S(1)}, u32[]{:S(2)}, u32[]{:S(2)}) collective-permute-start(bf16[512,256]{1,0:T(8,128)(2,1)S(1)} %collective-permute-done.22.refs_2_), channel_id=1, source_target_pairs={{0,4},{4,0},{1,5},{5,1},{2,6},{6,2},{3,7},{7,3},{8,12},{12,8},{9,1... | collective-permute-start | bytes 786440 | tf_op jit(solution)/shard_map/ppermute | solution.py:295
  96.7 2.3 %collective-permute-start.28 = (bf16[512,256]{1,0:T(8,128)(2,1)S(1)}, bf16[512,256]{1,0:T(8,128)(2,1)S(1)}, u32[]{:S(2)}, u32[]{:S(2)}) collective-permute-start(bf16[512,256]{1,0:T(8,128)(2,1)S(1)} %collective-permute-done.23.refs_3_), channel_id=1, source_target_pairs={{0,4},{4,0},{1,5},{5,1},{2,6},{6,2},{3,7},{7,3},{8,12},{12,8},{9,1... | collective-permute-start | bytes 786440 | tf_op jit(solution)/shard_map/ppermute | solution.py:295
  97.2 1.8 %collective-permute-start.24 = (bf16[256,256]{1,0:T(8,128)(2,1)S(1)}, bf16[256,256]{1,0:T(8,128)(2,1)S(1)}, u32[]{:S(2)}, u32[]{:S(2)}) collective-permute-start(bf16[256,256]{1,0:T(8,128)(2,1)S(1)} %get-tuple-element.77), channel_id=1, source_target_pairs={{0,4},{4,0},{1,5},{5,1},{2,6},{6,2},{3,7},{7,3},{8,12},{12,8},{9,1... | collective-permute-start | bytes 393224 | tf_op jit(solution)/shard_map/ppermute | solution.py:295
  100.4 9.6 %collective-permute-start.29 = (bf16[256,512]{1,0:T(8,128)(2,1)S(1)}, bf16[256,512]{1,0:T(8,128)(2,1)S(1)}, u32[]{:S(2)}, u32[]{:S(2)}) collective-permute-start(bf16[256,512]{1,0:T(8,128)(2,1)S(1)} %get-tuple-element.72), channel_id=1, source_target_pairs={{0,1},{1,2},{2,3},{3,0},{4,5},{5,6},{6,7},{7,4},{8,9},{9,10},{10,1... | collective-permute-start | bytes 786440 | tf_op jit(solution)/shard_map/ppermute | solution.py:434
  101.8 14.9 %collective-permute-start.30 = (bf16[256,512]{1,0:T(8,128)(2,1)S(1)}, bf16[256,512]{1,0:T(8,128)(2,1)S(1)}, u32[]{:S(2)}, u32[]{:S(2)}) collective-permute-start(bf16[256,512]{1,0:T(8,128)(2,1)S(1)} %get-tuple-element.73), channel_id=1, source_target_pairs={{0,2},{1,3},{2,0},{3,1},{4,6},{5,7},{6,4},{7,5},{8,10},{9,11},{10,... | collective-permute-start | bytes 786440 | tf_op jit(solution)/shard_map/ppermute | solution.py:434
  104.8 11.9 %collective-permute-start.31 = (bf16[256,512]{1,0:T(8,128)(2,1)S(1)}, bf16[256,512]{1,0:T(8,128)(2,1)S(1)}, u32[]{:S(2)}, u32[]{:S(2)}) collective-permute-start(bf16[256,512]{1,0:T(8,128)(2,1)S(1)} %get-tuple-element.74), channel_id=1, source_target_pairs={{0,3},{1,0},{2,1},{3,2},{4,7},{5,4},{6,5},{7,6},{8,11},{9,8},{10,9... | collective-permute-start | bytes 786440 | tf_op jit(solution)/shard_map/ppermute | solution.py:434

commit v5 on v4

--- a/solution.py
+++ b/solution.py
@@ -20,7 +20,7 @@
 VMEM_ALL = 63_400_000
 
 AWAY = (1, 7, 2, 6, 3, 5, 4)
-NEAR = 4
+NEAR = 3
 
 NT = (((1,), (1,)), ((), ()))
 

time: 119 us -> 117 us (0.983)
  waiting for transfers between devices: 37.4 us -> 34.4 us
  starting transfers between devices: 44.6 us -> 47 us
    ppermute x7, starting transfers between devices: 13 us -> 15.8 us  [on_device(): lax.ppermute(x, 'z', [(i, (i + zsize - k) % zsize) for i in range(zsize)])]
    ppermute x7, waiting for transfers between devices: 8.18 us -> 5.73 us  [on_device(): lax.ppermute(x, 'z', [(i, (i + zsize - k) % zsize) for i in range(zsize)])]
    pallas_call x1, Pallas kernels: 10.1 us -> 8.67 us  [on_device(): pl.pallas_call(first_kernel, out_shape=jax.ShapeDtypeStruct((4, chip_rows...]
    pallas_call x1, Pallas kernels: 7.88 us -> 9.19 us  [on_device(): pl.pallas_call(second_kernel, out_shape=jax.ShapeDtypeStruct((2, tok_rows...]
  transfers between devices with their start and end apart: 33 -> 33, of which waited for: 11 -> 10; matrix products, arithmetic and copies ran while one was open for 1% -> 1% of each run, Pallas kernels for 20% -> 20%
where the time goes in v5:
time: 117 us; the launch traced here: 116 us
  starting transfers between devices  47 us (40%)
  waiting for transfers between devices  34.4 us (29%)
  Pallas kernels  30.2 us (26%)
  local copies, waits for them, and re-layouts  2.58 us (2%)
    ppermute x12, waiting for transfers between devices, around(): lax.ppermute(x, axis, [((i + k) % size, i) for i in range(size)])  16.4 us
    ppermute x7, starting transfers between devices, on_device(): lax.ppermute(x, 'z', [(i, (i + zsize - k) % zsize) for i in range(zsize)])  15.8 us
    ppermute x12, starting transfers between devices, around(): lax.ppermute(x, axis, [((i + k) % size, i) for i in range(size)])  14.7 us
    ppermute x3, waiting for transfers between devices, on_device(): lax.ppermute(parts[k], 'mdl', [(i, (i + k) % 4) for i in range(4)])  10.6 us
    pallas_call x1, Pallas kernels, on_device(): pl.pallas_call(second_kernel, out_shape=jax.ShapeDtypeStruct((2, tok_rows...  9.19 us
    pallas_call x4, Pallas kernels, call(): pl.pallas_call(body, out_shape=outs, grid=(1,), in_specs=[sspec()] * scal...  8.77 us
    all_to_all x1, starting transfers between devices, on_device(): lax.all_to_all(fan, ('z', 'core'), 0, 0, tiled=True).reshape(depth, 10 * HD)  8.72 us
    pallas_call x1, Pallas kernels, on_device(): pl.pallas_call(first_kernel, out_shape=jax.ShapeDtypeStruct((4, chip_rows...  8.67 us
  transfers between devices with their start and end apart: 33, of which 10 were waited for; matrix products, arithmetic and copies ran while one was open for 1% of the time, Pallas kernels for 20%

profile of v5, /device:TPU:32, one launch (start us, length us, event | category | flops | bytes accessed | tf_op | source)
XLA Modules:
  0.0 115.9 jit_solution(11245168455554899087)
XLA Ops:
  0.7 0.6 stack.19.ids
  1.3 2.0 %split.1 = (bf16[16,32,640]{2,1,0:T(8,128)(2,1)}, bf16[256,128]{1,0:T(8,128)(2,1)}, bf16[256,128]{1,0:T(8,128)(2,1)}) custom-call(s32[5]{0:T(128)} %stack.19.ids, bf16[32,512]{1,0:T(8,128)(2,1)} %wq.1, bf16[32,128]{1,0:T(8,128)(2,1)} %wk.1, bf16[32,128]{1,0:T(8,128)(2,1)} %wv.1, bf16[32,512]{1,0:T(8,128)(2,1)} %wo.1, bf16[256,128]{1,0:T(8,128)(2,1)} %bitcast.21, ...), custom_call_target="tpu_custom_call" | custom-call | flops 1000000000 | bytes 999444 | tf_op jit(solution)/shard_map/split/pallas_call | solution.py:323
  3.3 8.7 %all-to-all-start = ((bf16[16,32,640]{2,1,0:T(8,128)(2,1)}), bf16[16,32,640]{2,1,0:T(8,128)(2,1)S(1)}, u32[]{:S(2)}, u32[]{:S(2)}) async-start(bf16[16,32,640]{2,1,0:T(8,128)(2,1)} %get-tuple-element.39), calls=%async_computation | async-start | bytes 1310720 | tf_op jit(solution)/shard_map/all_to_all | solution.py:349
  12.0 3.1 %collective-permute-start = (bf16[256,512]{1,0:T(8,128)(2,1)S(1)}, bf16[256,512]{1,0:T(8,128)(2,1)S(1)}, u32[]{:S(2)}, u32[]{:S(2)}) collective-permute-start(bf16[256,512]{1,0:T(8,128)(2,1)S(1)} %bitcast.17), channel_id=1, source_target_pairs={{1,0},{2,1},{3,2},{0,3},{5,4},{6,5},{7,6},{4,7},{9,8},{10,9},{11,1... | collective-permute-start | bytes 786440 | tf_op jit(solution)/shard_map/ppermute | solution.py:290
  15.1 0.6 collective-permute-start.1
  15.7 1.0 collective-permute-start.2
  16.7 9.9 %collective-permute-done.refs_1_ = bf16[256,512]{1,0:T(8,128)(2,1)S(1)} collective-permute-done((bf16[256,512]{1,0:T(8,128)(2,1)S(1)}, bf16[256,512]{1,0:T(8,128)(2,1)S(1)}, u32[]{:S(2)}, u32[]{:S(2)}) %collective-permute-start) | collective-permute-done | bytes 262176 | tf_op jit(solution)/shard_map/ppermute | solution.py:290
  26.6 0.0 collective-permute-done.1.refs_2_
  26.6 3.7 %collective-permute-done.2.refs_3_ = bf16[256,512]{1,0:T(8,128)(2,1)S(1)} collective-permute-done((bf16[256,512]{1,0:T(8,128)(2,1)S(1)}, bf16[256,512]{1,0:T(8,128)(2,1)S(1)}, u32[]{:S(2)}, u32[]{:S(2)}) %collective-permute-start.2) | collective-permute-done | bytes 262176 | tf_op jit(solution)/shard_map/ppermute | solution.py:290
  30.3 0.0 collective-permute-start.3
  30.3 0.5 collective-permute-start.4
  30.8 0.1 collective-permute-start.5
  30.9 0.4 collective-permute-start.6
  31.3 0.6 reshape.7.refs_8_
  32.0 2.8 %collective-permute-start.7 = (bf16[512,128]{1,0:T(8,128)(2,1)S(1)}, bf16[512,128]{1,0:T(8,128)(2,1)S(1)}, u32[]{:S(2)}, u32[]{:S(2)}) collective-permute-start(bf16[512,128]{1,0:T(8,128)(2,1)S(1)} %slice.16.w0), channel_id=1, source_target_pairs={{64,0},{128,64},{192,128},{0,192},{65,1},{129,65},{193,129},{1,193... | collective-permute-start | bytes 393224 | tf_op jit(solution)/shard_map/ppermute | solution.py:290
  34.8 0.0 collective-permute-done.3.refs_4_
  34.8 0.8 collective-permute-start.8
  35.6 0.0 collective-permute-done.4.refs_5_
  35.6 0.9 collective-permute-start.9
  36.5 0.0 collective-permute-done.5.refs_6_
  36.6 0.1 collective-permute-start.10
  36.7 0.0 collective-permute-done.6.refs_7_
  36.7 0.5 copy-done.13
  37.2 0.7 copy-done.14
  37.9 3.8 %norm.1.normed = bf16[512,2048]{1,0:T(8,128)(2,1)} custom-call(s32[5]{0:T(128)} %stack.19.ids, bf16[256,512]{1,0:T(8,128)(2,1)} %bitcast.16, bf16[256,512]{1,0:T(8,128)(2,1)} %copy-done.8, bf16[256,512]{1,0:T(8,128)(2,1)} %copy-done.9, bf16[256,512]{1,0:T(8,128)(2,1)} %copy-done.10, bf16[256,512]{1,0:T(8,128)(2,1)} %copy-done.11, ...), custom_call_target="tpu_custom_call" | custom-call | flops 1000000000 | bytes 4198420 | tf_op jit(solution)/shard_map/norm/pallas_call | solution.py:323
  41.7 0.0 copy-start.3
  41.8 0.0 copy-start.17
  41.8 1.0 collective-permute-done.8.w2
  42.8 1.6 %collective-permute-done.9.w3 = bf16[512,128]{1,0:T(8,128)(2,1)} collective-permute-done((bf16[512,128]{1,0:T(8,128)(2,1)S(1)}, bf16[512,128]{1,0:T(8,128)(2,1)}, u32[]{:S(2)}, u32[]{:S(2)}) %collective-permute-start.9) | collective-permute-done | bytes 131104 | tf_op jit(solution)/shard_map/ppermute | solution.py:290
  44.5 3.5 %kv_proj.1 = (bf16[512,128]{1,0:T(8,128)(2,1)}, bf16[512,128]{1,0:T(8,128)(2,1)}, bf16[512,128]{1,0:T(8,128)(2,1)}, bf16[512,128]{1,0:T(8,128)(2,1)}, bf16[512,1...) custom-call(s32[5]{0:T(128)} %stack.19.ids, ...), custom_call_target="tpu_custom_call" | custom-call | flops 1000000000 | bytes 4194304 | tf_op jit(solution)/shard_map/kv_proj/pallas_call | solution.py:366
  48.0 0.0 copy-start.4
  48.0 2.2 %collective-permute-start.12 = (bf16[512,128]{1,0:T(8,128)(2,1)}, bf16[512,128]{1,0:T(8,128)(2,1)S(1)}, u32[]{:S(2)}, u32[]{:S(2)}) collective-permute-start(bf16[512,128]{1,0:T(8,128)(2,1)} %get-tuple-element.49), channel_id=1, source_target_pairs={{0,56},{8,0},{16,8},{24,16},{32,24},{40,32},{48,40},{56,48},{1,57}... | collective-permute-start | bytes 393224 | tf_op jit(solution)/shard_map/ppermute | solution.py:379
  50.2 0.8 collective-permute-start.11
  51.0 0.9 collective-permute-start.15
  51.9 0.5 collective-permute-start.16
  52.4 0.0 collective-permute-start.13
  52.5 1.3 %collective-permute-done.12.refs_0_ = bf16[512,128]{1,0:T(8,128)(2,1)S(1)} collective-permute-done((bf16[512,128]{1,0:T(8,128)(2,1)}, bf16[512,128]{1,0:T(8,128)(2,1)S(1)}, u32[]{:S(2)}, u32[]{:S(2)}) %collective-permute-start.12) | collective-permute-done | bytes 131104 | tf_op jit(solution)/shard_map/ppermute | solution.py:379
  53.7 3.9 %collective-permute-start.14 = (bf16[512,128]{1,0:T(8,128)(2,1)}, bf16[512,128]{1,0:T(8,128)(2,1)S(1)}, u32[]{:S(2)}, u32[]{:S(2)}) collective-permute-start(bf16[512,128]{1,0:T(8,128)(2,1)} %get-tuple-element.51), channel_id=1, source_target_pairs={{0,48},{8,56},{16,0},{24,8},{32,16},{40,24},{48,32},{56,40},{1,49}... | collective-permute-start | bytes 393224 | tf_op jit(solution)/shard_map/ppermute | solution.py:379
  57.6 0.0 collective-permute-done.13.refs_1_
  57.6 1.1 collective-permute-start.17
  58.7 4.4 %collective-permute-done.14.refs_2_ = bf16[512,128]{1,0:T(8,128)(2,1)S(1)} collective-permute-done((bf16[512,128]{1,0:T(8,128)(2,1)}, bf16[512,128]{1,0:T(8,128)(2,1)S(1)}, u32[]{:S(2)}, u32[]{:S(2)}) %collective-permute-start.14) | collective-permute-done | bytes 131104 | tf_op jit(solution)/shard_map/ppermute | solution.py:379
  63.2 2.1 %collective-permute-start.18 = (bf16[512,128]{1,0:T(8,128)(2,1)}, bf16[512,128]{1,0:T(8,128)(2,1)S(1)}, u32[]{:S(2)}, u32[]{:S(2)}) collective-permute-start(bf16[512,128]{1,0:T(8,128)(2,1)} %get-tuple-element.60), channel_id=1, source_target_pairs={{0,40},{8,48},{16,56},{24,0},{32,8},{40,16},{48,24},{56,32},{1,41}... | collective-permute-start | bytes 393224 | tf_op jit(solution)/shard_map/ppermute | solution.py:379
  65.3 0.0 collective-permute-done.11.w1
  65.3 2.9 %collective-permute-start.19 = (bf16[512,128]{1,0:T(8,128)(2,1)}, bf16[512,128]{1,0:T(8,128)(2,1)S(1)}, u32[]{:S(2)}, u32[]{:S(2)}) collective-permute-start(bf16[512,128]{1,0:T(8,128)(2,1)} %get-tuple-element.61), channel_id=1, source_target_pairs={{0,24},{8,32},{16,40},{24,48},{32,56},{40,0},{48,8},{56,16},{1,25}... | collective-permute-start | bytes 393224 | tf_op jit(solution)/shard_map/ppermute | solution.py:379
  68.2 3.5 %collective-permute-start.20 = (bf16[512,128]{1,0:T(8,128)(2,1)}, bf16[512,128]{1,0:T(8,128)(2,1)S(1)}, u32[]{:S(2)}, u32[]{:S(2)}) collective-permute-start(bf16[512,128]{1,0:T(8,128)(2,1)} %get-tuple-element.62), channel_id=1, source_target_pairs={{0,32},{8,40},{16,48},{24,56},{32,0},{40,8},{48,16},{56,24},{1,33}... | collective-permute-start | bytes 393224 | tf_op jit(solution)/shard_map/ppermute | solution.py:379
  71.8 1.6 %q_proj.1.q = bf16[4,512,128]{2,1,0:T(8,128)(2,1)S(1)} custom-call(s32[5]{0:T(128)S(1)} %copy-done.2, bf16[512,2048]{1,0:T(8,128)(2,1)S(1)} %copy-done, bf16[512,256]{1,0:T(8,128)(2,1)S(1)} %get-tuple-element.48.w0, bf16[512,256]{1,0:T(8,128)(2,1)S(1)} %collective-permute-done.11.w1, bf16[512,256]{1,0:T(8,128)(2,1)S(1)} %collective-permute-done.15.w2, ...), custom_call_target="tpu_custom_call" | custom-call | flops 1000000000 | bytes 3936276 | tf_op jit(solution)/shard_map/q_proj/pallas_call | solution.py:323
  73.4 8.7 %attention_near.1.state = f32[4,512,128]{2,1,0:T(8,128)S(1)} custom-call(s32[5]{0:T(128)S(1)} %copy-done.2, f32[8]{0:T(128)S(1)} %copy-done.4, bf16[4,512,128]{2,1,0:T(8,128)(2,1)S(1)} %q_proj.1.q, bf16[512,128]{1,0:T(8,128)(2,1)S(1)} %copy-done.6, bf16[512,128]{1,0:T(8,128)(2,1)S(1)} %copy-done.5, bf16[512,128]{1,0:T(8,128)(2,1)S(1)} %collective-permute-done.12.refs_0_, ...), custom_call_target="tpu_custom_call" | custom-call | flops 5368709120 | bytes 4194304 | tf_op jit(solution)/shard_map/attention_near/pallas_call | solution.py:394
  82.1 1.0 collective-permute-start.21
  83.1 1.0 collective-permute-start.22
  84.1 1.3 %collective-permute-start.23 = (bf16[512,256]{1,0:T(8,128)(2,1)S(1)}, bf16[512,256]{1,0:T(8,128)(2,1)S(1)}, u32[]{:S(2)}, u32[]{:S(2)}) collective-permute-start(bf16[512,256]{1,0:T(8,128)(2,1)S(1)} %get-tuple-element.65.refs_0_), channel_id=1, source_target_pairs={{192,0},{0,64},{64,128},{128,192},{193,1},{1,65},{65,129},{129,193... | collective-permute-start | bytes 786440 | tf_op jit(solution)/shard_map/ppermute | solution.py:290
  85.4 9.2 %attention_far.1 = bf16[2,256,256]{2,1,0:T(8,128)(2,1)S(1)} custom-call(s32[5]{0:T(128)S(1)} %copy-done.2, bf16[4,512,128]{2,1,0:T(8,128)(2,1)S(1)} %q_proj.1.q, f32[4,512,128]{2,1,0:T(8,128)S(1)} %attention_near.1.state, bf16[512,128]{1,0:T(8,128)(2,1)S(1)} %collective-permute-done.17.refs_0_, bf16[512,128]{1,0:T(8,128)(2,1)S(1)} %collective-permute-done.18.refs_1_, ...), custom_call_target="tpu_custom_call" | custom-call | flops 4294967296 | bytes 4194304 | tf_op jit(solution)/shard_map/attention_far/pallas_call | solution.py:410
  94.6 0.1 collective-permute-done.23.refs_3_
  94.8 0.5 collective-permute-start.26
  95.3 0.1 collective-permute-start.27
  95.4 0.4 collective-permute-start.28
  95.8 0.2 collective-permute-start.24
  96.0 1.6 %collective-permute-done.24.got = bf16[256,256]{1,0:T(8,128)(2,1)S(1)} collective-permute-done((bf16[256,256]{1,0:T(8,128)(2,1)S(1)}, bf16[256,256]{1,0:T(8,128)(2,1)S(1)}, u32[]{:S(2)}, u32[]{:S(2)}) %collective-permute-start.24) | collective-permute-done | bytes 131104 | tf_op jit(solution)/shard_map/ppermute | solution.py:295
  97.6 1.3 %out_proj.1 = (bf16[256,512]{1,0:T(8,128)(2,1)S(1)}, bf16[256,512]{1,0:T(8,128)(2,1)S(1)}, bf16[256,512]{1,0:T(8,128)(2,1)S(1)}, bf16[256,512]{1,0:T(8,128)(2,1)S(1)}) custom-call(s32[5]{0:T(128)S(1)} %copy-done.2, bf16[256,256]{1,0:T(8,128)(2,1)S(1)} %get-tuple-element.76.keep, bf16[256,256]{1,0:T(8,128)(2,1)S(1)} %collective-permute-done.24.got, ...), custom_call_target="tpu_custom_call" | custom-call | flops 1000000000 | bytes 3407892 | tf_op jit(solution)/shard_map/out_proj/pallas_call | solution.py:323
  99.0 1.2 %collective-permute-start.29 = (bf16[256,512]{1,0:T(8,128)(2,1)S(1)}, bf16[256,512]{1,0:T(8,128)(2,1)S(1)}, u32[]{:S(2)}, u32[]{:S(2)}) collective-permute-start(bf16[256,512]{1,0:T(8,128)(2,1)S(1)} %get-tuple-element.70), channel_id=1, source_target_pairs={{0,1},{1,2},{2,3},{3,0},{4,5},{5,6},{6,7},{7,4},{8,9},{9,10},{10,1... | collective-permute-start | bytes 786440 | tf_op jit(solution)/shard_map/ppermute | solution.py:434
  100.2 2.9 %collective-permute-start.30 = (bf16[256,512]{1,0:T(8,128)(2,1)S(1)}, bf16[256,512]{1,0:T(8,128)(2,1)S(1)}, u32[]{:S(2)}, u32[]{:S(2)}) collective-permute-start(bf16[256,512]{1,0:T(8,128)(2,1)S(1)} %get-tuple-element.71), channel_id=1, source_target_pairs={{0,2},{1,3},{2,0},{3,1},{4,6},{5,7},{6,4},{7,5},{8,10},{9,11},{10,... | collective-permute-start | bytes 786440 | tf_op jit(solution)/shard_map/ppermute | solution.py:434
  103.1 1.3 %collective-permute-start.31 = (bf16[256,512]{1,0:T(8,128)(2,1)S(1)}, bf16[256,512]{1,0:T(8,128)(2,1)S(1)}, u32[]{:S(2)}, u32[]{:S(2)}) collective-permute-start(bf16[256,512]{1,0:T(8,128)(2,1)S(1)} %get-tuple-element.72), channel_id=1, source_target_pairs={{0,3},{1,0},{2,1},{3,2},{4,7},{5,4},{6,5},{7,6},{8,11},{9,8},{10,9... | collective-permute-start | bytes 786440 | tf_op jit(solution)/shard_map/ppermute | solution.py:434
  104.5 4.2 %collective-permute-done.29 = bf16[256,512]{1,0:T(8,128)(2,1)S(1)} collective-permute-done((bf16[256,512]{1,0:T(8,128)(2,1)S(1)}, bf16[256,512]{1,0:T(8,128)(2,1)S(1)}, u32[]{:S(2)}, u32[]{:S(2)}) %collective-permute-start.29) | collective-permute-done | bytes 262176 | tf_op jit(solution)/shard_map/ppermute | solution.py:434
  108.6 6.4 %collective-permute-done.30 = bf16[256,512]{1,0:T(8,128)(2,1)S(1)} collective-permute-done((bf16[256,512]{1,0:T(8,128)(2,1)S(1)}, bf16[256,512]{1,0:T(8,128)(2,1)S(1)}, u32[]{:S(2)}, u32[]{:S(2)}) %collective-permute-start.30) | collective-permute-done | bytes 262176 | tf_op jit(solution)/shard_map/ppermute | solution.py:434
  115.1 0.8 fusion
  (53 shorter events, 0.2 us)
Async XLA Ops:
  1.3 10.7 %copy-start.7 = (bf16[1,256,512]{2,1,0:T(8,128)(2,1)S(1)}, bf16[1,256,512]{2,1,0:T(8,128)(2,1)}, u32[]{:S(2)}) copy-start(bf16[1,256,512]{2,1,0:T(8,128)(2,1)} %param.12) | copy-start | bytes 786436
  1.3 30.1 %copy-start.16 = (bf16[2048]{0:T(1024)(128)(2,1)S(1)}, bf16[2048]{0:T(1024)(128)(2,1)}, u32[]{:S(2)}) copy-start(bf16[2048]{0:T(1024)(128)(2,1)} %param.14) | copy-start | bytes 12292
  3.3 33.3 %copy-start.18 = (bf16[256,128]{1,0:T(8,128)(2,1)S(1)}, bf16[256,128]{1,0:T(8,128)(2,1)}, u32[]{:S(2)}) copy-start(bf16[256,128]{1,0:T(8,128)(2,1)} %get-tuple-element.46) | copy-start | bytes 196612
  3.3 27.0 %all-to-all-start = ((bf16[16,32,640]{2,1,0:T(8,128)(2,1)}), bf16[16,32,640]{2,1,0:T(8,128)(2,1)S(1)}, u32[]{:S(2)}, u32[]{:S(2)}) async-start(bf16[16,32,640]{2,1,0:T(8,128)(2,1)} %get-tuple-element.39), calls=%async_computation | async-start | bytes 1310720 | tf_op jit(solution)/shard_map/all_to_all | solution.py:349
  12.0 14.6 %collective-permute-start = (bf16[256,512]{1,0:T(8,128)(2,1)S(1)}, bf16[256,512]{1,0:T(8,128)(2,1)S(1)}, u32[]{:S(2)}, u32[]{:S(2)}) collective-permute-start(bf16[256,512]{1,0:T(8,128)(2,1)S(1)} %bitcast.17), channel_id=1, source_target_pairs={{1,0},{2,1},{3,2},{0,3},{5,4},{6,5},{7,6},{4,7},{9,8},{10,9},{11,1... | collective-permute-start | bytes 786440 | tf_op jit(solution)/shard_map/ppermute | solution.py:290
  15.1 11.5 %collective-permute-start.1 = (bf16[256,512]{1,0:T(8,128)(2,1)S(1)}, bf16[256,512]{1,0:T(8,128)(2,1)S(1)}, u32[]{:S(2)}, u32[]{:S(2)}) collective-permute-start(bf16[256,512]{1,0:T(8,128)(2,1)S(1)} %bitcast.18), channel_id=1, source_target_pairs={{2,0},{3,1},{0,2},{1,3},{6,4},{7,5},{4,6},{5,7},{10,8},{11,9},{8,1... | collective-permute-start | bytes 786440 | tf_op jit(solution)/shard_map/ppermute | solution.py:290
  15.7 14.6 %collective-permute-start.2 = (bf16[256,512]{1,0:T(8,128)(2,1)S(1)}, bf16[256,512]{1,0:T(8,128)(2,1)S(1)}, u32[]{:S(2)}, u32[]{:S(2)}) collective-permute-start(bf16[256,512]{1,0:T(8,128)(2,1)S(1)} %bitcast.19), channel_id=1, source_target_pairs={{3,0},{0,1},{1,2},{2,3},{7,4},{4,5},{5,6},{6,7},{11,8},{8,9},{9,10... | collective-permute-start | bytes 786440 | tf_op jit(solution)/shard_map/ppermute | solution.py:290
  26.6 10.1 %copy-start.8 = (bf16[256,512]{1,0:T(8,128)(2,1)}, bf16[256,512]{1,0:T(8,128)(2,1)S(1)}, u32[]{:S(2)}) copy-start(bf16[256,512]{1,0:T(8,128)(2,1)S(1)} %collective-permute-done.refs_1_) | copy-start | bytes 786436
  26.6 10.1 %copy-start.9 = (bf16[256,512]{1,0:T(8,128)(2,1)}, bf16[256,512]{1,0:T(8,128)(2,1)S(1)}, u32[]{:S(2)}) copy-start(bf16[256,512]{1,0:T(8,128)(2,1)S(1)} %collective-permute-done.1.refs_2_) | copy-start | bytes 786436
  30.3 6.4 %copy-start.10 = (bf16[256,512]{1,0:T(8,128)(2,1)}, bf16[256,512]{1,0:T(8,128)(2,1)S(1)}, u32[]{:S(2)}) copy-start(bf16[256,512]{1,0:T(8,128)(2,1)S(1)} %collective-permute-done.2.refs_3_) | copy-start | bytes 786436
  30.3 4.5 %collective-permute-start.3 = (bf16[256,512]{1,0:T(8,128)(2,1)S(1)}, bf16[256,512]{1,0:T(8,128)(2,1)S(1)}, u32[]{:S(2)}, u32[]{:S(2)}) collective-permute-start(bf16[256,512]{1,0:T(8,128)(2,1)S(1)} %bitcast.20), channel_id=1, source_target_pairs={{0,4},{4,0},{1,5},{5,1},{2,6},{6,2},{3,7},{7,3},{8,12},{12,8},{9,1... | collective-permute-start | bytes 786440 | tf_op jit(solution)/shard_map/ppermute | solution.py:295
  30.3 5.3 %collective-permute-start.4 = (bf16[256,512]{1,0:T(8,128)(2,1)S(1)}, bf16[256,512]{1,0:T(8,128)(2,1)S(1)}, u32[]{:S(2)}, u32[]{:S(2)}) collective-permute-start(bf16[256,512]{1,0:T(8,128)(2,1)S(1)} %collective-permute-done.refs_1_), channel_id=1, source_target_pairs={{0,4},{4,0},{1,5},{5,1},{2,6},{6,2},{3,7},{7,3},{8,12},{12,8},{9,1... | collective-permute-start | bytes 786440 | tf_op jit(solution)/shard_map/ppermute | solution.py:295
  30.8 5.7 %collective-permute-start.5 = (bf16[256,512]{1,0:T(8,128)(2,1)S(1)}, bf16[256,512]{1,0:T(8,128)(2,1)S(1)}, u32[]{:S(2)}, u32[]{:S(2)}) collective-permute-start(bf16[256,512]{1,0:T(8,128)(2,1)S(1)} %collective-permute-done.1.refs_2_), channel_id=1, source_target_pairs={{0,4},{4,0},{1,5},{5,1},{2,6},{6,2},{3,7},{7,3},{8,12},{12,8},{9,1... | collective-permute-start | bytes 786440 | tf_op jit(solution)/shard_map/ppermute | solution.py:295
  30.9 5.8 %collective-permute-start.6 = (bf16[256,512]{1,0:T(8,128)(2,1)S(1)}, bf16[256,512]{1,0:T(8,128)(2,1)S(1)}, u32[]{:S(2)}, u32[]{:S(2)}) collective-permute-start(bf16[256,512]{1,0:T(8,128)(2,1)S(1)} %collective-permute-done.2.refs_3_), channel_id=1, source_target_pairs={{0,4},{4,0},{1,5},{5,1},{2,6},{6,2},{3,7},{7,3},{8,12},{12,8},{9,1... | collective-permute-start | bytes 786440 | tf_op jit(solution)/shard_map/ppermute | solution.py:295
  32.0 12.5 %copy-start.15 = (bf16[512,128]{1,0:T(8,128)(2,1)}, bf16[512,128]{1,0:T(8,128)(2,1)S(1)}, u32[]{:S(2)}) copy-start(bf16[512,128]{1,0:T(8,128)(2,1)S(1)} %slice.16.w0) | copy-start | bytes 393220
  32.0 9.8 %collective-permute-start.7 = (bf16[512,128]{1,0:T(8,128)(2,1)S(1)}, bf16[512,128]{1,0:T(8,128)(2,1)S(1)}, u32[]{:S(2)}, u32[]{:S(2)}) collective-permute-start(bf16[512,128]{1,0:T(8,128)(2,1)S(1)} %slice.16.w0), channel_id=1, source_target_pairs={{64,0},{128,64},{192,128},{0,192},{65,1},{129,65},{193,129},{1,193... | collective-permute-start | bytes 393224 | tf_op jit(solution)/shard_map/ppermute | solution.py:290
  34.8 1.9 %copy-start.11 = (bf16[256,512]{1,0:T(8,128)(2,1)}, bf16[256,512]{1,0:T(8,128)(2,1)S(1)}, u32[]{:S(2)}) copy-start(bf16[256,512]{1,0:T(8,128)(2,1)S(1)} %collective-permute-done.3.refs_4_) | copy-start | bytes 786436
  34.8 8.0 %collective-permute-start.8 = (bf16[512,128]{1,0:T(8,128)(2,1)S(1)}, bf16[512,128]{1,0:T(8,128)(2,1)}, u32[]{:S(2)}, u32[]{:S(2)}) collective-permute-start(bf16[512,128]{1,0:T(8,128)(2,1)S(1)} %slice.16.w0), channel_id=1, source_target_pairs={{128,0},{192,64},{0,128},{64,192},{129,1},{193,65},{1,129},{65,193... | collective-permute-start | bytes 393224 | tf_op jit(solution)/shard_map/ppermute | solution.py:290
  35.6 1.1 copy-start.12
  35.6 8.8 %collective-permute-start.9 = (bf16[512,128]{1,0:T(8,128)(2,1)S(1)}, bf16[512,128]{1,0:T(8,128)(2,1)}, u32[]{:S(2)}, u32[]{:S(2)}) collective-permute-start(bf16[512,128]{1,0:T(8,128)(2,1)S(1)} %slice.16.w0), channel_id=1, source_target_pairs={{192,0},{0,64},{64,128},{128,192},{193,1},{1,65},{65,129},{129,193... | collective-permute-start | bytes 393224 | tf_op jit(solution)/shard_map/ppermute | solution.py:290
  36.6 0.7 copy-start.13
  36.6 5.2 %collective-permute-start.10 = (bf16[256,128]{1,0:T(8,128)(2,1)S(1)}, bf16[256,128]{1,0:T(8,128)(2,1)}, u32[]{:S(2)}, u32[]{:S(2)}) collective-permute-start(bf16[256,128]{1,0:T(8,128)(2,1)S(1)} %copy-done.18), channel_id=1, source_target_pairs={{0,4},{4,0},{1,5},{5,1},{2,6},{6,2},{3,7},{7,3},{8,12},{12,8},{9,1... | collective-permute-start | bytes 196616 | tf_op jit(solution)/shard_map/ppermute | solution.py:295
  37.2 0.7 copy-start.14
  41.7 30.0 %copy-start = (bf16[512,2048]{1,0:T(8,128)(2,1)S(1)}, bf16[512,2048]{1,0:T(8,128)(2,1)}, u32[]{:S(2)}) copy-start(bf16[512,2048]{1,0:T(8,128)(2,1)} %norm.1.normed) | copy-start | bytes 6291460
  41.7 30.0 %copy-start.1 = (f32[512,128]{1,0:T(8,128)S(1)}, f32[512,128]{1,0:T(8,128)}, u32[]{:S(2)}) copy-start(f32[512,128]{1,0:T(8,128)} %constant.22.clone.fine) | copy-start | bytes 786436
  41.7 30.0 %copy-start.2 = (s32[5]{0:T(128)S(1)}, s32[5]{0:T(128)}, u32[]{:S(2)}) copy-start(s32[5]{0:T(128)} %stack.19.ids) | copy-start | bytes 64
  41.7 30.0 %copy-start.3 = (f32[8,128]{1,0:T(8,128)S(1)}, f32[8,128]{1,0:T(8,128)}, u32[]{:S(2)}) copy-start(f32[8,128]{1,0:T(8,128)} %constant.21.clone.coarse) | copy-start | bytes 12292
  41.8 2.7 %copy-start.17 = (bf16[512,128]{1,0:T(8,128)(2,1)}, bf16[512,128]{1,0:T(8,128)(2,1)S(1)}, u32[]{:S(2)}) copy-start(bf16[512,128]{1,0:T(8,128)(2,1)S(1)} %collective-permute-done.7.w1) | copy-start | bytes 393220
  48.0 25.4 %copy-start.4 = (f32[8]{0:T(128)S(1)}, f32[8]{0:T(128)}, u32[]{:S(2)}) copy-start(f32[8]{0:T(128)} %sinks.1) | copy-start | bytes 100
  48.0 25.4 %copy-start.5 = (bf16[512,128]{1,0:T(8,128)(2,1)S(1)}, bf16[512,128]{1,0:T(8,128)(2,1)}, u32[]{:S(2)}) copy-start(bf16[512,128]{1,0:T(8,128)(2,1)} %get-tuple-element.54.own_new) | copy-start | bytes 393220
  48.0 25.4 %copy-start.6 = (bf16[512,128]{1,0:T(8,128)(2,1)S(1)}, bf16[512,128]{1,0:T(8,128)(2,1)}, u32[]{:S(2)}) copy-start(bf16[512,128]{1,0:T(8,128)(2,1)} %get-tuple-element.53.own_prefix) | copy-start | bytes 393220
  48.0 5.7 %collective-permute-start.12 = (bf16[512,128]{1,0:T(8,128)(2,1)}, bf16[512,128]{1,0:T(8,128)(2,1)S(1)}, u32[]{:S(2)}, u32[]{:S(2)}) collective-permute-start(bf16[512,128]{1,0:T(8,128)(2,1)} %get-tuple-element.49), channel_id=1, source_target_pairs={{0,56},{8,0},{16,8},{24,16},{32,24},{40,32},{48,40},{56,48},{1,57}... | collective-permute-start | bytes 393224 | tf_op jit(solution)/shard_map/ppermute | solution.py:379
  50.2 15.1 %collective-permute-start.11 = (bf16[512,256]{1,0:T(8,128)(2,1)S(1)}, bf16[512,256]{1,0:T(8,128)(2,1)S(1)}, u32[]{:S(2)}, u32[]{:S(2)}) collective-permute-start(bf16[512,256]{1,0:T(8,128)(2,1)S(1)} %get-tuple-element.48.w0), channel_id=1, source_target_pairs={{64,0},{128,64},{192,128},{0,192},{65,1},{129,65},{193,129},{1,193... | collective-permute-start | bytes 786440 | tf_op jit(solution)/shard_map/ppermute | solution.py:290
  51.0 17.2 %collective-permute-start.15 = (bf16[512,256]{1,0:T(8,128)(2,1)S(1)}, bf16[512,256]{1,0:T(8,128)(2,1)S(1)}, u32[]{:S(2)}, u32[]{:S(2)}) collective-permute-start(bf16[512,256]{1,0:T(8,128)(2,1)S(1)} %get-tuple-element.48.w0), channel_id=1, source_target_pairs={{128,0},{192,64},{0,128},{64,192},{129,1},{193,65},{1,129},{65,193... | collective-permute-start | bytes 786440 | tf_op jit(solution)/shard_map/ppermute | solution.py:290
  51.9 19.8 %collective-permute-start.16 = (bf16[512,256]{1,0:T(8,128)(2,1)S(1)}, bf16[512,256]{1,0:T(8,128)(2,1)S(1)}, u32[]{:S(2)}, u32[]{:S(2)}) collective-permute-start(bf16[512,256]{1,0:T(8,128)(2,1)S(1)} %get-tuple-element.48.w0), channel_id=1, source_target_pairs={{192,0},{0,64},{64,128},{128,192},{193,1},{1,65},{65,129},{129,193... | collective-permute-start | bytes 786440 | tf_op jit(solution)/shard_map/ppermute | solution.py:290
  52.4 5.2 %collective-permute-start.13 = (bf16[512,128]{1,0:T(8,128)(2,1)}, bf16[512,128]{1,0:T(8,128)(2,1)S(1)}, u32[]{:S(2)}, u32[]{:S(2)}) collective-permute-start(bf16[512,128]{1,0:T(8,128)(2,1)} %get-tuple-element.50), channel_id=1, source_target_pairs={{0,8},{8,16},{16,24},{24,32},{32,40},{40,48},{48,56},{56,0},{1,9},... | collective-permute-start | bytes 393224 | tf_op jit(solution)/shard_map/ppermute | solution.py:379
  53.7 9.5 %collective-permute-start.14 = (bf16[512,128]{1,0:T(8,128)(2,1)}, bf16[512,128]{1,0:T(8,128)(2,1)S(1)}, u32[]{:S(2)}, u32[]{:S(2)}) collective-permute-start(bf16[512,128]{1,0:T(8,128)(2,1)} %get-tuple-element.51), channel_id=1, source_target_pairs={{0,48},{8,56},{16,0},{24,8},{32,16},{40,24},{48,32},{56,40},{1,49}... | collective-permute-start | bytes 393224 | tf_op jit(solution)/shard_map/ppermute | solution.py:379
  57.6 25.5 %collective-permute-start.17 = (bf16[512,128]{1,0:T(8,128)(2,1)}, bf16[512,128]{1,0:T(8,128)(2,1)S(1)}, u32[]{:S(2)}, u32[]{:S(2)}) collective-permute-start(bf16[512,128]{1,0:T(8,128)(2,1)} %get-tuple-element.59), channel_id=1, source_target_pairs={{0,16},{8,24},{16,32},{24,40},{32,48},{40,56},{48,0},{56,8},{1,17}... | collective-permute-start | bytes 393224 | tf_op jit(solution)/shard_map/ppermute | solution.py:379
  63.2 20.9 %collective-permute-start.18 = (bf16[512,128]{1,0:T(8,128)(2,1)}, bf16[512,128]{1,0:T(8,128)(2,1)S(1)}, u32[]{:S(2)}, u32[]{:S(2)}) collective-permute-start(bf16[512,128]{1,0:T(8,128)(2,1)} %get-tuple-element.60), channel_id=1, source_target_pairs={{0,40},{8,48},{16,56},{24,0},{32,8},{40,16},{48,24},{56,32},{1,41}... | collective-permute-start | bytes 393224 | tf_op jit(solution)/shard_map/ppermute | solution.py:379
  65.3 20.1 %collective-permute-start.19 = (bf16[512,128]{1,0:T(8,128)(2,1)}, bf16[512,128]{1,0:T(8,128)(2,1)S(1)}, u32[]{:S(2)}, u32[]{:S(2)}) collective-permute-start(bf16[512,128]{1,0:T(8,128)(2,1)} %get-tuple-element.61), channel_id=1, source_target_pairs={{0,24},{8,32},{16,40},{24,48},{32,56},{40,0},{48,8},{56,16},{1,25}... | collective-permute-start | bytes 393224 | tf_op jit(solution)/shard_map/ppermute | solution.py:379
  68.2 17.2 %collective-permute-start.20 = (bf16[512,128]{1,0:T(8,128)(2,1)}, bf16[512,128]{1,0:T(8,128)(2,1)S(1)}, u32[]{:S(2)}, u32[]{:S(2)}) collective-permute-start(bf16[512,128]{1,0:T(8,128)(2,1)} %get-tuple-element.62), channel_id=1, source_target_pairs={{0,32},{8,40},{16,48},{24,56},{32,0},{40,8},{48,16},{56,24},{1,33}... | collective-permute-start | bytes 393224 | tf_op jit(solution)/shard_map/ppermute | solution.py:379
  82.1 12.5 %collective-permute-start.21 = (bf16[512,256]{1,0:T(8,128)(2,1)S(1)}, bf16[512,256]{1,0:T(8,128)(2,1)S(1)}, u32[]{:S(2)}, u32[]{:S(2)}) collective-permute-start(bf16[512,256]{1,0:T(8,128)(2,1)S(1)} %get-tuple-element.65.refs_0_), channel_id=1, source_target_pairs={{64,0},{128,64},{192,128},{0,192},{65,1},{129,65},{193,129},{1,193... | collective-permute-start | bytes 786440 | tf_op jit(solution)/shard_map/ppermute | solution.py:290
  83.1 11.5 %collective-permute-start.22 = (bf16[512,256]{1,0:T(8,128)(2,1)S(1)}, bf16[512,256]{1,0:T(8,128)(2,1)S(1)}, u32[]{:S(2)}, u32[]{:S(2)}) collective-permute-start(bf16[512,256]{1,0:T(8,128)(2,1)S(1)} %get-tuple-element.65.refs_0_), channel_id=1, source_target_pairs={{128,0},{192,64},{0,128},{64,192},{129,1},{193,65},{1,129},{65,193... | collective-permute-start | bytes 786440 | tf_op jit(solution)/shard_map/ppermute | solution.py:290
  84.1 10.7 %collective-permute-start.23 = (bf16[512,256]{1,0:T(8,128)(2,1)S(1)}, bf16[512,256]{1,0:T(8,128)(2,1)S(1)}, u32[]{:S(2)}, u32[]{:S(2)}) collective-permute-start(bf16[512,256]{1,0:T(8,128)(2,1)S(1)} %get-tuple-element.65.refs_0_), channel_id=1, source_target_pairs={{192,0},{0,64},{64,128},{128,192},{193,1},{1,65},{65,129},{129,193... | collective-permute-start | bytes 786440 | tf_op jit(solution)/shard_map/ppermute | solution.py:290
  94.8 2.9 %collective-permute-start.25 = (bf16[512,256]{1,0:T(8,128)(2,1)S(1)}, bf16[512,256]{1,0:T(8,128)(2,1)S(1)}, u32[]{:S(2)}, u32[]{:S(2)}) collective-permute-start(bf16[512,256]{1,0:T(8,128)(2,1)S(1)} %get-tuple-element.65.refs_0_), channel_id=1, source_target_pairs={{0,4},{4,0},{1,5},{5,1},{2,6},{6,2},{3,7},{7,3},{8,12},{12,8},{9,1... | collective-permute-start | bytes 786440 | tf_op jit(solution)/shard_map/ppermute | solution.py:295
  94.8 2.9 %collective-permute-start.26 = (bf16[512,256]{1,0:T(8,128)(2,1)S(1)}, bf16[512,256]{1,0:T(8,128)(2,1)S(1)}, u32[]{:S(2)}, u32[]{:S(2)}) collective-permute-start(bf16[512,256]{1,0:T(8,128)(2,1)S(1)} %collective-permute-done.21.refs_1_), channel_id=1, source_target_pairs={{0,4},{4,0},{1,5},{5,1},{2,6},{6,2},{3,7},{7,3},{8,12},{12,8},{9,1... | collective-permute-start | bytes 786440 | tf_op jit(solution)/shard_map/ppermute | solution.py:295
  95.3 2.3 %collective-permute-start.27 = (bf16[512,256]{1,0:T(8,128)(2,1)S(1)}, bf16[512,256]{1,0:T(8,128)(2,1)S(1)}, u32[]{:S(2)}, u32[]{:S(2)}) collective-permute-start(bf16[512,256]{1,0:T(8,128)(2,1)S(1)} %collective-permute-done.22.refs_2_), channel_id=1, source_target_pairs={{0,4},{4,0},{1,5},{5,1},{2,6},{6,2},{3,7},{7,3},{8,12},{12,8},{9,1... | collective-permute-start | bytes 786440 | tf_op jit(solution)/shard_map/ppermute | solution.py:295
  95.4 2.3 %collective-permute-start.28 = (bf16[512,256]{1,0:T(8,128)(2,1)S(1)}, bf16[512,256]{1,0:T(8,128)(2,1)S(1)}, u32[]{:S(2)}, u32[]{:S(2)}) collective-permute-start(bf16[512,256]{1,0:T(8,128)(2,1)S(1)} %collective-permute-done.23.refs_3_), channel_id=1, source_target_pairs={{0,4},{4,0},{1,5},{5,1},{2,6},{6,2},{3,7},{7,3},{8,12},{12,8},{9,1... | collective-permute-start | bytes 786440 | tf_op jit(solution)/shard_map/ppermute | solution.py:295
  95.8 1.8 %collective-permute-start.24 = (bf16[256,256]{1,0:T(8,128)(2,1)S(1)}, bf16[256,256]{1,0:T(8,128)(2,1)S(1)}, u32[]{:S(2)}, u32[]{:S(2)}) collective-permute-start(bf16[256,256]{1,0:T(8,128)(2,1)S(1)} %get-tuple-element.75), channel_id=1, source_target_pairs={{0,4},{4,0},{1,5},{5,1},{2,6},{6,2},{3,7},{7,3},{8,12},{12,8},{9,1... | collective-permute-start | bytes 393224 | tf_op jit(solution)/shard_map/ppermute | solution.py:295
  99.0 9.6 %collective-permute-start.29 = (bf16[256,512]{1,0:T(8,128)(2,1)S(1)}, bf16[256,512]{1,0:T(8,128)(2,1)S(1)}, u32[]{:S(2)}, u32[]{:S(2)}) collective-permute-start(bf16[256,512]{1,0:T(8,128)(2,1)S(1)} %get-tuple-element.70), channel_id=1, source_target_pairs={{0,1},{1,2},{2,3},{3,0},{4,5},{5,6},{6,7},{7,4},{8,9},{9,10},{10,1... | collective-permute-start | bytes 786440 | tf_op jit(solution)/shard_map/ppermute | solution.py:434
  100.2 14.8 %collective-permute-start.30 = (bf16[256,512]{1,0:T(8,128)(2,1)S(1)}, bf16[256,512]{1,0:T(8,128)(2,1)S(1)}, u32[]{:S(2)}, u32[]{:S(2)}) collective-permute-start(bf16[256,512]{1,0:T(8,128)(2,1)S(1)} %get-tuple-element.71), channel_id=1, source_target_pairs={{0,2},{1,3},{2,0},{3,1},{4,6},{5,7},{6,4},{7,5},{8,10},{9,11},{10,... | collective-permute-start | bytes 786440 | tf_op jit(solution)/shard_map/ppermute | solution.py:434
  103.1 11.9 %collective-permute-start.31 = (bf16[256,512]{1,0:T(8,128)(2,1)S(1)}, bf16[256,512]{1,0:T(8,128)(2,1)S(1)}, u32[]{:S(2)}, u32[]{:S(2)}) collective-permute-start(bf16[256,512]{1,0:T(8,128)(2,1)S(1)} %get-tuple-element.72), channel_id=1, source_target_pairs={{0,3},{1,0},{2,1},{3,2},{4,7},{5,4},{6,5},{7,6},{8,11},{9,8},{10,9... | collective-permute-start | bytes 786440 | tf_op jit(solution)/shard_map/ppermute | solution.py:434
